TPU v7x, 256 devices: a whole 4x4x8 slice. The times are simulated.
256 devices in a mesh: fde: 8 (over z), pas: 32 (over x, y, core).
Axes of the slice: x: 4, y: 4, z: 8, core: 2. Of those that a mesh axis runs over, the one named last changes fastest.
Arguments:
- query_fixed_encoding: bfloat16 [128, 10240], P(None, 'fde'), may hold values from -6 to 6
- passage_fde: bfloat16 [8192, 10240], P('pas', 'fde'), may hold values from -0.0625 to 0.0625
- query_tokens: bfloat16 [128, 32, 128], P('fde'), may hold values from -6 to 6
- query_token_totals: int32 [128], P('fde'), may hold values from 1 to 32
- passage_tokens: bfloat16 [8192, 256, 128], P(('fde', 'pas')), may hold values from -0.5 to 0.5
- passage_lengths: int32 [8192], P(('fde', 'pas')), may hold values from 1 to 256
- candidates: int32 [128, 1024], P('fde', 'pas'), may hold values from 0 to 8191, as said below
Outputs:
- fde_scores: float32 [128, 8192], P('fde', 'pas')
- rerank: float32 [128, 1024], P('fde', 'pas')
Inputs may be any that keep to these rules, and one draw needn't show every extreme that they name: Passage p is held by the device of linear index p // 32 over fde then pas. Among the 16 x 32 candidates held by one device, one quarter of the 256 devices (the same quarter for every device) is named exactly 6 times each, another quarter 2 times each, the rest not at all; within an owner device the ids are uniform and may repeat.
All inputs are finite; a program needn't handle non-finite values.
Results may differ from a plain program's by a relative error of at most 0.0003.
Values may be sent and summed in bfloat16 or wider, within the bound.
No kernel may reach another device: no remote copies, remote signals or barrier semaphores. Data moves between devices by JAX's collectives and lax.ppermute only.
A program may use at most 128 MiB of HBM per device.

v0:
```python
import jax
import jax.numpy as jnp
from jax import lax
from jax.sharding import PartitionSpec as P

slot_block = 128


def cut_along(shard, dim, count):
    before, after = (shard.shape[:dim], shard.shape[dim + 1 :])
    return jnp.moveaxis(shard.reshape(*before, count, -1, *after), dim, 0)


def summed_on_arrival(shard, axis, dim):
    count = lax.axis_size(axis)
    tiles = lax.all_to_all(cut_along(shard, dim, count), axis, 0, 0, tiled=True)
    return jnp.sum(tiles, axis=0)


def in_order(tiles, dim):
    tiles = jnp.moveaxis(tiles, 0, dim)
    shape = tiles.shape
    return tiles.reshape(*shape[:dim], shape[dim] * shape[dim + 1], *shape[dim + 2 :])


def joined_exchange(shard, axis, axes, splits, concats):
    sizes = [lax.axis_size(a) for a in axes]
    tiles = cut_along(shard, splits[0], sizes[0])
    tiles = jnp.moveaxis(cut_along(tiles, splits[1] + 1, sizes[1]), 0, 1)
    inside = tiles.shape[2:]
    tiles = tiles.reshape(-1, *inside)
    tiles = lax.all_to_all(tiles, axis, split_axis=0, concat_axis=0, tiled=True)
    tiles = in_order(tiles.reshape(*sizes, *inside), concats[0] + 1)
    return in_order(tiles, concats[1])


def maxsim_block(token_vectors, counts, local_ids, passage_tokens, passage_lengths):
    corpus_texts = jnp.take(passage_tokens, local_ids, axis=0)
    lengths = jnp.take(passage_lengths, local_ids, axis=0)
    similarity_matrix = jnp.einsum(
        "zxg,zwg->zxw", token_vectors, corpus_texts, preferred_element_type=jnp.float32
    )
    positions = lax.broadcasted_iota(jnp.int32, similarity_matrix.shape, 2)
    best_match = jnp.max(
        jnp.where(positions < lengths[:, None, None], similarity_matrix, jnp.float32(-1e30)), axis=2
    )
    token_slot = lax.broadcasted_iota(jnp.int32, best_match.shape, 1)
    summed = jnp.sum(jnp.where(token_slot < counts[:, None], best_match, jnp.float32(0.0)), axis=1)
    return summed / counts.astype(jnp.float32)


def body(
    query_fixed_encoding,
    passage_fde,
    query_tokens,
    query_token_totals,
    passage_tokens,
    passage_lengths,
    candidates,
):
    groups = lax.axis_size("fde")
    shards = lax.axis_size("pas")
    owners = groups * shards
    query_local = query_tokens.shape[0]
    fde_scores = summed_on_arrival(
        jnp.einsum(
            "qf,pf->qp", query_fixed_encoding, passage_fde, preferred_element_type=jnp.float32
        ),
        "fde",
        0,
    )
    pass_local = passage_tokens.shape[0]
    cand_local = candidates.shape[1]
    flat_ids = candidates.reshape(-1)
    pair_count = flat_ids.shape[0]
    capacity = 3 * pair_count // owners
    slot_count = owners * capacity
    count_per_block = slot_count // slot_block
    owner_dev = flat_ids // pass_local
    local_ids = flat_ids % pass_local
    onehot = (owner_dev[:, None] == jnp.arange(owners, dtype=jnp.int32)[None, :]).astype(jnp.int32)
    before = jnp.cumsum(onehot, axis=0) - onehot
    slot_rank = jnp.sum(before * onehot, axis=1)
    target = owner_dev * capacity + slot_rank
    pair_row = jnp.arange(pair_count, dtype=jnp.int32) // cand_local

    def shaped(array):
        return array.reshape((groups, shards, capacity) + array.shape[1:])

    def blocked(array):
        return array.reshape((count_per_block, slot_block) + array.shape[3:])

    send_local = jnp.zeros((slot_count,), jnp.int32).at[target].set(local_ids)
    all_tokens, all_counts = (
        lax.all_gather(query_tokens, "fde", axis=0, tiled=True),
        lax.all_gather(query_token_totals, "fde", axis=0, tiled=True),
    )
    query_ids = lax.axis_index("fde") * query_local + pair_row
    send_query = jnp.zeros((slot_count,), jnp.int32).at[target].set(query_ids)
    recv_query, recv_local = (
        joined_exchange(shaped(send_query), ("fde", "pas"), ("fde", "pas"), (0, 1), (0, 1)),
        joined_exchange(shaped(send_local), ("fde", "pas"), ("fde", "pas"), (0, 1), (0, 1)),
    )

    def score_gathered(inputs):
        query_block, local_block = inputs
        return maxsim_block(
            jnp.take(all_tokens, query_block, axis=0),
            jnp.take(all_counts, query_block, axis=0),
            local_block,
            passage_tokens,
            passage_lengths,
        )

    scores = lax.map(score_gathered, (blocked(recv_query), blocked(recv_local)))
    returned = joined_exchange(
        shaped(scores.reshape(-1)), ("fde", "pas"), ("fde", "pas"), (0, 1), (0, 1)
    )
    rerank = jnp.take(returned.reshape(-1), target, axis=0).reshape(candidates.shape)
    return (fde_scores, rerank)


def solution(mesh):
    return jax.shard_map(
        body,
        mesh=mesh,
        in_specs=(
            P(None, "fde"),
            P("pas", "fde"),
            P("fde", None, None),
            P("fde"),
            P(("fde", "pas"), None, None),
            P(("fde", "pas")),
            P("fde", "pas"),
        ),
        out_specs=(P("fde", "pas"), P("fde", "pas")),
        check_vma=False,
    )
```

profile of v0, /device:TPU:1, one launch (start us, length us, event | category | flops | bytes accessed | tf_op | source)
XLA Modules:
  0.0 326.0 jit_solution(17883038020650839240)
XLA Ops:
  11.1 2.5 scatter_custom_fusion.1
  14.3 15.6 %all-to-all-start.2 = ((s32[256,1,1,6]{3,2,1,0:T(1,128)}), s32[256,1,1,6]{3,2,1,0:T(1,128)S(1)}, u32[]{:S(2)}, u32[]{:S(2)}) async-start(s32[256,1,1,6]{3,2,1,0:T(1,128)} %bitcast.20), calls=%async_computation.2 | async-start | bytes 262144 | tf_op jit(solution)/shard_map/all_to_all | solution.py:32
  30.0 2.5 scatter_custom_fusion
  33.2 10.2 %all-to-all-done.2 = s32[256,1,1,6]{3,2,1,0:T(1,128)S(1)} async-done(((s32[256,1,1,6]{3,2,1,0:T(1,128)}), s32[256,1,1,6]{3,2,1,0:T(1,128)S(1)}, u32[]{:S(2)}, u32[]{:S(2)}) %all-to-all-start.2) | async-done | bytes 6176 | tf_op jit(solution)/shard_map/all_to_all | solution.py:32
  43.5 5.7 %all-to-all-start.1 = ((s32[256,1,1,6]{3,2,1,0:T(1,128)}), s32[256,1,1,6]{3,2,1,0:T(1,128)S(1)}, u32[]{:S(2)}, u32[]{:S(2)}) async-start(s32[256,1,1,6]{3,2,1,0:T(1,128)} %bitcast.14), calls=%async_computation.1 | async-start | bytes 262144 | tf_op jit(solution)/shard_map/all_to_all | solution.py:32
  49.2 2.0 fusion.32
  54.0 12.6 %all-reduce = s32[128]{0:T(128)S(1)} all-reduce(s32[128]{0:T(128)S(1)} %dynamic-update-slice), channel_id=1, replica_groups=mesh['fde'=8,'pas'=32] {'fde'}, use_global_device_ids=true, to_apply=%add | all-reduce | flops 128 | bytes 1024
  66.7 3.4 %all-to-all-start = ((f32[8,16,256]{2,1,0:T(8,128)}), f32[8,16,256]{2,1,0:T(8,128)S(1)}, u32[]{:S(2)}, u32[]{:S(2)}) async-start(f32[8,16,256]{2,1,0:T(8,128)} %bitcast.8), calls=%async_computation | async-start | bytes 262144 | tf_op jit(solution)/shard_map/all_to_all | solution.py:16
  70.3 212.6 %while.10 = (s32[]{:T(128)}, f32[12,128]{1,0:T(8,128)S(1)}, s32[12,128]{1,0:T(8,128)S(1)}, s32[128]{0:T(128)S(1)}, s32[12,128]{1,0:T(8,128)S(1)}, /*index=5*/s32...) while((s32[]{:T(128)}, f32[12,128]{1,0:T(8,128)S(1)}, ...), condition=%wide.region_9.10_spmd, body=%wide.region_6.9_spmd.sunk | while | flops 276313600 | bytes 32562324 | solution.py:115
  71.6 1.6 gather_fusion
  73.2 8.0 %gather_fusion.1 = bf16[128,256,128]{2,1,0:T(8,128)(2,1)} fusion(bf16[32,256,128]{2,1,0:T(8,128)(2,1)} %get-tuple-element.157, s32[1024]{0:T(1024)S(1)} %pad_clamp_fusion.5), kind=kCustom, calls=%fused_computation.3.clone.1 | custom fusion | bytes 16777728 | tf_op jit(solution)/shard_map/while/body/eval_jaxpr/jit(_take)/gather | solution.py:38
  82.0 5.8 %select_reduce_fusion.4 = f32[128,32]{1,0:T(8,128)S(1)} fusion(s32[128]{0:T(128)S(1)} %get-tuple-element.125, bf16[128,256,128]{2,1,0:T(8,128)(2,1)} %gather_fusion.1, pred[128]{0:T(512)(128)(4,1)S(1)} %get-tuple-element.126, bf16[128,32,128]{2,1,0:T(8,128)(2,1)S(1)} %gather_fusion.2, pred[128]{0:T(512)(128)(4,1)S(1)} %get-tuple-element.128), kind=kOutput, calls=%fused_computation.10.clone.1 | convolution fusion | flops 276295680 | bytes 9454336 | tf_op jit(solution)/shard_map/while/body/eval_jaxpr/zxg,zwg->zxw/dot_general | solution.py:40
  89.3 1.6 gather_fusion
  90.9 8.0 %gather_fusion.1 = bf16[128,256,128]{2,1,0:T(8,128)(2,1)} fusion(bf16[32,256,128]{2,1,0:T(8,128)(2,1)} %get-tuple-element.157, s32[1024]{0:T(1024)S(1)} %pad_clamp_fusion.5), kind=kCustom, calls=%fused_computation.3.clone.1 | custom fusion | bytes 16777728 | tf_op jit(solution)/shard_map/while/body/eval_jaxpr/jit(_take)/gather | solution.py:38
  99.6 5.8 %select_reduce_fusion.4 = f32[128,32]{1,0:T(8,128)S(1)} fusion(s32[128]{0:T(128)S(1)} %get-tuple-element.125, bf16[128,256,128]{2,1,0:T(8,128)(2,1)} %gather_fusion.1, pred[128]{0:T(512)(128)(4,1)S(1)} %get-tuple-element.126, bf16[128,32,128]{2,1,0:T(8,128)(2,1)S(1)} %gather_fusion.2, pred[128]{0:T(512)(128)(4,1)S(1)} %get-tuple-element.128), kind=kOutput, calls=%fused_computation.10.clone.1 | convolution fusion | flops 276295680 | bytes 9454336 | tf_op jit(solution)/shard_map/while/body/eval_jaxpr/zxg,zwg->zxw/dot_general | solution.py:40
  107.0 1.6 gather_fusion
  108.6 7.9 %gather_fusion.1 = bf16[128,256,128]{2,1,0:T(8,128)(2,1)} fusion(bf16[32,256,128]{2,1,0:T(8,128)(2,1)} %get-tuple-element.157, s32[1024]{0:T(1024)S(1)} %pad_clamp_fusion.5), kind=kCustom, calls=%fused_computation.3.clone.1 | custom fusion | bytes 16777728 | tf_op jit(solution)/shard_map/while/body/eval_jaxpr/jit(_take)/gather | solution.py:38
  117.3 5.8 %select_reduce_fusion.4 = f32[128,32]{1,0:T(8,128)S(1)} fusion(s32[128]{0:T(128)S(1)} %get-tuple-element.125, bf16[128,256,128]{2,1,0:T(8,128)(2,1)} %gather_fusion.1, pred[128]{0:T(512)(128)(4,1)S(1)} %get-tuple-element.126, bf16[128,32,128]{2,1,0:T(8,128)(2,1)S(1)} %gather_fusion.2, pred[128]{0:T(512)(128)(4,1)S(1)} %get-tuple-element.128), kind=kOutput, calls=%fused_computation.10.clone.1 | convolution fusion | flops 276295680 | bytes 9454336 | tf_op jit(solution)/shard_map/while/body/eval_jaxpr/zxg,zwg->zxw/dot_general | solution.py:40
  124.7 1.6 gather_fusion
  126.3 8.0 %gather_fusion.1 = bf16[128,256,128]{2,1,0:T(8,128)(2,1)} fusion(bf16[32,256,128]{2,1,0:T(8,128)(2,1)} %get-tuple-element.157, s32[1024]{0:T(1024)S(1)} %pad_clamp_fusion.5), kind=kCustom, calls=%fused_computation.3.clone.1 | custom fusion | bytes 16777728 | tf_op jit(solution)/shard_map/while/body/eval_jaxpr/jit(_take)/gather | solution.py:38
  135.0 5.8 %select_reduce_fusion.4 = f32[128,32]{1,0:T(8,128)S(1)} fusion(s32[128]{0:T(128)S(1)} %get-tuple-element.125, bf16[128,256,128]{2,1,0:T(8,128)(2,1)} %gather_fusion.1, pred[128]{0:T(512)(128)(4,1)S(1)} %get-tuple-element.126, bf16[128,32,128]{2,1,0:T(8,128)(2,1)S(1)} %gather_fusion.2, pred[128]{0:T(512)(128)(4,1)S(1)} %get-tuple-element.128), kind=kOutput, calls=%fused_computation.10.clone.1 | convolution fusion | flops 276295680 | bytes 9454336 | tf_op jit(solution)/shard_map/while/body/eval_jaxpr/zxg,zwg->zxw/dot_general | solution.py:40
  142.4 1.6 gather_fusion
  144.0 8.0 %gather_fusion.1 = bf16[128,256,128]{2,1,0:T(8,128)(2,1)} fusion(bf16[32,256,128]{2,1,0:T(8,128)(2,1)} %get-tuple-element.157, s32[1024]{0:T(1024)S(1)} %pad_clamp_fusion.5), kind=kCustom, calls=%fused_computation.3.clone.1 | custom fusion | bytes 16777728 | tf_op jit(solution)/shard_map/while/body/eval_jaxpr/jit(_take)/gather | solution.py:38
  152.8 5.8 %select_reduce_fusion.4 = f32[128,32]{1,0:T(8,128)S(1)} fusion(s32[128]{0:T(128)S(1)} %get-tuple-element.125, bf16[128,256,128]{2,1,0:T(8,128)(2,1)} %gather_fusion.1, pred[128]{0:T(512)(128)(4,1)S(1)} %get-tuple-element.126, bf16[128,32,128]{2,1,0:T(8,128)(2,1)S(1)} %gather_fusion.2, pred[128]{0:T(512)(128)(4,1)S(1)} %get-tuple-element.128), kind=kOutput, calls=%fused_computation.10.clone.1 | convolution fusion | flops 276295680 | bytes 9454336 | tf_op jit(solution)/shard_map/while/body/eval_jaxpr/zxg,zwg->zxw/dot_general | solution.py:40
  160.1 1.6 gather_fusion
  161.7 8.0 %gather_fusion.1 = bf16[128,256,128]{2,1,0:T(8,128)(2,1)} fusion(bf16[32,256,128]{2,1,0:T(8,128)(2,1)} %get-tuple-element.157, s32[1024]{0:T(1024)S(1)} %pad_clamp_fusion.5), kind=kCustom, calls=%fused_computation.3.clone.1 | custom fusion | bytes 16777728 | tf_op jit(solution)/shard_map/while/body/eval_jaxpr/jit(_take)/gather | solution.py:38
  170.5 5.8 %select_reduce_fusion.4 = f32[128,32]{1,0:T(8,128)S(1)} fusion(s32[128]{0:T(128)S(1)} %get-tuple-element.125, bf16[128,256,128]{2,1,0:T(8,128)(2,1)} %gather_fusion.1, pred[128]{0:T(512)(128)(4,1)S(1)} %get-tuple-element.126, bf16[128,32,128]{2,1,0:T(8,128)(2,1)S(1)} %gather_fusion.2, pred[128]{0:T(512)(128)(4,1)S(1)} %get-tuple-element.128), kind=kOutput, calls=%fused_computation.10.clone.1 | convolution fusion | flops 276295680 | bytes 9454336 | tf_op jit(solution)/shard_map/while/body/eval_jaxpr/zxg,zwg->zxw/dot_general | solution.py:40
  177.8 1.6 gather_fusion
  179.4 8.0 %gather_fusion.1 = bf16[128,256,128]{2,1,0:T(8,128)(2,1)} fusion(bf16[32,256,128]{2,1,0:T(8,128)(2,1)} %get-tuple-element.157, s32[1024]{0:T(1024)S(1)} %pad_clamp_fusion.5), kind=kCustom, calls=%fused_computation.3.clone.1 | custom fusion | bytes 16777728 | tf_op jit(solution)/shard_map/while/body/eval_jaxpr/jit(_take)/gather | solution.py:38
  188.3 5.8 %select_reduce_fusion.4 = f32[128,32]{1,0:T(8,128)S(1)} fusion(s32[128]{0:T(128)S(1)} %get-tuple-element.125, bf16[128,256,128]{2,1,0:T(8,128)(2,1)} %gather_fusion.1, pred[128]{0:T(512)(128)(4,1)S(1)} %get-tuple-element.126, bf16[128,32,128]{2,1,0:T(8,128)(2,1)S(1)} %gather_fusion.2, pred[128]{0:T(512)(128)(4,1)S(1)} %get-tuple-element.128), kind=kOutput, calls=%fused_computation.10.clone.1 | convolution fusion | flops 276295680 | bytes 9454336 | tf_op jit(solution)/shard_map/while/body/eval_jaxpr/zxg,zwg->zxw/dot_general | solution.py:40
  195.6 1.6 gather_fusion
  197.2 8.0 %gather_fusion.1 = bf16[128,256,128]{2,1,0:T(8,128)(2,1)} fusion(bf16[32,256,128]{2,1,0:T(8,128)(2,1)} %get-tuple-element.157, s32[1024]{0:T(1024)S(1)} %pad_clamp_fusion.5), kind=kCustom, calls=%fused_computation.3.clone.1 | custom fusion | bytes 16777728 | tf_op jit(solution)/shard_map/while/body/eval_jaxpr/jit(_take)/gather | solution.py:38
  206.0 5.8 %select_reduce_fusion.4 = f32[128,32]{1,0:T(8,128)S(1)} fusion(s32[128]{0:T(128)S(1)} %get-tuple-element.125, bf16[128,256,128]{2,1,0:T(8,128)(2,1)} %gather_fusion.1, pred[128]{0:T(512)(128)(4,1)S(1)} %get-tuple-element.126, bf16[128,32,128]{2,1,0:T(8,128)(2,1)S(1)} %gather_fusion.2, pred[128]{0:T(512)(128)(4,1)S(1)} %get-tuple-element.128), kind=kOutput, calls=%fused_computation.10.clone.1 | convolution fusion | flops 276295680 | bytes 9454336 | tf_op jit(solution)/shard_map/while/body/eval_jaxpr/zxg,zwg->zxw/dot_general | solution.py:40
  213.3 1.6 gather_fusion
  214.9 8.0 %gather_fusion.1 = bf16[128,256,128]{2,1,0:T(8,128)(2,1)} fusion(bf16[32,256,128]{2,1,0:T(8,128)(2,1)} %get-tuple-element.157, s32[1024]{0:T(1024)S(1)} %pad_clamp_fusion.5), kind=kCustom, calls=%fused_computation.3.clone.1 | custom fusion | bytes 16777728 | tf_op jit(solution)/shard_map/while/body/eval_jaxpr/jit(_take)/gather | solution.py:38
  223.7 5.8 %select_reduce_fusion.4 = f32[128,32]{1,0:T(8,128)S(1)} fusion(s32[128]{0:T(128)S(1)} %get-tuple-element.125, bf16[128,256,128]{2,1,0:T(8,128)(2,1)} %gather_fusion.1, pred[128]{0:T(512)(128)(4,1)S(1)} %get-tuple-element.126, bf16[128,32,128]{2,1,0:T(8,128)(2,1)S(1)} %gather_fusion.2, pred[128]{0:T(512)(128)(4,1)S(1)} %get-tuple-element.128), kind=kOutput, calls=%fused_computation.10.clone.1 | convolution fusion | flops 276295680 | bytes 9454336 | tf_op jit(solution)/shard_map/while/body/eval_jaxpr/zxg,zwg->zxw/dot_general | solution.py:40
  231.0 1.6 gather_fusion
  232.6 8.0 %gather_fusion.1 = bf16[128,256,128]{2,1,0:T(8,128)(2,1)} fusion(bf16[32,256,128]{2,1,0:T(8,128)(2,1)} %get-tuple-element.157, s32[1024]{0:T(1024)S(1)} %pad_clamp_fusion.5), kind=kCustom, calls=%fused_computation.3.clone.1 | custom fusion | bytes 16777728 | tf_op jit(solution)/shard_map/while/body/eval_jaxpr/jit(_take)/gather | solution.py:38
  241.4 5.8 %select_reduce_fusion.4 = f32[128,32]{1,0:T(8,128)S(1)} fusion(s32[128]{0:T(128)S(1)} %get-tuple-element.125, bf16[128,256,128]{2,1,0:T(8,128)(2,1)} %gather_fusion.1, pred[128]{0:T(512)(128)(4,1)S(1)} %get-tuple-element.126, bf16[128,32,128]{2,1,0:T(8,128)(2,1)S(1)} %gather_fusion.2, pred[128]{0:T(512)(128)(4,1)S(1)} %get-tuple-element.128), kind=kOutput, calls=%fused_computation.10.clone.1 | convolution fusion | flops 276295680 | bytes 9454336 | tf_op jit(solution)/shard_map/while/body/eval_jaxpr/zxg,zwg->zxw/dot_general | solution.py:40
  248.7 1.6 gather_fusion
  250.3 8.0 %gather_fusion.1 = bf16[128,256,128]{2,1,0:T(8,128)(2,1)} fusion(bf16[32,256,128]{2,1,0:T(8,128)(2,1)} %get-tuple-element.157, s32[1024]{0:T(1024)S(1)} %pad_clamp_fusion.5), kind=kCustom, calls=%fused_computation.3.clone.1 | custom fusion | bytes 16777728 | tf_op jit(solution)/shard_map/while/body/eval_jaxpr/jit(_take)/gather | solution.py:38
  259.1 5.8 %select_reduce_fusion.4 = f32[128,32]{1,0:T(8,128)S(1)} fusion(s32[128]{0:T(128)S(1)} %get-tuple-element.125, bf16[128,256,128]{2,1,0:T(8,128)(2,1)} %gather_fusion.1, pred[128]{0:T(512)(128)(4,1)S(1)} %get-tuple-element.126, bf16[128,32,128]{2,1,0:T(8,128)(2,1)S(1)} %gather_fusion.2, pred[128]{0:T(512)(128)(4,1)S(1)} %get-tuple-element.128), kind=kOutput, calls=%fused_computation.10.clone.1 | convolution fusion | flops 276295680 | bytes 9454336 | tf_op jit(solution)/shard_map/while/body/eval_jaxpr/zxg,zwg->zxw/dot_general | solution.py:40
  266.4 1.6 gather_fusion
  268.1 8.0 %gather_fusion.1 = bf16[128,256,128]{2,1,0:T(8,128)(2,1)} fusion(bf16[32,256,128]{2,1,0:T(8,128)(2,1)} %get-tuple-element.157, s32[1024]{0:T(1024)S(1)} %pad_clamp_fusion.5), kind=kCustom, calls=%fused_computation.3.clone.1 | custom fusion | bytes 16777728 | tf_op jit(solution)/shard_map/while/body/eval_jaxpr/jit(_take)/gather | solution.py:38
  276.8 5.8 %select_reduce_fusion.4 = f32[128,32]{1,0:T(8,128)S(1)} fusion(s32[128]{0:T(128)S(1)} %get-tuple-element.125, bf16[128,256,128]{2,1,0:T(8,128)(2,1)} %gather_fusion.1, pred[128]{0:T(512)(128)(4,1)S(1)} %get-tuple-element.126, bf16[128,32,128]{2,1,0:T(8,128)(2,1)S(1)} %gather_fusion.2, pred[128]{0:T(512)(128)(4,1)S(1)} %get-tuple-element.128), kind=kOutput, calls=%fused_computation.10.clone.1 | convolution fusion | flops 276295680 | bytes 9454336 | tf_op jit(solution)/shard_map/while/body/eval_jaxpr/zxg,zwg->zxw/dot_general | solution.py:40
  283.6 18.6 %all-to-all-start.3 = ((f32[256,1,1,6]{3,2,1,0:T(1,128)}), f32[256,1,1,6]{3,2,1,0:T(1,128)S(1)}, u32[]{:S(2)}, u32[]{:S(2)}) async-start(f32[256,1,1,6]{3,2,1,0:T(1,128)} %bitcast.25), calls=%async_computation.3 | async-start | bytes 262144 | tf_op jit(solution)/shard_map/all_to_all | solution.py:32
  302.9 12.3 %all-to-all-done.3 = f32[256,1,1,6]{3,2,1,0:T(1,128)S(1)} async-done(((f32[256,1,1,6]{3,2,1,0:T(1,128)}), f32[256,1,1,6]{3,2,1,0:T(1,128)S(1)}, u32[]{:S(2)}, u32[]{:S(2)}) %all-to-all-start.3) | async-done | bytes 6176 | tf_op jit(solution)/shard_map/all_to_all | solution.py:32
  315.3 3.1 gather_fusion.4
  (184 shorter events, 37.3 us)
Async XLA Ops:
  7.2 42.0 %copy-start = (bf16[256,1280]{1,0:T(8,128)(2,1)S(1)}, bf16[256,1280]{1,0:T(8,128)(2,1)}, u32[]{:S(2)}) copy-start(bf16[256,1280]{1,0:T(8,128)(2,1)} %param.10) | copy-start | bytes 1966084
  7.2 63.1 %all-gather.2.cloned.1.call-start = ((), (), s32[]{:S(2)}) async-start(), calls=%async_computation.4 | async-start | bytes 1179648 | tf_op jit(solution)/shard_map/all_gather | solution.py:95
  14.3 29.1 %all-to-all-start.2 = ((s32[256,1,1,6]{3,2,1,0:T(1,128)}), s32[256,1,1,6]{3,2,1,0:T(1,128)S(1)}, u32[]{:S(2)}, u32[]{:S(2)}) async-start(s32[256,1,1,6]{3,2,1,0:T(1,128)} %bitcast.20), calls=%async_computation.2 | async-start | bytes 262144 | tf_op jit(solution)/shard_map/all_to_all | solution.py:32
  43.5 23.2 %all-to-all-start.1 = ((s32[256,1,1,6]{3,2,1,0:T(1,128)}), s32[256,1,1,6]{3,2,1,0:T(1,128)S(1)}, u32[]{:S(2)}, u32[]{:S(2)}) async-start(s32[256,1,1,6]{3,2,1,0:T(1,128)} %bitcast.14), calls=%async_computation.1 | async-start | bytes 262144 | tf_op jit(solution)/shard_map/all_to_all | solution.py:32
  66.7 216.9 %all-to-all-start = ((f32[8,16,256]{2,1,0:T(8,128)}), f32[8,16,256]{2,1,0:T(8,128)S(1)}, u32[]{:S(2)}, u32[]{:S(2)}) async-start(f32[8,16,256]{2,1,0:T(8,128)} %bitcast.8), calls=%async_computation | async-start | bytes 262144 | tf_op jit(solution)/shard_map/all_to_all | solution.py:16
  70.3 248.3 %copy-start.2 = (s32[16,32]{1,0:T(8,128)S(1)}, s32[16,32]{1,0:T(8,128)}, u32[]{:S(2)}) copy-start(s32[16,32]{1,0:T(8,128)} %param.15) | copy-start | bytes 6148
  73.2 8.0 %copy-start.1 = (bf16[128,32,128]{2,1,0:T(8,128)(2,1)S(1)}, bf16[128,32,128]{2,1,0:T(8,128)(2,1)}, u32[]{:S(2)}) copy-start(bf16[128,32,128]{2,1,0:T(8,128)(2,1)} %get-tuple-element.156) | copy-start | bytes 3145732 | tf_op jit(solution)/shard_map/while
  90.9 8.0 %copy-start.1 = (bf16[128,32,128]{2,1,0:T(8,128)(2,1)S(1)}, bf16[128,32,128]{2,1,0:T(8,128)(2,1)}, u32[]{:S(2)}) copy-start(bf16[128,32,128]{2,1,0:T(8,128)(2,1)} %get-tuple-element.156) | copy-start | bytes 3145732 | tf_op jit(solution)/shard_map/while
  108.6 8.0 %copy-start.1 = (bf16[128,32,128]{2,1,0:T(8,128)(2,1)S(1)}, bf16[128,32,128]{2,1,0:T(8,128)(2,1)}, u32[]{:S(2)}) copy-start(bf16[128,32,128]{2,1,0:T(8,128)(2,1)} %get-tuple-element.156) | copy-start | bytes 3145732 | tf_op jit(solution)/shard_map/while
  126.3 8.0 %copy-start.1 = (bf16[128,32,128]{2,1,0:T(8,128)(2,1)S(1)}, bf16[128,32,128]{2,1,0:T(8,128)(2,1)}, u32[]{:S(2)}) copy-start(bf16[128,32,128]{2,1,0:T(8,128)(2,1)} %get-tuple-element.156) | copy-start | bytes 3145732 | tf_op jit(solution)/shard_map/while
  144.0 8.0 %copy-start.1 = (bf16[128,32,128]{2,1,0:T(8,128)(2,1)S(1)}, bf16[128,32,128]{2,1,0:T(8,128)(2,1)}, u32[]{:S(2)}) copy-start(bf16[128,32,128]{2,1,0:T(8,128)(2,1)} %get-tuple-element.156) | copy-start | bytes 3145732 | tf_op jit(solution)/shard_map/while
  161.7 8.0 %copy-start.1 = (bf16[128,32,128]{2,1,0:T(8,128)(2,1)S(1)}, bf16[128,32,128]{2,1,0:T(8,128)(2,1)}, u32[]{:S(2)}) copy-start(bf16[128,32,128]{2,1,0:T(8,128)(2,1)} %get-tuple-element.156) | copy-start | bytes 3145732 | tf_op jit(solution)/shard_map/while
  179.4 8.1 %copy-start.1 = (bf16[128,32,128]{2,1,0:T(8,128)(2,1)S(1)}, bf16[128,32,128]{2,1,0:T(8,128)(2,1)}, u32[]{:S(2)}) copy-start(bf16[128,32,128]{2,1,0:T(8,128)(2,1)} %get-tuple-element.156) | copy-start | bytes 3145732 | tf_op jit(solution)/shard_map/while
  197.2 8.0 %copy-start.1 = (bf16[128,32,128]{2,1,0:T(8,128)(2,1)S(1)}, bf16[128,32,128]{2,1,0:T(8,128)(2,1)}, u32[]{:S(2)}) copy-start(bf16[128,32,128]{2,1,0:T(8,128)(2,1)} %get-tuple-element.156) | copy-start | bytes 3145732 | tf_op jit(solution)/shard_map/while
  214.9 8.0 %copy-start.1 = (bf16[128,32,128]{2,1,0:T(8,128)(2,1)S(1)}, bf16[128,32,128]{2,1,0:T(8,128)(2,1)}, u32[]{:S(2)}) copy-start(bf16[128,32,128]{2,1,0:T(8,128)(2,1)} %get-tuple-element.156) | copy-start | bytes 3145732 | tf_op jit(solution)/shard_map/while
  232.6 8.0 %copy-start.1 = (bf16[128,32,128]{2,1,0:T(8,128)(2,1)S(1)}, bf16[128,32,128]{2,1,0:T(8,128)(2,1)}, u32[]{:S(2)}) copy-start(bf16[128,32,128]{2,1,0:T(8,128)(2,1)} %get-tuple-element.156) | copy-start | bytes 3145732 | tf_op jit(solution)/shard_map/while
  250.3 8.0 %copy-start.1 = (bf16[128,32,128]{2,1,0:T(8,128)(2,1)S(1)}, bf16[128,32,128]{2,1,0:T(8,128)(2,1)}, u32[]{:S(2)}) copy-start(bf16[128,32,128]{2,1,0:T(8,128)(2,1)} %get-tuple-element.156) | copy-start | bytes 3145732 | tf_op jit(solution)/shard_map/while
  268.0 8.0 %copy-start.1 = (bf16[128,32,128]{2,1,0:T(8,128)(2,1)S(1)}, bf16[128,32,128]{2,1,0:T(8,128)(2,1)}, u32[]{:S(2)}) copy-start(bf16[128,32,128]{2,1,0:T(8,128)(2,1)} %get-tuple-element.156) | copy-start | bytes 3145732 | tf_op jit(solution)/shard_map/while
  283.6 31.6 %all-to-all-start.3 = ((f32[256,1,1,6]{3,2,1,0:T(1,128)}), f32[256,1,1,6]{3,2,1,0:T(1,128)S(1)}, u32[]{:S(2)}, u32[]{:S(2)}) async-start(f32[256,1,1,6]{3,2,1,0:T(1,128)} %bitcast.25), calls=%async_computation.3 | async-start | bytes 262144 | tf_op jit(solution)/shard_map/all_to_all | solution.py:32
Sparse Core Ops, SparseCore 0:
  9.8 38.9 all-gather.1
where the time goes:
time: 326 us
  local copies, waits for them, and re-layouts  155 us (48%)
  matrix products  71.4 us (22%)
  starting transfers between devices  43.4 us (13%)
  waiting for transfers between devices  23.2 us (7%)
  between operations  14.9 us (5%)
  blocking collectives  12.6 us (4%)
  other arithmetic  4.8 us (1%)
    gather x12, local copies, waits for them, and re-layouts, maxsim_block(): corpus_texts = jnp.take(passage_tokens, local_ids, axis=0)  95.9 us
    dot_general x12, matrix products, maxsim_block(): jnp.einsum('zxg,zwg->zxw', token_vectors, corpus_texts, preferred_element...  69.4 us
    all_to_all x3, starting transfers between devices, joined_exchange(): tiles = lax.all_to_all(tiles, axis, split_axis=0, concat_axis=0, tiled=True)  40 us
    all_to_all x3, waiting for transfers between devices, joined_exchange(): tiles = lax.all_to_all(tiles, axis, split_axis=0, concat_axis=0, tiled=True)  22.5 us
    gather x12, local copies, waits for them, and re-layouts, maxsim_block(): lengths = jnp.take(passage_lengths, local_ids, axis=0)  19 us
    gather x12, local copies, waits for them, and re-layouts, score_gathered(): jnp.take(all_counts, query_block, axis=0)  14.7 us
    unnamed x1, blocking collectives  12.6 us
    gather x12, local copies, waits for them, and re-layouts, score_gathered(): jnp.take(all_tokens, query_block, axis=0)  9.01 us
  transfers between devices with their start and end apart: 5, of which 2 were waited for; matrix products, arithmetic and copies ran while one was open for 70% of the time, Pallas kernels for 0%

commit v1 on v0

v1 whole, which is shorter than its diff:
```python
import jax
import jax.numpy as jnp
from jax import lax
from jax.experimental import pallas as pl
from jax.experimental.pallas import tpu as pltpu
from jax.sharding import PartitionSpec as P

f32, bf16, i32 = jnp.float32, jnp.bfloat16, jnp.int32
NT = (((1,), (1,)), ((), ()))
NN = (((1,), (0,)), ((), ()))
VM = pl.BlockSpec(memory_space=pltpu.VMEM)
SM = pl.BlockSpec(memory_space=pltpu.SMEM)
CH = 64
GRP = 8
COLS = 512


def iota(shape, dim):
    return lax.broadcasted_iota(i32, shape, dim)


def split2(x):
    hi = x.astype(bf16)
    return hi, (x - hi.astype(f32)).astype(bf16)


def route_kernel(cand_ref, send_ref, meta_ref, hot_ref):
    nq, nc = cand_ref.shape
    n = nq * nc
    owners = hot_ref.shape[0]
    ids = jnp.concatenate([cand_ref[q : q + 1, :] for q in range(nq)], axis=1)
    owner, local = ids >> 5, ids & 31
    mine = iota((owners, n), 0) == owner
    hot = jnp.where(mine, 1.0, 0.0)
    hot_b = hot.astype(bf16)
    hot_ref[...] = hot_b
    earlier = jnp.where(iota((n, n), 0) < iota((n, n), 1), 1.0, 0.0).astype(bf16)
    before = lax.dot_general(hot_b, earlier, NN, preferred_element_type=f32)
    rank = jnp.sum(hot * before, axis=0, keepdims=True).astype(i32)
    here = iota((8, n), 0) == rank
    row = (iota((1, n), 1) // nc).astype(f32)
    vals = jnp.concatenate(
        [jnp.where(here, row, 0.0), jnp.where(here, local.astype(f32), 0.0)], axis=0
    ).astype(bf16)
    vals = jnp.concatenate([vals, jnp.zeros((112, n), bf16)], axis=0)
    table = lax.dot_general(hot_b, vals, NT, preferred_element_type=f32).astype(i32)
    moved = pltpu.roll(table, 120, 1)
    send_ref[...] = jnp.where(iota(table.shape, 1) < 8, table * 65536 + moved, 0)
    meta_ref[...] = jnp.broadcast_to(rank, meta_ref.shape)


def prep_kernel(len_ref, p_ref, o_ref, sched_ref):
    count, pt, dim = p_ref.shape
    per = pt // CH

    def clean(p, _):
        rows = p_ref[p].astype(f32)
        keep = iota((pt, dim), 0) < len_ref[p]
        o_ref[p] = jnp.where(keep, rows, rows[0:1, :]).astype(bf16)
        return 0

    lax.fori_loop(0, count, clean, 0, unroll=4)

    def listed(p, at):
        live = (len_ref[p] + (CH - 1)) // CH
        sched_ref[160 + p] = at
        sched_ref[192 + p] = live
        for k in range(per):
            sched_ref[at + k] = p * pt + k * CH
        return at + live

    total = lax.fori_loop(0, count, listed, 0)
    for k in range(GRP):
        sched_ref[total + k] = 0
    sched_ref[224] = (total + GRP - 1) // GRP


def best_matches(sched_ref, p_ref, q_ref, part_ref, best_ref):
    width = q_ref.shape[0]
    count = best_ref.shape[0]

    def step(g, _):
        rows = jnp.concatenate(
            [p_ref[pl.ds(pl.multiple_of(sched_ref[g * GRP + k], CH), CH), :] for k in range(GRP)],
            axis=0,
        )
        for c in range(width // COLS):
            sim = lax.dot_general(
                rows, q_ref[c * COLS : (c + 1) * COLS, :], NT, preferred_element_type=f32
            )
            m = jnp.max(sim.reshape(GRP, CH // 8, 8, COLS), axis=1)
            part_ref[pl.ds(pl.multiple_of(g * GRP * 8, GRP * 8), GRP * 8), c * COLS : (c + 1) * COLS] = (
                m.reshape(GRP * 8, COLS)
            )
        return 0

    lax.fori_loop(0, sched_ref[224], step, 0)

    def gather(p, _):
        at, live = sched_ref[160 + p], sched_ref[192 + p]
        m = None
        for k in range(256 // CH):
            c = at + jnp.minimum(k, live - 1)
            v = part_ref[pl.ds(pl.multiple_of(c * 8, 8), 8), :]
            m = v if m is None else jnp.maximum(m, v)
        best_ref[pl.ds(p, 1), :] = jnp.max(m, axis=0, keepdims=True)
        return 0

    lax.fori_loop(0, count, gather, 0)


def query_sums(best_ref):
    count, width = best_ref.shape
    hi, lo = split2(best_ref[...])
    nq = 128
    member = jnp.where(iota((nq, width), 1) // 32 == iota((nq, width), 0), 1.0, 0.0).astype(bf16)
    s = lax.dot_general(
        jnp.concatenate([hi, lo], axis=0), member, NT, preferred_element_type=f32
    )
    return s[:count] + s[count:]


def first_kernel(sched_ref, p_ref, q_ref, t_ref, part_ref, best_ref):
    best_matches(sched_ref, p_ref, q_ref, part_ref, best_ref)
    t_ref[...] = query_sums(best_ref)


def second_kernel(sched_ref, core_ref, p_ref, q_ref, ta_ref, req_ref, o_ref, part_ref, best_ref):
    best_matches(sched_ref, p_ref, q_ref, part_ref, best_ref)
    tb = query_sums(best_ref)
    ta = ta_ref[...]
    table = jnp.where(iota(ta.shape, 1) < 64, ta, pltpu.roll(tb, 64, 1))
    hi, lo = split2(table)
    table = jnp.concatenate([hi, lo], axis=0)
    req = req_ref[...]
    src = req.shape[0]
    q = req >> 16
    local = req & 65535
    half = (q >> 3) ^ core_ref[0]
    col = half * 64 + (iota(req.shape, 0) >> 5) * 8 + (q & 7)
    lane = iota(req.shape, 1)
    lane64 = iota((src, 64), 1) & 31
    out = jnp.zeros(req.shape, f32)
    for s in range(6):
        pick = jnp.where(lane == col[:, s : s + 1], 1.0, 0.0).astype(bf16)
        x = lax.dot_general(pick, table, NT, preferred_element_type=f32)
        x = jnp.sum(jnp.where(lane64 == local[:, s : s + 1], x, 0.0), axis=1, keepdims=True)
        out = jnp.where(lane == s, x, out)
    o_ref[...] = out


def final_kernel(count_ref, ret_ref, meta_ref, hot_ref, o_ref):
    nq, nc = o_ref.shape
    t = jnp.transpose(ret_ref[...])[:8, :]
    hi, lo = split2(t)
    x = lax.dot_general(
        jnp.concatenate([hi, lo], axis=0), hot_ref[...], NN, preferred_element_type=f32
    )
    x = x[:8] + x[8:]
    row = jnp.sum(jnp.where(iota(x.shape, 0) == meta_ref[...], x, 0.0), axis=0, keepdims=True)
    for q in range(nq):
        o_ref[q : q + 1, :] = row[:, q * nc : (q + 1) * nc] / count_ref[q].astype(f32)


def call(kernel, outs, ins, out_specs=VM, in_specs=None, scratch=(), name=None):
    return pl.pallas_call(
        kernel,
        out_shape=outs,
        in_specs=[VM] * len(ins) if in_specs is None else in_specs,
        out_specs=out_specs,
        scratch_shapes=scratch,
        name=name,
    )(*ins)


def body(
    query_fixed_encoding,
    passage_fde,
    query_tokens,
    query_token_totals,
    passage_tokens,
    passage_lengths,
    candidates,
):
    groups, shards = lax.axis_size("fde"), lax.axis_size("pas")
    owners = groups * shards
    nq, qt, dim = query_tokens.shape
    count, pt, _ = passage_tokens.shape
    core = lax.axis_index("pas") % 2
    S = jax.ShapeDtypeStruct

    live = iota((nq, qt, dim), 1) < query_token_totals[:, None, None]
    mine = jnp.where(live, query_tokens, jnp.zeros((), bf16)).reshape(2, nq * qt // 2, dim)
    mine = lax.dynamic_index_in_dim(mine, core, 0, keepdims=False)
    near = lax.all_to_all(
        jnp.broadcast_to(mine[None], (groups,) + mine.shape), "fde", 0, 0, tiled=True
    ).reshape(-1, dim)
    far = lax.ppermute(near, "pas", [(k, k ^ 1) for k in range(shards)])

    send, meta, hot = call(
        route_kernel,
        (S((owners, 128), i32), S((8, nq * candidates.shape[1]), i32), S((owners, nq * candidates.shape[1]), bf16)),
        (candidates,),
        (VM, VM, VM),
        name="route",
    )
    req = lax.all_to_all(send, ("fde", "pas"), 0, 0, tiled=True)

    clean, sched = call(
        prep_kernel,
        (S(passage_tokens.shape, bf16), S((256,), i32)),
        (passage_lengths, passage_tokens),
        (VM, SM),
        [SM, VM],
        name="prep",
    )
    clean = clean.reshape(count * pt, dim)

    partial = jnp.einsum(
        "qf,pf->qp", query_fixed_encoding, passage_fde, preferred_element_type=f32
    )
    tiles = lax.all_to_all(partial.reshape(groups, nq, -1), "fde", 0, 0, tiled=True)
    fde_scores = jnp.sum(tiles, axis=0)

    width = near.shape[0]
    scratch = [pltpu.VMEM((count * pt // CH * 8, width), f32), pltpu.VMEM((count, width), f32)]
    ta = call(
        first_kernel, S((count, 128), f32), (sched, clean, near), VM, [SM, VM, VM], scratch, "first"
    )
    resp = call(
        second_kernel,
        S((owners, 128), f32),
        (sched, core.reshape(1), clean, far, ta, req),
        VM,
        [SM, SM, VM, VM, VM, VM],
        scratch,
        "second",
    )
    ret = lax.all_to_all(resp, ("fde", "pas"), 0, 0, tiled=True)
    rerank = call(
        final_kernel,
        S(candidates.shape, f32),
        (query_token_totals, ret, meta[:1], hot),
        VM,
        [SM, VM, VM, VM],
        name="final",
    )
    return fde_scores, rerank


def solution(mesh):
    return jax.shard_map(
        body,
        mesh=mesh,
        in_specs=(
            P(None, "fde"),
            P("pas", "fde"),
            P("fde", None, None),
            P("fde"),
            P(("fde", "pas"), None, None),
            P(("fde", "pas")),
            P("fde", "pas"),
        ),
        out_specs=(P("fde", "pas"), P("fde", "pas")),
        check_vma=False,
    )
```

time: 326 us -> 110 us (0.34)
  local copies, waits for them, and re-layouts: 155 us -> 2.86 us
  matrix products: 71.4 us -> 1.03 us
  Pallas kernels: 0 us -> 30.6 us
  starting transfers between devices: 43.4 us -> 24.4 us
  between operations: 14.9 us -> 0.75 us
  blocking collectives: 12.6 us -> 24.9 us
    gather x50 -> x0, local copies, waits for them, and re-layouts: 142 us -> none  [the longest x12 95.9 us: maxsim_block(): corpus_texts = jnp.take(passage_tokens, local_ids, axis=0)]
    dot_general x12 -> x0, matrix products: 69.4 us -> none  [maxsim_block(): jnp.einsum('zxg,zwg->zxw', token_vectors, corpus_texts, preferred_element...]
    pallas_call x0 -> x5, Pallas kernels: none -> 30.6 us  [call(): pl.pallas_call(kernel, out_shape=outs, in_specs=[VM] * len(ins) if in_spe...]
    all_to_all x0 -> x1, blocking collectives: none -> 24.9 us  [body(): lax.all_to_all(jnp.broadcast_to(mine[None], (groups,) + mine.shape), 'fde...]
    all_to_all x4 -> x3, starting transfers between devices: 43.4 us -> 22.1 us  [the longest x1 11.1 us: body(): ret = lax.all_to_all(resp, ('fde', 'pas'), 0, 0, tiled=True)]
    unnamed x1 -> x0, blocking collectives: 12.6 us -> none
    scatter x2 -> x0, local copies, waits for them, and re-layouts: 4.9 us -> none  [the longest x1 2.45 us: body(): send_local = jnp.zeros((slot_count,), jnp.int32).at[target].set(local_ids)]
    all_to_all x4 -> x3, waiting for transfers between devices: 22.5 us -> 23 us  [the longest x1 11.9 us: body(): req = lax.all_to_all(send, ('fde', 'pas'), 0, 0, tiled=True)]
  transfers between devices with their start and end apart: 5 -> 4, of which waited for: 2 -> 2; matrix products, arithmetic and copies ran while one was open for 70% -> 3% of each run, Pallas kernels for 0% -> 26%
where the time goes in v1:
time: 110 us; the launch traced here: 109 us
  Pallas kernels  30.6 us (28%)
  blocking collectives  24.9 us (23%)
  starting transfers between devices  24.4 us (22%)
  waiting for transfers between devices  23 us (21%)
  local copies, waits for them, and re-layouts  2.86 us (3%)
  other arithmetic  1.7 us (2%)
    pallas_call x5, Pallas kernels, call(): pl.pallas_call(kernel, out_shape=outs, in_specs=[VM] * len(ins) if in_spe...  30.6 us
    all_to_all x1, blocking collectives, body(): lax.all_to_all(jnp.broadcast_to(mine[None], (groups,) + mine.shape), 'fde...  24.9 us
    all_to_all x1, waiting for transfers between devices, body(): req = lax.all_to_all(send, ('fde', 'pas'), 0, 0, tiled=True)  11.9 us
    all_to_all x1, starting transfers between devices, body(): ret = lax.all_to_all(resp, ('fde', 'pas'), 0, 0, tiled=True)  11.1 us
    all_to_all x1, waiting for transfers between devices, body(): ret = lax.all_to_all(resp, ('fde', 'pas'), 0, 0, tiled=True)  11.1 us
    all_to_all x1, starting transfers between devices, body(): req = lax.all_to_all(send, ('fde', 'pas'), 0, 0, tiled=True)  7.64 us
    all_to_all x1, starting transfers between devices, body(): lax.all_to_all(partial.reshape(groups, nq, -1), 'fde', 0, 0, tiled=True)  3.37 us
    ppermute x1, starting transfers between devices, body(): far = lax.ppermute(near, 'pas', [(k, k ^ 1) for k in range(shards)])  2.34 us
  transfers between devices with their start and end apart: 4, of which 2 were waited for; matrix products, arithmetic and copies ran while one was open for 3% of the time, Pallas kernels for 26%

profile of v1, /device:TPU:1, one launch (start us, length us, event | category | flops | bytes accessed | tf_op | source)
XLA Modules:
  0.0 109.3 jit_solution(14380763757788250005)
XLA Ops:
  0.6 0.0 copy-start
  0.6 0.0 copy-start.5
  0.7 1.1 fusion
  1.8 0.1 broadcast_in_dim.15
  1.9 24.9 %all_to_all.32 = bf16[8,256,128]{2,1,0:T(8,128)(2,1)S(1)} all-to-all(bf16[8,256,128]{2,1,0:T(8,128)(2,1)S(1)} %broadcast_in_dim.15), channel_id=1, replica_groups=mesh['fde'=8,'pas'=32] {'fde'}, dimensions={0} | all-to-all | bytes 1048576 | tf_op jit(solution)/shard_map/all_to_all | solution.py:195
  26.8 0.0 copy-start.1
  26.8 2.3 %collective-permute-start = (bf16[2048,128]{1,0:T(8,128)(2,1)S(1)}, bf16[2048,128]{1,0:T(8,128)(2,1)S(1)}, u32[]{:S(2)}, u32[]{:S(2)}) collective-permute-start(bf16[2048,128]{1,0:T(8,128)(2,1)S(1)} %bitcast.19), channel_id=1, source_target_pairs={{0,1},{1,0},{2,3},{3,2},{4,5},{5,4},{6,7},{7,6},{8,9},{9,8},{10,11... | collective-permute-start | bytes 1572872 | tf_op jit(solution)/shard_map/ppermute | solution.py:198
  29.1 2.1 %route.1 = (s32[256,128]{1,0:T(8,128)}, s32[8,512]{1,0:T(8,128)}, bf16[256,512]{1,0:T(8,128)(2,1)}) custom-call(s32[16,32]{1,0:T(8,128)} %cand_ref.1), custom_call_target="tpu_custom_call" | custom-call | tf_op jit(solution)/shard_map/route/pallas_call | solution.py:166
  31.2 7.6 %all-to-all-start.2 = ((s32[256,1,128]{2,1,0:T(1,128)}), s32[256,1,128]{2,1,0:T(1,128)S(1)}, u32[]{:S(2)}, u32[]{:S(2)}) async-start(s32[256,1,128]{2,1,0:T(1,128)} %bitcast.25), calls=%async_computation.2 | async-start | bytes 262144 | tf_op jit(solution)/shard_map/all_to_all | solution.py:207
  38.8 0.0 copy-done
  38.8 0.0 copy-done.5
  38.8 1.0 fusion.1
  39.9 11.9 %all-to-all-done.2 = s32[256,1,128]{2,1,0:T(1,128)S(1)} async-done(((s32[256,1,128]{2,1,0:T(1,128)}), s32[256,1,128]{2,1,0:T(1,128)S(1)}, u32[]{:S(2)}, u32[]{:S(2)}) %all-to-all-start.2) | async-done | bytes 131104 | tf_op jit(solution)/shard_map/all_to_all | solution.py:207
  51.8 0.0 copy-start.2
  51.8 3.4 %all-to-all-start = ((f32[8,16,256]{2,1,0:T(8,128)}), f32[8,16,256]{2,1,0:T(8,128)S(1)}, u32[]{:S(2)}, u32[]{:S(2)}) async-start(f32[8,16,256]{2,1,0:T(8,128)} %bitcast), calls=%async_computation | async-start | bytes 262144 | tf_op jit(solution)/shard_map/all_to_all | solution.py:222
  55.2 3.9 %prep.1 = (bf16[32,256,128]{2,1,0:T(8,128)(2,1)}, s32[256]{0:T(256)}) custom-call(s32[32]{0:T(128)} %len_ref.1, bf16[32,256,128]{2,1,0:T(8,128)(2,1)} %p_ref.1), custom_call_target="tpu_custom_call" | custom-call | tf_op jit(solution)/shard_map/prep/pallas_call | solution.py:166
  59.1 0.0 copy-done.1
  59.1 10.9 %first.1.ta_ref = f32[32,128]{1,0:T(8,128)} custom-call(s32[256]{0:T(256)} %get-tuple-element.7.sched_ref, bf16[8192,128]{1,0:T(8,128)(2,1)} %bitcast.17, bf16[2048,128]{1,0:T(8,128)(2,1)} %bitcast.20), custom_call_target="tpu_custom_call" | custom-call | tf_op jit(solution)/shard_map/first/pallas_call | solution.py:166
  70.0 0.0 copy-done.2
  70.1 0.0 collective-permute-done.q_ref
  70.1 0.0 copy-start.4
  70.1 0.8 copy-done.4
  70.9 11.8 %second.1 = f32[256,128]{1,0:T(8,128)} custom-call(s32[256]{0:T(256)} %get-tuple-element.7.sched_ref, s32[1]{0:T(128)} %bitcast.1.core_ref, bf16[8192,128]{1,0:T(8,128)(2,1)} %bitcast.18, bf16[2048,128]{1,0:T(8,128)(2,1)} %copy-done.4, f32[32,128]{1,0:T(8,128)} %first.1.ta_ref, s32[256,128]{1,0:T(8,128)} %bitcast.21), custom_call_target="tpu_custom_call" | custom-call | tf_op jit(solution)/shard_map/second/pallas_call | solution.py:166
  82.7 0.0 all-to-all-done
  82.7 11.1 %all-to-all-start.3 = ((f32[256,1,128]{2,1,0:T(1,128)}), f32[256,1,128]{2,1,0:T(1,128)S(1)}, u32[]{:S(2)}, u32[]{:S(2)}) async-start(f32[256,1,128]{2,1,0:T(1,128)} %bitcast.22), calls=%async_computation.3 | async-start | bytes 262144 | tf_op jit(solution)/shard_map/all_to_all | solution.py:239
  93.8 1.3 %slice.3.meta_ref = s32[1,512]{1,0:T(1,128)} slice(s32[8,512]{1,0:T(8,128)} %get-tuple-element.10), slice={[0:1], [0:512]} | slice | bytes 4096 | tf_op jit(solution)/shard_map/slice | solution.py:243
  95.1 0.6 reduce_sum.9
  95.7 11.1 %all-to-all-done.3 = f32[256,1,128]{2,1,0:T(1,128)S(1)} async-done(((f32[256,1,128]{2,1,0:T(1,128)}), f32[256,1,128]{2,1,0:T(1,128)S(1)}, u32[]{:S(2)}, u32[]{:S(2)}) %all-to-all-start.3) | async-done | bytes 131104 | tf_op jit(solution)/shard_map/all_to_all | solution.py:239
  106.8 0.0 copy-start.3
  106.8 0.6 copy-done.3
  107.4 1.9 %final.1 = f32[16,32]{1,0:T(8,128)} custom-call(s32[16]{0:T(128)} %count_ref.1, f32[256,128]{1,0:T(8,128)} %bitcast.23, s32[1,512]{1,0:T(1,128)} %slice.3.meta_ref, bf16[256,512]{1,0:T(8,128)(2,1)} %get-tuple-element.11.hot_ref), custom_call_target="tpu_custom_call" | custom-call | tf_op jit(solution)/shard_map/final/pallas_call | solution.py:166
  (1 shorter events, 0.0 us)
Async XLA Ops:
  0.6 38.2 %copy-start = (bf16[256,1280]{1,0:T(8,128)(2,1)S(1)}, bf16[256,1280]{1,0:T(8,128)(2,1)}, u32[]{:S(2)}) copy-start(bf16[256,1280]{1,0:T(8,128)(2,1)} %param.8) | copy-start | bytes 1966084
  0.6 38.2 %copy-start.5 = (bf16[128,1280]{1,0:T(8,128)(2,1)S(1)}, bf16[128,1280]{1,0:T(8,128)(2,1)}, u32[]{:S(2)}) copy-start(bf16[128,1280]{1,0:T(8,128)(2,1)} %param.7) | copy-start | bytes 983044
  26.8 32.3 %copy-start.1 = (bf16[8,256,128]{2,1,0:T(8,128)(2,1)}, bf16[8,256,128]{2,1,0:T(8,128)(2,1)S(1)}, u32[]{:S(2)}) copy-start(bf16[8,256,128]{2,1,0:T(8,128)(2,1)S(1)} %all_to_all.32) | copy-start | bytes 1572868
  26.8 43.3 %collective-permute-start = (bf16[2048,128]{1,0:T(8,128)(2,1)S(1)}, bf16[2048,128]{1,0:T(8,128)(2,1)S(1)}, u32[]{:S(2)}, u32[]{:S(2)}) collective-permute-start(bf16[2048,128]{1,0:T(8,128)(2,1)S(1)} %bitcast.19), channel_id=1, source_target_pairs={{0,1},{1,0},{2,3},{3,2},{4,5},{5,4},{6,7},{7,6},{8,9},{9,8},{10,11... | collective-permute-start | bytes 1572872 | tf_op jit(solution)/shard_map/ppermute | solution.py:198
  31.2 20.6 %all-to-all-start.2 = ((s32[256,1,128]{2,1,0:T(1,128)}), s32[256,1,128]{2,1,0:T(1,128)S(1)}, u32[]{:S(2)}, u32[]{:S(2)}) async-start(s32[256,1,128]{2,1,0:T(1,128)} %bitcast.25), calls=%async_computation.2 | async-start | bytes 262144 | tf_op jit(solution)/shard_map/all_to_all | solution.py:207
  51.8 18.2 %copy-start.2 = (s32[256,1,128]{2,1,0:T(1,128)}, s32[256,1,128]{2,1,0:T(1,128)S(1)}, u32[]{:S(2)}) copy-start(s32[256,1,128]{2,1,0:T(1,128)S(1)} %all-to-all-done.2) | copy-start | bytes 393220
  51.8 30.8 %all-to-all-start = ((f32[8,16,256]{2,1,0:T(8,128)}), f32[8,16,256]{2,1,0:T(8,128)S(1)}, u32[]{:S(2)}, u32[]{:S(2)}) async-start(f32[8,16,256]{2,1,0:T(8,128)} %bitcast), calls=%async_computation | async-start | bytes 262144 | tf_op jit(solution)/shard_map/all_to_all | solution.py:222
  70.1 0.8 copy-start.4
  82.7 24.1 %all-to-all-start.3 = ((f32[256,1,128]{2,1,0:T(1,128)}), f32[256,1,128]{2,1,0:T(1,128)S(1)}, u32[]{:S(2)}, u32[]{:S(2)}) async-start(f32[256,1,128]{2,1,0:T(1,128)} %bitcast.22), calls=%async_computation.3 | async-start | bytes 262144 | tf_op jit(solution)/shard_map/all_to_all | solution.py:239
  106.8 0.7 copy-start.3

commit v2 on v1

v2 whole, which is shorter than its diff:
```python
import jax
import jax.numpy as jnp
from jax import lax
from jax.experimental import pallas as pl
from jax.experimental.pallas import tpu as pltpu
from jax.sharding import PartitionSpec as P


f32, bf16, i32 = jnp.float32, jnp.bfloat16, jnp.int32
NT = (((1,), (1,)), ((), ()))
TN = (((0,), (0,)), ((), ()))
VM = pl.BlockSpec(memory_space=pltpu.VMEM)
SM = pl.BlockSpec(memory_space=pltpu.SMEM)
CH = 64
GRP = 8
COLS = 512


def iota(shape, dim):
    return lax.broadcasted_iota(i32, shape, dim)


def split2(x):
    hi = x.astype(bf16)
    return hi, (x - hi.astype(f32)).astype(bf16)


def prep_kernel(len_ref, p_ref, o_ref, sched_ref):
    count, pt, dim = p_ref.shape
    per = pt // CH

    def clean(p, _):
        rows = p_ref[p].astype(f32)
        keep = iota((pt, dim), 0) < len_ref[p]
        o_ref[p] = jnp.where(keep, rows, rows[0:1, :]).astype(bf16)
        return 0

    lax.fori_loop(0, count, clean, 0, unroll=4)

    def listed(p, at):
        live = (len_ref[p] + (CH - 1)) // CH
        sched_ref[160 + p] = at
        sched_ref[192 + p] = live
        for k in range(per):
            sched_ref[at + k] = p * pt + k * CH
        return at + live

    total = lax.fori_loop(0, count, listed, 0)
    for k in range(GRP):
        sched_ref[total + k] = 0
    sched_ref[224] = (total + GRP - 1) // GRP


def best_matches(sched_ref, p_ref, q_ref, part_ref, best_ref):
    width = q_ref.shape[0]
    count = best_ref.shape[0]

    def step(g, _):
        rows = jnp.concatenate(
            [p_ref[pl.ds(pl.multiple_of(sched_ref[g * GRP + k], CH), CH), :] for k in range(GRP)],
            axis=0,
        )
        for c in range(width // COLS):
            sim = lax.dot_general(
                rows, q_ref[c * COLS : (c + 1) * COLS, :], NT, preferred_element_type=f32
            )
            m = jnp.max(sim.reshape(GRP, CH // 8, 8, COLS), axis=1)
            part_ref[pl.ds(pl.multiple_of(g * GRP * 8, GRP * 8), GRP * 8), c * COLS : (c + 1) * COLS] = (
                m.reshape(GRP * 8, COLS)
            )
        return 0

    lax.fori_loop(0, sched_ref[224], step, 0)

    def gather(p, _):
        at, live = sched_ref[160 + p], sched_ref[192 + p]
        m = None
        for k in range(256 // CH):
            c = at + jnp.minimum(k, live - 1)
            v = part_ref[pl.ds(pl.multiple_of(c * 8, 8), 8), :]
            m = v if m is None else jnp.maximum(m, v)
        best_ref[pl.ds(p, 1), :] = jnp.max(m, axis=0, keepdims=True)
        return 0

    lax.fori_loop(0, count, gather, 0)


def query_sums(best_ref):
    count, width = best_ref.shape
    nq = width // 32
    r = iota((nq, width), 0)
    member = jnp.where(iota((nq, width), 1) // 32 == (r & 7) * 8 + (r >> 3), 1.0, 0.0).astype(bf16)
    hi, lo = split2(best_ref[...])
    s = lax.dot_general(member, jnp.concatenate([hi, lo], axis=0), NT, preferred_element_type=f32)
    s = s[:, :count] + s[:, count:]
    return jnp.concatenate([s[k * 8 : k * 8 + 8] for k in range(nq // 8)], axis=1)


def first_kernel(sched_ref, p_ref, q_ref, t_ref, part_ref, best_ref):
    best_matches(sched_ref, p_ref, q_ref, part_ref, best_ref)
    t_ref[...] = query_sums(best_ref)


def second_kernel(sched_ref, core_ref, p_ref, q_ref, near_ref, o_ref, part_ref, best_ref):
    best_matches(sched_ref, p_ref, q_ref, part_ref, best_ref)
    near, far = near_ref[...], query_sums(best_ref)
    low = core_ref[0] == 0
    wide = jnp.concatenate([jnp.where(low, near, far), jnp.where(low, far, near)], axis=1)
    for g in range(o_ref.shape[1]):
        o_ref[:, g, :] = wide[:, g * 128 : (g + 1) * 128]


def final_kernel(count_ref, core_ref, cand_ref, near_ref, far_ref, o_ref):
    nq, nc = o_ref.shape
    rows = near_ref.shape[0]
    ids = jnp.concatenate([cand_ref[q : q + 1, :] for q in range(nq)], axis=1)
    owner, local = ids >> 5, ids & 31
    m = iota((rows, 1), 0)
    at = (m & 7) * 32 + (m >> 3) * 2
    step = 128 // nc
    out = []
    for g in range(nq // step):
        lanes = slice(g * 128, (g + 1) * 128)
        own, want = owner[:, lanes], local[:, lanes] + (iota((1, 128), 1) // nc) * 32
        x = None
        for ref, c in ((near_ref, core_ref[0]), (far_ref, 1 - core_ref[0])):
            hot = jnp.where(at + c == own, 1.0, 0.0).astype(bf16)
            for part in split2(ref[:, g, :]):
                y = lax.dot_general(part, hot, TN, preferred_element_type=f32)
                x = y if x is None else x + y
        out.append(jnp.sum(jnp.where(iota(x.shape, 0) == want, x, 0.0), axis=0, keepdims=True))
    for q in range(nq):
        row = out[q // step][:, (q % step) * nc : (q % step + 1) * nc]
        o_ref[q : q + 1, :] = row / count_ref[q].astype(f32)


def call(kernel, outs, ins, out_specs=VM, in_specs=None, scratch=()):
    return pl.pallas_call(
        kernel,
        out_shape=outs,
        in_specs=[VM] * len(ins) if in_specs is None else in_specs,
        out_specs=out_specs,
        scratch_shapes=scratch,
    )(*ins)


def body(
    query_fixed_encoding,
    passage_fde,
    query_tokens,
    query_token_totals,
    passage_tokens,
    passage_lengths,
    candidates,
):
    groups, shards = lax.axis_size("fde"), lax.axis_size("pas")
    nq, qt, dim = query_tokens.shape
    count, pt, _ = passage_tokens.shape
    core = lax.axis_index("pas") % 2
    swap = [(k, k ^ 1) for k in range(shards)]
    S = jax.ShapeDtypeStruct

    live = iota((nq, qt, dim), 1) < query_token_totals[:, None, None]
    mine = jnp.where(live, query_tokens, jnp.zeros((), bf16)).reshape(2, nq * qt // 2, dim)
    mine = lax.dynamic_index_in_dim(mine, core, 0, keepdims=False)
    tiles = jnp.broadcast_to(mine[None], (groups,) + mine.shape)
    near = lax.all_to_all(tiles, "fde", 0, 0, tiled=True)
    near = near.reshape(-1, dim)
    far = lax.ppermute(near, "pas", swap)

    clean, sched = call(
        prep_kernel,
        (S(passage_tokens.shape, bf16), S((256,), i32)),
        (passage_lengths, passage_tokens),
        (VM, SM),
        [SM, VM],
    )
    clean = clean.reshape(count * pt, dim)

    partial = lax.dot_general(
        query_fixed_encoding, passage_fde, NT, preferred_element_type=f32
    )
    tiles = lax.all_to_all(partial.reshape(groups, nq, -1), "fde", 0, 0, tiled=True)
    fde_scores = jnp.sum(tiles, axis=0)

    width = near.shape[0]
    scratch = [pltpu.VMEM((count * pt // CH * 8, width), f32), pltpu.VMEM((count, width), f32)]
    near_sums = call(
        first_kernel,
        S((groups, nq // 2 * count), f32),
        (sched, clean, near),
        VM,
        [SM, VM, VM],
        scratch,
    )
    sums = call(
        second_kernel,
        S((groups, nq * count // 128, 128), f32),
        (sched, core.reshape(1), clean, far, near_sums),
        VM,
        [SM, SM, VM, VM, VM],
        scratch,
    )
    mine = lax.all_to_all(sums, "fde", 0, 0, tiled=True)
    half = shards // 2
    near = lax.all_to_all(
        jnp.broadcast_to(mine[None], (half,) + mine.shape),
        "pas",
        0,
        0,
        axis_index_groups=[[2 * k + c for k in range(half)] for c in range(2)],
        tiled=True,
    ).reshape(half * groups, -1, 128)
    far = lax.ppermute(near, "pas", swap)
    rerank = call(
        final_kernel,
        S(candidates.shape, f32),
        (query_token_totals, core.reshape(1), candidates, near, far),
        VM,
        [SM, SM, VM, VM, VM],
    )
    return fde_scores, rerank


def solution(mesh):
    return jax.shard_map(
        body,
        mesh=mesh,
        in_specs=(
            P(None, "fde"),
            P("pas", "fde"),
            P("fde", None, None),
            P("fde"),
            P(("fde", "pas"), None, None),
            P(("fde", "pas")),
            P("fde", "pas"),
        ),
        out_specs=(P("fde", "pas"), P("fde", "pas")),
        check_vma=False,
    )
```

time: 110 us -> 101 us (0.918)
  blocking collectives: 24.9 us -> 60.3 us
  waiting for transfers between devices: 23 us -> 0.01 us
  starting transfers between devices: 24.4 us -> 5.15 us
  local copies, waits for them, and re-layouts: 2.86 us -> 1.65 us
    all_to_all x1 -> x4, blocking collectives: 24.9 us -> 60.3 us  [the longest x1 24.9 us: body(): near = lax.all_to_all(tiles, 'fde', 0, 0, tiled=True)]
    all_to_all x3 -> x0, waiting for transfers between devices: 23 us -> none  [the longest x1 11.9 us: body(): req = lax.all_to_all(send, ('fde', 'pas'), 0, 0, tiled=True)]
    all_to_all x3 -> x0, starting transfers between devices: 22.1 us -> none  [the longest x1 11.1 us: body(): ret = lax.all_to_all(resp, ('fde', 'pas'), 0, 0, tiled=True)]
    ppermute x1 -> x2, starting transfers between devices: 2.34 us -> 5.15 us  [body(): far = lax.ppermute(near, 'pas', swap)]
    slice x1 -> x0, local copies, waits for them, and re-layouts: 1.3 us -> none  [body(): meta[:1]]
    pallas_call x5 -> x4, Pallas kernels: 30.6 us -> 30.9 us  [call(): pl.pallas_call(kernel, out_shape=outs, in_specs=[VM] * len(ins) if in_spe...]
  transfers between devices with their start and end apart: 4 -> 2, of which waited for: 2 -> 0; matrix products, arithmetic and copies ran while one was open for 3% -> 1% of each run, Pallas kernels for 26% -> 16%
where the time goes in v2:
time: 101 us
  blocking collectives  60.3 us (60%)
  Pallas kernels  30.9 us (31%)
  starting transfers between devices  5.15 us (5%)
  other arithmetic  1.68 us (2%)
  local copies, waits for them, and re-layouts  1.65 us (2%)
    pallas_call x4, Pallas kernels, call(): pl.pallas_call(kernel, out_shape=outs, in_specs=[VM] * len(ins) if in_spe...  30.9 us
    all_to_all x1, blocking collectives, body(): near = lax.all_to_all(tiles, 'fde', 0, 0, tiled=True)  24.9 us
    all_to_all x1, blocking collectives, body(): lax.all_to_all(jnp.broadcast_to(mine[None], (half,) + mine.shape), 'pas',...  13.7 us
    all_to_all x1, blocking collectives, body(): lax.all_to_all(partial.reshape(groups, nq, -1), 'fde', 0, 0, tiled=True)  11.9 us
    all_to_all x1, blocking collectives, body(): mine = lax.all_to_all(sums, 'fde', 0, 0, tiled=True)  9.86 us
    ppermute x2, starting transfers between devices, body(): far = lax.ppermute(near, 'pas', swap)  5.15 us
  transfers between devices with their start and end apart: 2, of which 0 were waited for; matrix products, arithmetic and copies ran while one was open for 1% of the time, Pallas kernels for 16%

profile of v2, /device:TPU:1, one launch (start us, length us, event | category | flops | bytes accessed | tf_op | source)
XLA Modules:
  0.0 100.8 jit_solution(8007968993823551455)
XLA Ops:
  0.6 0.0 copy-start
  0.7 1.1 %fusion = bf16[16,32,128]{2,1,0:T(8,128)(2,1)S(1)} fusion(bf16[16,32,128]{2,1,0:T(8,128)(2,1)} %param.9, s32[16]{0:T(128)} %count_ref.1), kind=kLoop, calls=%fused_computation.1 | loop fusion | flops 131072 | bytes 262208 | tf_op jit(solution)/shard_map/jit(_where)/select_n | solution.py:164
  1.8 0.1 broadcast_in_dim.21
  1.8 24.9 %all_to_all.20 = bf16[8,256,128]{2,1,0:T(8,128)(2,1)S(1)} all-to-all(bf16[8,256,128]{2,1,0:T(8,128)(2,1)S(1)} %broadcast_in_dim.21), channel_id=1, replica_groups=mesh['fde'=8,'pas'=32] {'fde'}, dimensions={0} | all-to-all | bytes 1048576 | tf_op jit(solution)/shard_map/all_to_all | solution.py:167
  26.7 0.0 copy-start.1
  26.8 2.3 %collective-permute-start = (bf16[2048,128]{1,0:T(8,128)(2,1)S(1)}, bf16[2048,128]{1,0:T(8,128)(2,1)S(1)}, u32[]{:S(2)}, u32[]{:S(2)}) collective-permute-start(bf16[2048,128]{1,0:T(8,128)(2,1)S(1)} %bitcast.12), channel_id=1, source_target_pairs={{0,1},{1,0},{2,3},{3,2},{4,5},{5,4},{6,7},{7,6},{8,9},{9,8},{10,11... | collective-permute-start | bytes 1572872 | tf_op jit(solution)/shard_map/ppermute | solution.py:169
  29.1 3.9 %shard_map.86 = (bf16[32,256,128]{2,1,0:T(8,128)(2,1)}, s32[256]{0:T(256)}) custom-call(s32[32]{0:T(128)} %len_ref.1, bf16[32,256,128]{2,1,0:T(8,128)(2,1)} %p_ref.1), custom_call_target="tpu_custom_call" | custom-call | tf_op jit(solution)/shard_map/pallas_call | solution.py:138
  33.0 0.0 copy-done.1
  33.0 11.8 %shard_map.87.near_ref = f32[8,256]{1,0:T(8,128)} custom-call(s32[256]{0:T(256)} %get-tuple-element.4.sched_ref, bf16[8192,128]{1,0:T(8,128)(2,1)} %bitcast.10, bf16[2048,128]{1,0:T(8,128)(2,1)} %bitcast.13), custom_call_target="tpu_custom_call" | custom-call | tf_op jit(solution)/shard_map/pallas_call | solution.py:138
  44.8 0.0 copy-start.4
  44.8 0.0 collective-permute-done.q_ref
  44.8 0.0 copy-start.3
  44.8 0.8 copy-done.3
  45.6 11.9 %shard_map.88 = f32[8,4,128]{2,1,0:T(4,128)} custom-call(s32[256]{0:T(256)} %get-tuple-element.4.sched_ref, s32[1]{0:T(128)} %bitcast.1.core_ref, bf16[8192,128]{1,0:T(8,128)(2,1)} %bitcast.11, bf16[2048,128]{1,0:T(8,128)(2,1)} %copy-done.3, f32[8,256]{1,0:T(8,128)} %shard_map.87.near_ref), custom_call_target="tpu_custom_call" | custom-call | tf_op jit(solution)/shard_map/pallas_call | solution.py:138
  57.5 9.9 %all_to_all.21 = f32[8,4,128]{2,1,0:T(4,128)S(1)} all-to-all(f32[8,4,128]{2,1,0:T(4,128)} %shard_map.88), channel_id=1, replica_groups=mesh['fde'=8,'pas'=32] {'fde'}, dimensions={0} | all-to-all | bytes 32768 | tf_op jit(solution)/shard_map/all_to_all | solution.py:204
  67.4 13.7 %all_to_all.22 = f32[16,8,4,128]{3,2,1,0:T(4,128)S(1)} all-to-all(f32[16,8,4,128]{3,2,1,0:T(4,128)S(1)} %broadcast_in_dim.22), channel_id=1, replica_groups={{0,2,4,6,8,10,12,14,16,18,20,22,24,26,28,30},{1,3,5,7,9,11,13,15,17,19,..., dimensions={0} | all-to-all | bytes 524288 | tf_op jit(solution)/shard_map/all_to_all | solution.py:206
  81.1 0.0 copy-start.2
  81.1 2.8 %collective-permute-start.1 = (f32[128,4,128]{2,1,0:T(4,128)S(1)}, f32[128,4,128]{2,1,0:T(4,128)S(1)}, u32[]{:S(2)}, u32[]{:S(2)}) collective-permute-start(f32[128,4,128]{2,1,0:T(4,128)S(1)} %bitcast.14), channel_id=1, source_target_pairs={{0,1},{1,0},{2,3},{3,2},{4,5},{5,4},{6,7},{7,6},{8,9},{9,8},{10,11... | collective-permute-start | bytes 786440 | tf_op jit(solution)/shard_map/ppermute | solution.py:214
  83.9 0.0 copy-done
  83.9 0.0 copy-done.4
  83.9 0.4 fusion.1
  84.3 11.9 %all_to_all.23 = f32[8,16,256]{2,1,0:T(8,128)S(1)} all-to-all(f32[8,16,256]{2,1,0:T(8,128)S(1)} %bitcast.16), channel_id=1, replica_groups=mesh['fde'=8,'pas'=32] {'fde'}, dimensions={0} | all-to-all | bytes 262144 | tf_op jit(solution)/shard_map/all_to_all | solution.py:183
  96.1 0.6 reduce_sum.9
  96.8 0.0 collective-permute-done.1.far_ref
  96.8 0.0 copy-done.2
  96.8 0.0 copy-start.5
  96.8 0.7 copy-done.5
  97.5 3.3 %shard_map.89 = f32[16,32]{1,0:T(8,128)} custom-call(s32[16]{0:T(128)} %count_ref.1, s32[1]{0:T(128)} %bitcast.1.core_ref, s32[16,32]{1,0:T(8,128)} %cand_ref.1, f32[128,4,128]{2,1,0:T(4,128)} %bitcast.15, f32[128,4,128]{2,1,0:T(4,128)} %copy-done.5), custom_call_target="tpu_custom_call" | custom-call | tf_op jit(solution)/shard_map/pallas_call | solution.py:138
  (2 shorter events, 0.1 us)
Async XLA Ops:
  0.6 83.3 %copy-start = (bf16[256,1280]{1,0:T(8,128)(2,1)S(1)}, bf16[256,1280]{1,0:T(8,128)(2,1)}, u32[]{:S(2)}) copy-start(bf16[256,1280]{1,0:T(8,128)(2,1)} %param.8) | copy-start | bytes 1966084
  26.7 6.3 %copy-start.1 = (bf16[8,256,128]{2,1,0:T(8,128)(2,1)}, bf16[8,256,128]{2,1,0:T(8,128)(2,1)S(1)}, u32[]{:S(2)}) copy-start(bf16[8,256,128]{2,1,0:T(8,128)(2,1)S(1)} %all_to_all.20) | copy-start | bytes 1572868
  26.8 18.0 %collective-permute-start = (bf16[2048,128]{1,0:T(8,128)(2,1)S(1)}, bf16[2048,128]{1,0:T(8,128)(2,1)S(1)}, u32[]{:S(2)}, u32[]{:S(2)}) collective-permute-start(bf16[2048,128]{1,0:T(8,128)(2,1)S(1)} %bitcast.12), channel_id=1, source_target_pairs={{0,1},{1,0},{2,3},{3,2},{4,5},{5,4},{6,7},{7,6},{8,9},{9,8},{10,11... | collective-permute-start | bytes 1572872 | tf_op jit(solution)/shard_map/ppermute | solution.py:169
  44.8 39.1 %copy-start.4 = (bf16[128,1280]{1,0:T(8,128)(2,1)S(1)}, bf16[128,1280]{1,0:T(8,128)(2,1)}, u32[]{:S(2)}) copy-start(bf16[128,1280]{1,0:T(8,128)(2,1)} %param.7) | copy-start | bytes 983044
  44.8 0.8 copy-start.3
  81.1 15.7 %copy-start.2 = (f32[16,8,4,128]{3,2,1,0:T(4,128)}, f32[16,8,4,128]{3,2,1,0:T(4,128)S(1)}, u32[]{:S(2)}) copy-start(f32[16,8,4,128]{3,2,1,0:T(4,128)S(1)} %all_to_all.22) | copy-start | bytes 786436
  81.1 15.7 %collective-permute-start.1 = (f32[128,4,128]{2,1,0:T(4,128)S(1)}, f32[128,4,128]{2,1,0:T(4,128)S(1)}, u32[]{:S(2)}, u32[]{:S(2)}) collective-permute-start(f32[128,4,128]{2,1,0:T(4,128)S(1)} %bitcast.14), channel_id=1, source_target_pairs={{0,1},{1,0},{2,3},{3,2},{4,5},{5,4},{6,7},{7,6},{8,9},{9,8},{10,11... | collective-permute-start | bytes 786440 | tf_op jit(solution)/shard_map/ppermute | solution.py:214
  96.8 0.7 copy-start.5

commit v3 on v2

v3 whole, which is shorter than its diff:
```python
import jax
import jax.numpy as jnp
from jax import lax
from jax.experimental import pallas as pl
from jax.experimental.pallas import tpu as pltpu
from jax.sharding import PartitionSpec as P


f32, bf16, i32 = jnp.float32, jnp.bfloat16, jnp.int32
NT = (((1,), (1,)), ((), ()))
TN = (((0,), (0,)), ((), ()))
VM = pl.BlockSpec(memory_space=pltpu.VMEM)
SM = pl.BlockSpec(memory_space=pltpu.SMEM)
CH = 64
GRP = 16
COLS = 256


def iota(shape, dim):
    return lax.broadcasted_iota(i32, shape, dim)


def split2(x):
    hi = x.astype(bf16)
    return hi, (x - hi.astype(f32)).astype(bf16)


def prep_kernel(len_ref, p_ref, o_ref, sched_ref):
    count, pt, dim = p_ref.shape
    per = pt // CH

    def clean(p, _):
        rows = p_ref[p].astype(f32)
        keep = iota((pt, dim), 0) < len_ref[p]
        o_ref[p] = jnp.where(keep, rows, rows[0:1, :]).astype(bf16)
        return 0

    lax.fori_loop(0, count, clean, 0, unroll=4)

    def listed(p, at):
        live = (len_ref[p] + (CH - 1)) // CH
        sched_ref[160 + p] = at
        sched_ref[192 + p] = live
        for k in range(per):
            sched_ref[at + k] = p * pt + k * CH
        return at + live

    total = lax.fori_loop(0, count, listed, 0)
    for k in range(GRP):
        sched_ref[total + k] = 0
    rest = total % GRP
    sched_ref[224] = total // GRP + jnp.where(rest > GRP // 2, 1, 0)
    sched_ref[225] = jnp.where((rest > 0) & (rest <= GRP // 2), 1, 0)


def best_matches(sched_ref, p_ref, q_ref, starts, part_ref, best_ref):
    count = best_ref.shape[0]

    def run(at, n):
        rows = jnp.concatenate(
            [p_ref[pl.ds(pl.multiple_of(sched_ref[at + k], CH), CH), :] for k in range(n)], axis=0
        )
        for c, start in enumerate(starts):
            sim = lax.dot_general(
                rows, q_ref[pl.ds(start, COLS), :], NT, preferred_element_type=f32
            )
            m = jnp.max(sim.reshape(n, CH // 8, 8, COLS), axis=1)
            part_ref[pl.ds(pl.multiple_of(at * 8, 64), n * 8), c * COLS : (c + 1) * COLS] = m.reshape(
                n * 8, COLS
            )

    def step(g, _):
        run(g * GRP, GRP)
        return 0

    full = sched_ref[224]
    lax.fori_loop(0, full, step, 0)

    @pl.when(sched_ref[225] == 1)
    def _():
        run(full * GRP, GRP // 2)

    def gather(p, _):
        at, live = sched_ref[160 + p], sched_ref[192 + p]
        m = None
        for k in range(256 // CH):
            c = at + jnp.minimum(k, live - 1)
            v = part_ref[pl.ds(pl.multiple_of(c * 8, 8), 8), :]
            m = v if m is None else jnp.maximum(m, v)
        best_ref[pl.ds(p, 1), :] = jnp.max(m, axis=0, keepdims=True)
        return 0

    lax.fori_loop(0, count, gather, 0, unroll=8)


def add_rows(member, best_ref):
    count = best_ref.shape[0]
    hi, lo = split2(best_ref[...])
    s = lax.dot_general(
        jnp.where(member, 1.0, 0.0).astype(bf16),
        jnp.concatenate([hi, lo], axis=0),
        NT,
        preferred_element_type=f32,
    )
    return s[:, :count] + s[:, count:]


def other_starts(pos_ref):
    return [pl.multiple_of(((pos_ref[0] + 1 + d) & 7) * COLS, COLS) for d in range(7)]


def query_sums(pos_ref, best_ref):
    shape = (64, best_ref.shape[1])
    r = iota(shape, 0)
    block = ((r & 7) - pos_ref[0] + 7) & 7
    s = add_rows(iota(shape, 1) // 32 == block * 8 + (r >> 3), best_ref)
    return jnp.concatenate([s[k * 8 : k * 8 + 8] for k in range(8)], axis=1)


def pack_kernel(pos_ref, count_ref, q_ref, all_ref, tiles_ref):
    nq, qt, dim = q_ref.shape

    def masked(q):
        keep = iota((qt, dim), 0) < count_ref[q]
        return jnp.where(keep, q_ref[q].astype(f32), 0.0).astype(bf16)

    for q in range(nq):
        all_ref[q * qt : (q + 1) * qt, :] = masked(q)
    for k in range(nq // 2):
        v = all_ref[pl.ds(pl.multiple_of((pos_ref[1] * (nq // 2) + k) * qt, qt), qt), :]
        for g in range(tiles_ref.shape[0]):
            tiles_ref[g, k * qt : (k + 1) * qt, :] = v


def own_kernel(sched_ref, pos_ref, p_ref, q_ref, t_ref, part_ref, best_ref):
    starts = range(0, q_ref.shape[0], COLS)
    best_matches(sched_ref, p_ref, q_ref, starts, part_ref, best_ref)
    shape = (q_ref.shape[0] // 32, q_ref.shape[0])
    s = add_rows(iota(shape, 1) // 32 == iota(shape, 0), best_ref)
    row = jnp.concatenate([s[q : q + 1] for q in range(shape[0])], axis=1)
    t_ref[...] = jnp.where(iota(t_ref.shape, 0) == pos_ref[0], row, 0.0)


def first_kernel(sched_ref, pos_ref, p_ref, q_ref, t_ref, part_ref, best_ref):
    best_matches(sched_ref, p_ref, q_ref, other_starts(pos_ref), part_ref, best_ref)
    t_ref[...] = query_sums(pos_ref, best_ref)


def second_kernel(sched_ref, pos_ref, p_ref, q_ref, own_ref, near_ref, o_ref, part_ref, best_ref):
    best_matches(sched_ref, p_ref, q_ref, other_starts(pos_ref), part_ref, best_ref)
    near, far = near_ref[...], query_sums(pos_ref, best_ref)
    low = pos_ref[1] == 0
    wide = jnp.concatenate([jnp.where(low, near, far), jnp.where(low, far, near)], axis=1)
    wide = wide + own_ref[...]
    for g in range(o_ref.shape[1]):
        o_ref[:, g, :] = wide[:, g * 128 : (g + 1) * 128]


def final_kernel(count_ref, pos_ref, cand_ref, near_ref, far_ref, o_ref):
    nq, nc = o_ref.shape
    rows, n = near_ref.shape[0], nq * nc
    ids = jnp.concatenate([cand_ref[q : q + 1, :] for q in range(nq)], axis=1)
    query = iota((1, n), 1) // nc
    want = (query & 3) * 32 + (ids & 31)
    key = (ids >> 5) * 4 + (query >> 2)
    r = iota((rows, 1), 0)
    at = ((r >> 2) & 7) * 128 + (r >> 5) * 8 + (r & 3)
    x = None
    for ref, c in ((near_ref, pos_ref[1]), (far_ref, 1 - pos_ref[1])):
        hot = jnp.where(at + c * 4 == key, 1.0, 0.0).astype(bf16)
        for part in split2(ref[...]):
            y = lax.dot_general(part, hot, TN, preferred_element_type=f32)
            x = y if x is None else x + y
    row = jnp.sum(jnp.where(iota(x.shape, 0) == want, x, 0.0), axis=0, keepdims=True)
    for q in range(nq):
        o_ref[q : q + 1, :] = row[:, q * nc : (q + 1) * nc] / count_ref[q].astype(f32)


def here(x):
    return pltpu.with_memory_space_constraint(x, pltpu.VMEM)


def call(kernel, outs, ins, out_specs=VM, in_specs=None, scratch=()):
    return pl.pallas_call(
        kernel,
        out_shape=outs,
        in_specs=[VM] * len(ins) if in_specs is None else in_specs,
        out_specs=out_specs,
        scratch_shapes=scratch,
        compiler_params=pltpu.CompilerParams(vmem_limit_bytes=20 << 20),
    )(*ins)


def body(
    query_fixed_encoding,
    passage_fde,
    query_tokens,
    query_token_totals,
    passage_tokens,
    passage_lengths,
    candidates,
):
    groups, shards = lax.axis_size("fde"), lax.axis_size("pas")
    nq, qt, dim = query_tokens.shape
    count, pt, _ = passage_tokens.shape
    core = lax.axis_index("pas") % 2
    swap = [(k, k ^ 1) for k in range(shards)]
    S = jax.ShapeDtypeStruct

    pos = jnp.stack([lax.axis_index("fde"), core])
    rows, tiles = call(
        pack_kernel,
        (pltpu.VMEM((nq * qt, dim), bf16), pltpu.VMEM((groups, nq * qt // 2, dim), bf16)),
        (pos, query_token_totals, query_tokens),
        (VM, VM),
        [SM, SM, VM],
    )
    near = lax.all_to_all(tiles, "fde", 0, 0, tiled=True)
    near = near.reshape(-1, dim)
    far = lax.ppermute(near, "pas", swap)

    clean, sched = call(
        prep_kernel,
        (pltpu.VMEM(passage_tokens.shape, bf16), S((256,), i32)),
        (passage_lengths, passage_tokens),
        (VM, SM),
        [SM, VM],
    )
    clean = clean.reshape(count * pt, dim)

    partial = lax.dot_general(
        query_fixed_encoding, passage_fde, NT, preferred_element_type=f32
    )
    tiles = lax.all_to_all(partial.reshape(groups, nq, -1), "fde", 0, 0, tiled=True)
    fde_scores = jnp.sum(tiles, axis=0)

    def scratch(width):
        return [pltpu.VMEM((count * pt // CH * 8, width), f32), pltpu.VMEM((count, width), f32)]

    own_sums = call(
        own_kernel,
        pltpu.VMEM((groups, nq * count), f32),
        (sched, pos, here(clean), here(rows)),
        VM,
        [SM, SM, VM, VM],
        scratch(nq * qt),
    )
    width = near.shape[0] - COLS
    near_sums = call(
        first_kernel,
        pltpu.VMEM((groups, nq // 2 * count), f32),
        (sched, pos, here(clean), here(near)),
        VM,
        [SM, SM, VM, VM],
        scratch(width),
    )
    sums = call(
        second_kernel,
        pltpu.VMEM((groups, nq * count // 128, 128), f32),
        (sched, pos, here(clean), here(far), here(own_sums), here(near_sums)),
        VM,
        [SM, SM, VM, VM, VM, VM],
        scratch(width),
    )
    mine = lax.all_to_all(sums, "fde", 0, 0, tiled=True)
    half = shards // 2
    near = lax.all_to_all(
        jnp.broadcast_to(mine[None], (half,) + mine.shape),
        "pas",
        0,
        0,
        axis_index_groups=[[2 * k + c for k in range(half)] for c in range(2)],
        tiled=True,
    ).reshape(-1, 128)
    far = lax.ppermute(near, "pas", swap)
    rerank = call(
        final_kernel,
        S(candidates.shape, f32),
        (query_token_totals, pos, candidates, here(near), here(far)),
        VM,
        [SM, SM, VM, VM, VM],
    )
    return fde_scores, rerank


def solution(mesh):
    return jax.shard_map(
        body,
        mesh=mesh,
        in_specs=(
            P(None, "fde"),
            P("pas", "fde"),
            P("fde", None, None),
            P("fde"),
            P(("fde", "pas"), None, None),
            P(("fde", "pas")),
            P("fde", "pas"),
        ),
        out_specs=(P("fde", "pas"), P("fde", "pas")),
        check_vma=False,
    )
```

time: 101 us -> 94.7 us (0.938)
  Pallas kernels: 30.9 us -> 24.2 us
  local copies, waits for them, and re-layouts: 1.65 us -> 3.92 us
    pallas_call x4 -> x6, Pallas kernels: 30.9 us -> 24.2 us  [call(): pl.pallas_call(kernel, out_shape=outs, in_specs=[VM] * len(ins) if in_spe...]
    unnamed x12 -> x16, local copies, waits for them, and re-layouts: 1.52 us -> 3.88 us
    select_n x1 -> x0, other arithmetic: 1.07 us -> none  [body(): jnp.where(live, query_tokens, jnp.zeros((), bf16))]
  transfers between devices with their start and end apart: 2 -> 2, of which waited for: 0 -> 0; matrix products, arithmetic and copies ran while one was open for 1% -> 1% of each run, Pallas kernels for 16% -> 15%
where the time goes in v3:
time: 94.7 us; the launch traced here: 94.4 us
  blocking collectives  59.7 us (63%)
  Pallas kernels  24.2 us (26%)
  starting transfers between devices  4.86 us (5%)
  local copies, waits for them, and re-layouts  3.92 us (4%)
    all_to_all x1, blocking collectives, body(): near = lax.all_to_all(tiles, 'fde', 0, 0, tiled=True)  24.9 us
    pallas_call x6, Pallas kernels, call(): pl.pallas_call(kernel, out_shape=outs, in_specs=[VM] * len(ins) if in_spe...  24.2 us
    all_to_all x1, blocking collectives, body(): lax.all_to_all(jnp.broadcast_to(mine[None], (half,) + mine.shape), 'pas',...  13.8 us
    all_to_all x1, blocking collectives, body(): lax.all_to_all(partial.reshape(groups, nq, -1), 'fde', 0, 0, tiled=True)  11.9 us
    all_to_all x1, blocking collectives, body(): mine = lax.all_to_all(sums, 'fde', 0, 0, tiled=True)  9.09 us
    ppermute x2, starting transfers between devices, body(): far = lax.ppermute(near, 'pas', swap)  4.86 us
    unnamed x16, local copies, waits for them, and re-layouts  3.88 us
  transfers between devices with their start and end apart: 2, of which 0 were waited for; matrix products, arithmetic and copies ran while one was open for 1% of the time, Pallas kernels for 15%

profile of v3, /device:TPU:1, one launch (start us, length us, event | category | flops | bytes accessed | tf_op | source)
XLA Modules:
  0.0 94.4 jit_solution(6223132023591220854)
XLA Ops:
  0.6 0.0 copy-start
  0.7 0.1 pad_add_fusion.pos_ref
  0.7 0.0 copy-start.2
  0.7 1.0 %copy-done.2 = bf16[16,32,128]{2,1,0:T(8,128)(2,1)S(1)} copy-done((bf16[16,32,128]{2,1,0:T(8,128)(2,1)S(1)}, bf16[16,32,128]{2,1,0:T(8,128)(2,1)}, u32[]{:S(2)}) %copy-start.2) | copy-done | bytes 131096
  1.7 0.0 copy-start.4
  1.7 0.7 copy-done.4
  2.3 0.6 shard_map.87
  3.0 24.9 %all_to_all.20 = bf16[8,256,128]{2,1,0:T(8,128)(2,1)S(1)} all-to-all(bf16[8,256,128]{2,1,0:T(8,128)(2,1)S(1)} %get-tuple-element.8), channel_id=1, replica_groups=mesh['fde'=8,'pas'=32] {'fde'}, dimensions={0} | all-to-all | bytes 1048576 | tf_op jit(solution)/shard_map/all_to_all | solution.py:218
  27.9 2.3 %collective-permute-start = (bf16[2048,128]{1,0:T(8,128)(2,1)S(1)}, bf16[2048,128]{1,0:T(8,128)(2,1)S(1)}, u32[]{:S(2)}, u32[]{:S(2)}) collective-permute-start(bf16[2048,128]{1,0:T(8,128)(2,1)S(1)} %bitcast.11), channel_id=1, source_target_pairs={{0,1},{1,0},{2,3},{3,2},{4,5},{5,4},{6,7},{7,6},{8,9},{9,8},{10,11... | collective-permute-start | bytes 1572872 | tf_op jit(solution)/shard_map/ppermute | solution.py:220
  30.2 0.0 copy-start.1
  30.2 1.6 %copy-done.1 = bf16[32,256,128]{2,1,0:T(8,128)(2,1)S(1)} copy-done((bf16[32,256,128]{2,1,0:T(8,128)(2,1)S(1)}, bf16[32,256,128]{2,1,0:T(8,128)(2,1)}, u32[]{:S(2)}) %copy-start.1) | copy-done | bytes 2097176
  31.8 0.0 copy-start.6
  31.8 0.7 copy-done.6
  32.5 2.1 %shard_map.86 = (bf16[32,256,128]{2,1,0:T(8,128)(2,1)S(1)}, s32[256]{0:T(256)S(1)}) custom-call(s32[32]{0:T(128)S(1)} %copy-done.6, bf16[32,256,128]{2,1,0:T(8,128)(2,1)S(1)} %copy-done.1), custom_call_target="tpu_custom_call" | custom-call | tf_op jit(solution)/shard_map/pallas_call | solution.py:184
  34.6 3.8 %shard_map.88.own_ref = f32[8,512]{1,0:T(8,128)S(1)} custom-call(s32[256]{0:T(256)S(1)} %get-tuple-element.6.sched_ref, s32[2]{0:T(128)S(1)} %pad_add_fusion.pos_ref, bf16[8192,128]{1,0:T(8,128)(2,1)S(1)} %bitcast.8, bf16[512,128]{1,0:T(8,128)(2,1)S(1)} %get-tuple-element.9.q_ref), custom_call_target="tpu_custom_call" | custom-call | tf_op jit(solution)/shard_map/pallas_call | solution.py:184
  38.4 7.9 %shard_map.89.near_ref = f32[8,256]{1,0:T(8,128)S(1)} custom-call(s32[256]{0:T(256)S(1)} %get-tuple-element.6.sched_ref, s32[2]{0:T(128)S(1)} %pad_add_fusion.pos_ref, bf16[8192,128]{1,0:T(8,128)(2,1)S(1)} %bitcast.9, bf16[2048,128]{1,0:T(8,128)(2,1)S(1)} %bitcast.12), custom_call_target="tpu_custom_call" | custom-call | tf_op jit(solution)/shard_map/pallas_call | solution.py:184
  46.3 0.0 copy-start.7
  46.3 0.0 copy-start.3
  46.3 0.0 copy-start.5
  46.3 0.0 collective-permute-done.q_ref
  46.3 7.9 %shard_map.90 = f32[8,4,128]{2,1,0:T(4,128)S(1)} custom-call(s32[256]{0:T(256)S(1)} %get-tuple-element.6.sched_ref, s32[2]{0:T(128)S(1)} %pad_add_fusion.pos_ref, bf16[8192,128]{1,0:T(8,128)(2,1)S(1)} %bitcast.10, bf16[2048,128]{1,0:T(8,128)(2,1)S(1)} %collective-permute-done.q_ref, f32[8,512]{1,0:T(8,128)S(1)} %shard_map.88.own_ref, ...), custom_call_target="tpu_custom_call" | custom-call | tf_op jit(solution)/shard_map/pallas_call | solution.py:184
  54.3 9.1 %all_to_all.21 = f32[8,4,128]{2,1,0:T(4,128)S(1)} all-to-all(f32[8,4,128]{2,1,0:T(4,128)S(1)} %shard_map.90), channel_id=1, replica_groups=mesh['fde'=8,'pas'=32] {'fde'}, dimensions={0} | all-to-all | bytes 32768 | tf_op jit(solution)/shard_map/all_to_all | solution.py:265
  63.4 13.8 %all_to_all.22 = f32[16,8,4,128]{3,2,1,0:T(4,128)S(1)} all-to-all(f32[16,8,4,128]{3,2,1,0:T(4,128)S(1)} %broadcast_in_dim.2), channel_id=1, replica_groups={{0,2,4,6,8,10,12,14,16,18,20,22,24,26,28,30},{1,3,5,7,9,11,13,15,17,19,..., dimensions={0} | all-to-all | bytes 524288 | tf_op jit(solution)/shard_map/all_to_all | solution.py:267
  77.2 2.5 %collective-permute-start.1 = (f32[512,128]{1,0:T(8,128)S(1)}, f32[512,128]{1,0:T(8,128)S(1)}, u32[]{:S(2)}, u32[]{:S(2)}) collective-permute-start(f32[512,128]{1,0:T(8,128)S(1)} %bitcast.13), channel_id=1, source_target_pairs={{0,1},{1,0},{2,3},{3,2},{4,5},{5,4},{6,7},{7,6},{8,9},{9,8},{10,11... | collective-permute-start | bytes 786440 | tf_op jit(solution)/shard_map/ppermute | solution.py:275
  79.7 0.0 copy-done
  79.7 0.0 copy-done.7
  79.7 0.4 fusion
  80.1 11.9 %all_to_all.23 = f32[8,16,256]{2,1,0:T(8,128)S(1)} all-to-all(f32[8,16,256]{2,1,0:T(8,128)S(1)} %bitcast.15), channel_id=1, replica_groups=mesh['fde'=8,'pas'=32] {'fde'}, dimensions={0} | all-to-all | bytes 262144 | tf_op jit(solution)/shard_map/all_to_all | solution.py:234
  92.0 0.6 reduce_sum.9
  92.6 0.0 collective-permute-done.1.far_ref
  92.6 0.0 copy-done.3
  92.6 0.0 copy-done.5
  92.6 1.8 %shard_map.91 = f32[16,32]{1,0:T(8,128)} custom-call(s32[16]{0:T(128)S(1)} %copy-done.5, s32[2]{0:T(128)S(1)} %pad_add_fusion.pos_ref, s32[16,32]{1,0:T(8,128)S(1)} %copy-done.3, f32[512,128]{1,0:T(8,128)S(1)} %bitcast.14, f32[512,128]{1,0:T(8,128)S(1)} %collective-permute-done.1.far_ref), custom_call_target="tpu_custom_call" | custom-call | tf_op jit(solution)/shard_map/pallas_call | solution.py:184
  (1 shorter events, 0.0 us)
Async XLA Ops:
  0.6 79.1 %copy-start = (bf16[256,1280]{1,0:T(8,128)(2,1)S(1)}, bf16[256,1280]{1,0:T(8,128)(2,1)}, u32[]{:S(2)}) copy-start(bf16[256,1280]{1,0:T(8,128)(2,1)} %param.8) | copy-start | bytes 1966084
  0.7 1.0 %copy-start.2 = (bf16[16,32,128]{2,1,0:T(8,128)(2,1)S(1)}, bf16[16,32,128]{2,1,0:T(8,128)(2,1)}, u32[]{:S(2)}) copy-start(bf16[16,32,128]{2,1,0:T(8,128)(2,1)} %q_ref.1) | copy-start | bytes 393220
  1.7 0.7 copy-start.4
  27.9 18.4 %collective-permute-start = (bf16[2048,128]{1,0:T(8,128)(2,1)S(1)}, bf16[2048,128]{1,0:T(8,128)(2,1)S(1)}, u32[]{:S(2)}, u32[]{:S(2)}) collective-permute-start(bf16[2048,128]{1,0:T(8,128)(2,1)S(1)} %bitcast.11), channel_id=1, source_target_pairs={{0,1},{1,0},{2,3},{3,2},{4,5},{5,4},{6,7},{7,6},{8,9},{9,8},{10,11... | collective-permute-start | bytes 1572872 | tf_op jit(solution)/shard_map/ppermute | solution.py:220
  30.2 1.6 %copy-start.1 = (bf16[32,256,128]{2,1,0:T(8,128)(2,1)S(1)}, bf16[32,256,128]{2,1,0:T(8,128)(2,1)}, u32[]{:S(2)}) copy-start(bf16[32,256,128]{2,1,0:T(8,128)(2,1)} %p_ref.1) | copy-start | bytes 6291460
  31.8 0.7 copy-start.6
  46.3 33.4 %copy-start.7 = (bf16[128,1280]{1,0:T(8,128)(2,1)S(1)}, bf16[128,1280]{1,0:T(8,128)(2,1)}, u32[]{:S(2)}) copy-start(bf16[128,1280]{1,0:T(8,128)(2,1)} %param.7) | copy-start | bytes 983044
  46.3 46.3 %copy-start.3 = (s32[16,32]{1,0:T(8,128)S(1)}, s32[16,32]{1,0:T(8,128)}, u32[]{:S(2)}) copy-start(s32[16,32]{1,0:T(8,128)} %cand_ref.1) | copy-start | bytes 6148
  46.3 46.3 %copy-start.5 = (s32[16]{0:T(128)S(1)}, s32[16]{0:T(128)}, u32[]{:S(2)}) copy-start(s32[16]{0:T(128)} %count_ref.3) | copy-start | bytes 196
  77.2 15.4 %collective-permute-start.1 = (f32[512,128]{1,0:T(8,128)S(1)}, f32[512,128]{1,0:T(8,128)S(1)}, u32[]{:S(2)}, u32[]{:S(2)}) collective-permute-start(f32[512,128]{1,0:T(8,128)S(1)} %bitcast.13), channel_id=1, source_target_pairs={{0,1},{1,0},{2,3},{3,2},{4,5},{5,4},{6,7},{7,6},{8,9},{9,8},{10,11... | collective-permute-start | bytes 786440 | tf_op jit(solution)/shard_map/ppermute | solution.py:275

commit v4 on v3

--- a/solution.py
+++ b/solution.py
@@ -146,14 +146,32 @@
     t_ref[...] = query_sums(pos_ref, best_ref)
 
 
-def second_kernel(sched_ref, pos_ref, p_ref, q_ref, own_ref, near_ref, o_ref, part_ref, best_ref):
+def second_kernel(
+    sched_ref, pos_ref, p_ref, q_ref, own_ref, near_ref, fde_ref, o_ref, part_ref, best_ref
+):
+    nq = fde_ref.shape[0] // o_ref.shape[0]
+    for i in range(o_ref.shape[0]):
+        for h in range(fde_ref.shape[1] // 128):
+            o_ref[i, h * nq : (h + 1) * nq, :] = fde_ref[
+                i * nq : (i + 1) * nq, h * 128 : (h + 1) * 128
+            ]
+        o_ref[i, 32:40, :] = jnp.zeros((8, 128), f32)
     best_matches(sched_ref, p_ref, q_ref, other_starts(pos_ref), part_ref, best_ref)
     near, far = near_ref[...], query_sums(pos_ref, best_ref)
     low = pos_ref[1] == 0
     wide = jnp.concatenate([jnp.where(low, near, far), jnp.where(low, far, near)], axis=1)
     wide = wide + own_ref[...]
-    for g in range(o_ref.shape[1]):
-        o_ref[:, g, :] = wide[:, g * 128 : (g + 1) * 128]
+    for g in range(wide.shape[1] // 128):
+        o_ref[:, 32 + g, :] = wide[:, g * 128 : (g + 1) * 128]
+
+
+def fold_kernel(x_ref, o_ref):
+    nq, width = o_ref.shape
+    for h in range(width // 128):
+        x = x_ref[0, h * nq : (h + 1) * nq, :]
+        for i in range(1, x_ref.shape[0]):
+            x = x + x_ref[i, h * nq : (h + 1) * nq, :]
+        o_ref[:, h * 128 : (h + 1) * 128] = x
 
 
 def final_kernel(count_ref, pos_ref, cand_ref, near_ref, far_ref, o_ref):
@@ -176,8 +194,12 @@
         o_ref[q : q + 1, :] = row[:, q * nc : (q + 1) * nc] / count_ref[q].astype(f32)
 
 
-def here(x):
+def in_vmem(x):
     return pltpu.with_memory_space_constraint(x, pltpu.VMEM)
+
+
+def in_hbm(x):
+    return pltpu.with_memory_space_constraint(x, pltpu.HBM)
 
 
 def call(kernel, outs, ins, out_specs=VM, in_specs=None, scratch=()):
@@ -207,11 +229,11 @@
     swap = [(k, k ^ 1) for k in range(shards)]
     S = jax.ShapeDtypeStruct
 
-    pos = jnp.stack([lax.axis_index("fde"), core])
+    pos = in_hbm(jnp.stack([lax.axis_index("fde"), core]))
     rows, tiles = call(
         pack_kernel,
         (pltpu.VMEM((nq * qt, dim), bf16), pltpu.VMEM((groups, nq * qt // 2, dim), bf16)),
-        (pos, query_token_totals, query_tokens),
+        (pos, in_hbm(query_token_totals), in_hbm(query_tokens)),
         (VM, VM),
         [SM, SM, VM],
     )
@@ -222,17 +244,15 @@
     clean, sched = call(
         prep_kernel,
         (pltpu.VMEM(passage_tokens.shape, bf16), S((256,), i32)),
-        (passage_lengths, passage_tokens),
+        (in_hbm(passage_lengths), in_hbm(passage_tokens)),
         (VM, SM),
         [SM, VM],
     )
-    clean = clean.reshape(count * pt, dim)
+    clean, sched = clean.reshape(count * pt, dim), in_hbm(sched)
 
     partial = lax.dot_general(
         query_fixed_encoding, passage_fde, NT, preferred_element_type=f32
     )
-    tiles = lax.all_to_all(partial.reshape(groups, nq, -1), "fde", 0, 0, tiled=True)
-    fde_scores = jnp.sum(tiles, axis=0)
 
     def scratch(width):
         return [pltpu.VMEM((count * pt // CH * 8, width), f32), pltpu.VMEM((count, width), f32)]
@@ -240,7 +260,7 @@
     own_sums = call(
         own_kernel,
         pltpu.VMEM((groups, nq * count), f32),
-        (sched, pos, here(clean), here(rows)),
+        (sched, pos, in_vmem(clean), in_vmem(rows)),
         VM,
         [SM, SM, VM, VM],
         scratch(nq * qt),
@@ -249,20 +269,22 @@
     near_sums = call(
         first_kernel,
         pltpu.VMEM((groups, nq // 2 * count), f32),
-        (sched, pos, here(clean), here(near)),
+        (sched, pos, in_vmem(clean), in_vmem(near)),
         VM,
         [SM, SM, VM, VM],
         scratch(width),
     )
     sums = call(
         second_kernel,
-        pltpu.VMEM((groups, nq * count // 128, 128), f32),
-        (sched, pos, here(clean), here(far), here(own_sums), here(near_sums)),
+        pltpu.VMEM((groups, 40, 128), f32),
+        (sched, pos, in_vmem(clean), in_vmem(far), in_vmem(own_sums), in_vmem(near_sums), in_vmem(partial)),
         VM,
-        [SM, SM, VM, VM, VM, VM],
+        [SM, SM, VM, VM, VM, VM, VM],
         scratch(width),
     )
-    mine = lax.all_to_all(sums, "fde", 0, 0, tiled=True)
+    back = lax.all_to_all(sums, "fde", 0, 0, tiled=True)
+    mine = back[:, 32 : 32 + nq * count // 128]
+    fde_scores = call(fold_kernel, S((nq, passage_fde.shape[0]), f32), (in_vmem(back),))
     half = shards // 2
     near = lax.all_to_all(
         jnp.broadcast_to(mine[None], (half,) + mine.shape),
@@ -276,7 +298,7 @@
     rerank = call(
         final_kernel,
         S(candidates.shape, f32),
-        (query_token_totals, pos, candidates, here(near), here(far)),
+        (in_hbm(query_token_totals), pos, in_hbm(candidates), in_vmem(near), in_vmem(far)),
         VM,
         [SM, SM, VM, VM, VM],
     )

time: 94.7 us -> 86 us (0.908)
  blocking collectives: 59.7 us -> 51.6 us
  local copies, waits for them, and re-layouts: 3.92 us -> 0.62 us
  Pallas kernels: 24.2 us -> 26.8 us
    all_to_all x2 -> x1, blocking collectives: 21 us -> 12.4 us  [body(): back = lax.all_to_all(sums, 'fde', 0, 0, tiled=True)]
    unnamed x16 -> x6, local copies, waits for them, and re-layouts: 3.88 us -> 0.57 us
    pallas_call x6 -> x7, Pallas kernels: 24.2 us -> 26.8 us  [call(): pl.pallas_call(kernel, out_shape=outs, in_specs=[VM] * len(ins) if in_spe...]
  transfers between devices with their start and end apart: 2 -> 2, of which waited for: 0 -> 1; matrix products, arithmetic and copies ran while one was open for 1% -> 0% of each run, Pallas kernels for 15% -> 18%
where the time goes in v4:
time: 86 us; the launch traced here: 85.6 us
  blocking collectives  51.6 us (60%)
  Pallas kernels  26.8 us (31%)
  starting transfers between devices  4.27 us (5%)
    pallas_call x7, Pallas kernels, call(): pl.pallas_call(kernel, out_shape=outs, in_specs=[VM] * len(ins) if in_spe...  26.8 us
    all_to_all x1, blocking collectives, body(): near = lax.all_to_all(tiles, 'fde', 0, 0, tiled=True)  24.9 us
    all_to_all x1, blocking collectives, body(): lax.all_to_all(jnp.broadcast_to(mine[None], (half,) + mine.shape), 'pas',...  14.3 us
    all_to_all x1, blocking collectives, body(): back = lax.all_to_all(sums, 'fde', 0, 0, tiled=True)  12.4 us
    ppermute x2, starting transfers between devices, body(): far = lax.ppermute(near, 'pas', swap)  4.27 us
  transfers between devices with their start and end apart: 2, of which 1 were waited for; matrix products, arithmetic and copies ran while one was open for 0% of the time, Pallas kernels for 18%

profile of v4, /device:TPU:1, one launch (start us, length us, event | category | flops | bytes accessed | tf_op | source)
XLA Modules:
  0.0 85.6 jit_solution(4152927861057310289)
XLA Ops:
  0.6 0.0 copy-start
  0.7 0.7 pad_add_fusion.pos_ref
  1.3 1.0 %shard_map.87 = (bf16[512,128]{1,0:T(8,128)(2,1)S(1)}, bf16[8,256,128]{2,1,0:T(8,128)(2,1)S(1)}) custom-call(s32[2]{0:T(128)} %pad_add_fusion.pos_ref, s32[16]{0:T(128)} %count_ref.3, bf16[16,32,128]{2,1,0:T(8,128)(2,1)} %q_ref.1), custom_call_target="tpu_custom_call" | custom-call | tf_op jit(solution)/shard_map/pallas_call | solution.py:206
  2.3 24.9 %all_to_all.15 = bf16[8,256,128]{2,1,0:T(8,128)(2,1)S(1)} all-to-all(bf16[8,256,128]{2,1,0:T(8,128)(2,1)S(1)} %get-tuple-element.8), channel_id=1, replica_groups=mesh['fde'=8,'pas'=32] {'fde'}, dimensions={0} | all-to-all | bytes 1048576 | tf_op jit(solution)/shard_map/all_to_all | solution.py:240
  27.3 0.0 copy-start.2
  27.3 2.3 %collective-permute-start = (bf16[2048,128]{1,0:T(8,128)(2,1)S(1)}, bf16[2048,128]{1,0:T(8,128)(2,1)S(1)}, u32[]{:S(2)}, u32[]{:S(2)}) collective-permute-start(bf16[2048,128]{1,0:T(8,128)(2,1)S(1)} %bitcast.10), channel_id=1, source_target_pairs={{0,1},{1,0},{2,3},{3,2},{4,5},{5,4},{6,7},{7,6},{8,9},{9,8},{10,11... | collective-permute-start | bytes 1572872 | tf_op jit(solution)/shard_map/ppermute | solution.py:242
  29.6 3.2 %shard_map.86 = (bf16[32,256,128]{2,1,0:T(8,128)(2,1)S(1)}, s32[256]{0:T(256)S(1)}) custom-call(s32[32]{0:T(128)} %len_ref.1, bf16[32,256,128]{2,1,0:T(8,128)(2,1)} %p_ref.1), custom_call_target="tpu_custom_call" | custom-call | tf_op jit(solution)/shard_map/pallas_call | solution.py:206
  32.8 0.0 copy-start.1
  32.8 0.6 copy-done.1
  33.4 3.9 %shard_map.88.own_ref = f32[8,512]{1,0:T(8,128)S(1)} custom-call(s32[256]{0:T(256)} %copy-done.1, s32[2]{0:T(128)} %pad_add_fusion.pos_ref, bf16[8192,128]{1,0:T(8,128)(2,1)S(1)} %bitcast.7, bf16[512,128]{1,0:T(8,128)(2,1)S(1)} %get-tuple-element.9.q_ref), custom_call_target="tpu_custom_call" | custom-call | tf_op jit(solution)/shard_map/pallas_call | solution.py:206
  37.3 0.0 copy-done
  37.3 0.0 copy-done.2
  37.3 0.4 fusion.fde_ref
  37.6 8.0 %shard_map.89.near_ref = f32[8,256]{1,0:T(8,128)S(1)} custom-call(s32[256]{0:T(256)} %copy-done.1, s32[2]{0:T(128)} %pad_add_fusion.pos_ref, bf16[8192,128]{1,0:T(8,128)(2,1)S(1)} %bitcast.8, bf16[2048,128]{1,0:T(8,128)(2,1)S(1)} %bitcast.11), custom_call_target="tpu_custom_call" | custom-call | tf_op jit(solution)/shard_map/pallas_call | solution.py:206
  45.7 0.0 collective-permute-done.q_ref
  45.7 8.1 %shard_map.90 = f32[8,40,128]{2,1,0:T(8,128)S(1)} custom-call(s32[256]{0:T(256)} %copy-done.1, s32[2]{0:T(128)} %pad_add_fusion.pos_ref, bf16[8192,128]{1,0:T(8,128)(2,1)S(1)} %bitcast.9, bf16[2048,128]{1,0:T(8,128)(2,1)S(1)} %collective-permute-done.q_ref, f32[8,512]{1,0:T(8,128)S(1)} %shard_map.88.own_ref, f32[8,256]{1,0:T(8,128)S(1)} %shard_map.89.near_ref, ...), custom_call_target="tpu_custom_call" | custom-call | tf_op jit(solution)/shard_map/pallas_call | solution.py:206
  53.8 12.4 %all_to_all.16.x_ref = f32[8,40,128]{2,1,0:T(8,128)S(1)} all-to-all(f32[8,40,128]{2,1,0:T(8,128)S(1)} %shard_map.90), channel_id=1, replica_groups=mesh['fde'=8,'pas'=32] {'fde'}, dimensions={0} | all-to-all | bytes 327680 | tf_op jit(solution)/shard_map/all_to_all | solution.py:285
  66.2 14.3 %all_to_all.17 = f32[16,8,4,128]{3,2,1,0:T(4,128)S(1)} all-to-all(f32[16,8,4,128]{3,2,1,0:T(4,128)S(1)} %broadcast_in_dim.2), channel_id=1, replica_groups={{0,2,4,6,8,10,12,14,16,18,20,22,24,26,28,30},{1,3,5,7,9,11,13,15,17,19,..., dimensions={0} | all-to-all | bytes 524288 | tf_op jit(solution)/shard_map/all_to_all | solution.py:289
  80.5 1.9 %collective-permute-start.1 = (f32[512,128]{1,0:T(8,128)S(1)}, f32[512,128]{1,0:T(8,128)S(1)}, u32[]{:S(2)}, u32[]{:S(2)}) collective-permute-start(f32[512,128]{1,0:T(8,128)S(1)} %bitcast.12), channel_id=1, source_target_pairs={{0,1},{1,0},{2,3},{3,2},{4,5},{5,4},{6,7},{7,6},{8,9},{9,8},{10,11... | collective-permute-start | bytes 786440 | tf_op jit(solution)/shard_map/ppermute | solution.py:297
  82.5 0.6 shard_map.91
  83.1 0.5 collective-permute-done.1.far_ref
  83.6 2.0 %shard_map.92 = f32[16,32]{1,0:T(8,128)} custom-call(s32[16]{0:T(128)} %count_ref.3, s32[2]{0:T(128)} %pad_add_fusion.pos_ref, s32[16,32]{1,0:T(8,128)} %cand_ref.1, f32[512,128]{1,0:T(8,128)S(1)} %bitcast.13, f32[512,128]{1,0:T(8,128)S(1)} %collective-permute-done.1.far_ref), custom_call_target="tpu_custom_call" | custom-call | tf_op jit(solution)/shard_map/pallas_call | solution.py:206
  (2 shorter events, 0.0 us)
Async XLA Ops:
  0.6 36.6 %copy-start = (bf16[256,1280]{1,0:T(8,128)(2,1)S(1)}, bf16[256,1280]{1,0:T(8,128)(2,1)}, u32[]{:S(2)}) copy-start(bf16[256,1280]{1,0:T(8,128)(2,1)} %param.8) | copy-start | bytes 1966084
  27.3 10.0 %copy-start.2 = (bf16[128,1280]{1,0:T(8,128)(2,1)S(1)}, bf16[128,1280]{1,0:T(8,128)(2,1)}, u32[]{:S(2)}) copy-start(bf16[128,1280]{1,0:T(8,128)(2,1)} %param.7) | copy-start | bytes 983044
  27.3 18.4 %collective-permute-start = (bf16[2048,128]{1,0:T(8,128)(2,1)S(1)}, bf16[2048,128]{1,0:T(8,128)(2,1)S(1)}, u32[]{:S(2)}, u32[]{:S(2)}) collective-permute-start(bf16[2048,128]{1,0:T(8,128)(2,1)S(1)} %bitcast.10), channel_id=1, source_target_pairs={{0,1},{1,0},{2,3},{3,2},{4,5},{5,4},{6,7},{7,6},{8,9},{9,8},{10,11... | collective-permute-start | bytes 1572872 | tf_op jit(solution)/shard_map/ppermute | solution.py:242
  32.8 0.6 copy-start.1
  80.5 3.1 %collective-permute-start.1 = (f32[512,128]{1,0:T(8,128)S(1)}, f32[512,128]{1,0:T(8,128)S(1)}, u32[]{:S(2)}, u32[]{:S(2)}) collective-permute-start(f32[512,128]{1,0:T(8,128)S(1)} %bitcast.12), channel_id=1, source_target_pairs={{0,1},{1,0},{2,3},{3,2},{4,5},{5,4},{6,7},{7,6},{8,9},{9,8},{10,11... | collective-permute-start | bytes 786440 | tf_op jit(solution)/shard_map/ppermute | solution.py:297

commit v5 on v4

--- a/solution.py
+++ b/solution.py
@@ -11,8 +11,8 @@
 TN = (((0,), (0,)), ((), ()))
 VM = pl.BlockSpec(memory_space=pltpu.VMEM)
 SM = pl.BlockSpec(memory_space=pltpu.SMEM)
-CH = 64
-GRP = 16
+CH = 32
+GRP = 32
 COLS = 256
 
 
@@ -39,8 +39,8 @@
 
     def listed(p, at):
         live = (len_ref[p] + (CH - 1)) // CH
-        sched_ref[160 + p] = at
-        sched_ref[192 + p] = live
+        sched_ref[320 + p] = at
+        sched_ref[352 + p] = live
         for k in range(per):
             sched_ref[at + k] = p * pt + k * CH
         return at + live
@@ -49,8 +49,8 @@
     for k in range(GRP):
         sched_ref[total + k] = 0
     rest = total % GRP
-    sched_ref[224] = total // GRP + jnp.where(rest > GRP // 2, 1, 0)
-    sched_ref[225] = jnp.where((rest > 0) & (rest <= GRP // 2), 1, 0)
+    sched_ref[384] = total // GRP + jnp.where(rest > GRP // 2, 1, 0)
+    sched_ref[385] = jnp.where((rest > 0) & (rest <= GRP // 2), 1, 0)
 
 
 def best_matches(sched_ref, p_ref, q_ref, starts, part_ref, best_ref):
@@ -73,15 +73,15 @@
         run(g * GRP, GRP)
         return 0
 
-    full = sched_ref[224]
+    full = sched_ref[384]
     lax.fori_loop(0, full, step, 0)
 
-    @pl.when(sched_ref[225] == 1)
+    @pl.when(sched_ref[385] == 1)
     def _():
         run(full * GRP, GRP // 2)
 
     def gather(p, _):
-        at, live = sched_ref[160 + p], sched_ref[192 + p]
+        at, live = sched_ref[320 + p], sched_ref[352 + p]
         m = None
         for k in range(256 // CH):
             c = at + jnp.minimum(k, live - 1)
@@ -105,19 +105,19 @@
     return s[:, :count] + s[:, count:]
 
 
-def other_starts(pos_ref):
-    return [pl.multiple_of(((pos_ref[0] + 1 + d) & 7) * COLS, COLS) for d in range(7)]
-
-
-def query_sums(pos_ref, best_ref):
+def other_starts():
+    return [pl.multiple_of(((lax.axis_index("fde") + 1 + d) & 7) * COLS, COLS) for d in range(7)]
+
+
+def query_sums(best_ref):
     shape = (64, best_ref.shape[1])
     r = iota(shape, 0)
-    block = ((r & 7) - pos_ref[0] + 7) & 7
+    block = ((r & 7) - lax.axis_index("fde") + 7) & 7
     s = add_rows(iota(shape, 1) // 32 == block * 8 + (r >> 3), best_ref)
     return jnp.concatenate([s[k * 8 : k * 8 + 8] for k in range(8)], axis=1)
 
 
-def pack_kernel(pos_ref, count_ref, q_ref, all_ref, tiles_ref):
+def pack_kernel(count_ref, q_ref, all_ref, tiles_ref):
     nq, qt, dim = q_ref.shape
 
     def masked(q):
@@ -127,27 +127,27 @@
     for q in range(nq):
         all_ref[q * qt : (q + 1) * qt, :] = masked(q)
     for k in range(nq // 2):
-        v = all_ref[pl.ds(pl.multiple_of((pos_ref[1] * (nq // 2) + k) * qt, qt), qt), :]
+        v = all_ref[pl.ds(pl.multiple_of(((lax.axis_index("pas") & 1) * (nq // 2) + k) * qt, qt), qt), :]
         for g in range(tiles_ref.shape[0]):
             tiles_ref[g, k * qt : (k + 1) * qt, :] = v
 
 
-def own_kernel(sched_ref, pos_ref, p_ref, q_ref, t_ref, part_ref, best_ref):
+def own_kernel(sched_ref, p_ref, q_ref, t_ref, part_ref, best_ref):
     starts = range(0, q_ref.shape[0], COLS)
     best_matches(sched_ref, p_ref, q_ref, starts, part_ref, best_ref)
     shape = (q_ref.shape[0] // 32, q_ref.shape[0])
     s = add_rows(iota(shape, 1) // 32 == iota(shape, 0), best_ref)
     row = jnp.concatenate([s[q : q + 1] for q in range(shape[0])], axis=1)
-    t_ref[...] = jnp.where(iota(t_ref.shape, 0) == pos_ref[0], row, 0.0)
-
-
-def first_kernel(sched_ref, pos_ref, p_ref, q_ref, t_ref, part_ref, best_ref):
-    best_matches(sched_ref, p_ref, q_ref, other_starts(pos_ref), part_ref, best_ref)
-    t_ref[...] = query_sums(pos_ref, best_ref)
+    t_ref[...] = jnp.where(iota(t_ref.shape, 0) == lax.axis_index("fde"), row, 0.0)
+
+
+def first_kernel(sched_ref, p_ref, q_ref, t_ref, part_ref, best_ref):
+    best_matches(sched_ref, p_ref, q_ref, other_starts(), part_ref, best_ref)
+    t_ref[...] = query_sums(best_ref)
 
 
 def second_kernel(
-    sched_ref, pos_ref, p_ref, q_ref, own_ref, near_ref, fde_ref, o_ref, part_ref, best_ref
+    sched_ref, p_ref, q_ref, own_ref, near_ref, fde_ref, o_ref, part_ref, best_ref
 ):
     nq = fde_ref.shape[0] // o_ref.shape[0]
     for i in range(o_ref.shape[0]):
@@ -156,13 +156,19 @@
                 i * nq : (i + 1) * nq, h * 128 : (h + 1) * 128
             ]
         o_ref[i, 32:40, :] = jnp.zeros((8, 128), f32)
-    best_matches(sched_ref, p_ref, q_ref, other_starts(pos_ref), part_ref, best_ref)
-    near, far = near_ref[...], query_sums(pos_ref, best_ref)
-    low = pos_ref[1] == 0
+    best_matches(sched_ref, p_ref, q_ref, other_starts(), part_ref, best_ref)
+    near, far = near_ref[...], query_sums(best_ref)
+    low = (lax.axis_index("pas") & 1) == 0
     wide = jnp.concatenate([jnp.where(low, near, far), jnp.where(low, far, near)], axis=1)
     wide = wide + own_ref[...]
     for g in range(wide.shape[1] // 128):
         o_ref[:, 32 + g, :] = wide[:, g * 128 : (g + 1) * 128]
+
+
+def spread_kernel(x_ref, o_ref):
+    mine = x_ref[:, 32 : 32 + o_ref.shape[2], :]
+    for k in range(o_ref.shape[0]):
+        o_ref[k] = mine
 
 
 def fold_kernel(x_ref, o_ref):
@@ -174,21 +180,28 @@
         o_ref[:, h * 128 : (h + 1) * 128] = x
 
 
-def final_kernel(count_ref, pos_ref, cand_ref, near_ref, far_ref, o_ref):
-    nq, nc = o_ref.shape
-    rows, n = near_ref.shape[0], nq * nc
+def plan_kernel(cand_ref, near_ref, far_ref, want_ref):
+    nq, nc = cand_ref.shape
+    rows, n = near_ref.shape
     ids = jnp.concatenate([cand_ref[q : q + 1, :] for q in range(nq)], axis=1)
     query = iota((1, n), 1) // nc
-    want = (query & 3) * 32 + (ids & 31)
+    want_ref[...] = jnp.broadcast_to((query & 3) * 32 + (ids & 31), want_ref.shape)
     key = (ids >> 5) * 4 + (query >> 2)
     r = iota((rows, 1), 0)
     at = ((r >> 2) & 7) * 128 + (r >> 5) * 8 + (r & 3)
+    core = lax.axis_index("pas") & 1
+    for ref, c in ((near_ref, core), (far_ref, 1 - core)):
+        ref[...] = jnp.where(at + c * 4 == key, 1.0, 0.0).astype(bf16)
+
+
+def final_kernel(count_ref, want_ref, hot_near_ref, hot_far_ref, near_ref, far_ref, o_ref):
+    nq, nc = o_ref.shape
     x = None
-    for ref, c in ((near_ref, pos_ref[1]), (far_ref, 1 - pos_ref[1])):
-        hot = jnp.where(at + c * 4 == key, 1.0, 0.0).astype(bf16)
+    for ref, hot in ((near_ref, hot_near_ref), (far_ref, hot_far_ref)):
         for part in split2(ref[...]):
-            y = lax.dot_general(part, hot, TN, preferred_element_type=f32)
+            y = lax.dot_general(part, hot[...], TN, preferred_element_type=f32)
             x = y if x is None else x + y
+    want = want_ref[0:1, :]
     row = jnp.sum(jnp.where(iota(x.shape, 0) == want, x, 0.0), axis=0, keepdims=True)
     for q in range(nq):
         o_ref[q : q + 1, :] = row[:, q * nc : (q + 1) * nc] / count_ref[q].astype(f32)
@@ -225,17 +238,15 @@
     groups, shards = lax.axis_size("fde"), lax.axis_size("pas")
     nq, qt, dim = query_tokens.shape
     count, pt, _ = passage_tokens.shape
-    core = lax.axis_index("pas") % 2
     swap = [(k, k ^ 1) for k in range(shards)]
     S = jax.ShapeDtypeStruct
 
-    pos = in_hbm(jnp.stack([lax.axis_index("fde"), core]))
     rows, tiles = call(
         pack_kernel,
         (pltpu.VMEM((nq * qt, dim), bf16), pltpu.VMEM((groups, nq * qt // 2, dim), bf16)),
-        (pos, in_hbm(query_token_totals), in_hbm(query_tokens)),
+        (in_hbm(query_token_totals), in_hbm(query_tokens)),
         (VM, VM),
-        [SM, SM, VM],
+        [SM, VM],
     )
     near = lax.all_to_all(tiles, "fde", 0, 0, tiled=True)
     near = near.reshape(-1, dim)
@@ -243,7 +254,7 @@
 
     clean, sched = call(
         prep_kernel,
-        (pltpu.VMEM(passage_tokens.shape, bf16), S((256,), i32)),
+        (pltpu.VMEM(passage_tokens.shape, bf16), S((512,), i32)),
         (in_hbm(passage_lengths), in_hbm(passage_tokens)),
         (VM, SM),
         [SM, VM],
@@ -253,6 +264,11 @@
     partial = lax.dot_general(
         query_fixed_encoding, passage_fde, NT, preferred_element_type=f32
     )
+    pairs, flat = nq * candidates.shape[1], shards // 2 * groups * nq * count // 128
+    hot = pltpu.VMEM((flat, pairs), bf16)
+    hot_near, hot_far, want = call(
+        plan_kernel, (hot, hot, pltpu.VMEM((8, pairs), i32)), (candidates,), (VM, VM, VM)
+    )
 
     def scratch(width):
         return [pltpu.VMEM((count * pt // CH * 8, width), f32), pltpu.VMEM((count, width), f32)]
@@ -260,34 +276,37 @@
     own_sums = call(
         own_kernel,
         pltpu.VMEM((groups, nq * count), f32),
-        (sched, pos, in_vmem(clean), in_vmem(rows)),
+        (sched, in_vmem(clean), in_vmem(rows)),
         VM,
-        [SM, SM, VM, VM],
+        [SM, VM, VM],
         scratch(nq * qt),
     )
     width = near.shape[0] - COLS
     near_sums = call(
         first_kernel,
         pltpu.VMEM((groups, nq // 2 * count), f32),
-        (sched, pos, in_vmem(clean), in_vmem(near)),
+        (sched, in_vmem(clean), in_vmem(near)),
         VM,
-        [SM, SM, VM, VM],
+        [SM, VM, VM],
         scratch(width),
     )
     sums = call(
         second_kernel,
         pltpu.VMEM((groups, 40, 128), f32),
-        (sched, pos, in_vmem(clean), in_vmem(far), in_vmem(own_sums), in_vmem(near_sums), in_vmem(partial)),
+        (sched, in_vmem(clean), in_vmem(far), in_vmem(own_sums), in_vmem(near_sums), in_vmem(partial)),
         VM,
-        [SM, SM, VM, VM, VM, VM, VM],
+        [SM, VM, VM, VM, VM, VM],
         scratch(width),
     )
     back = lax.all_to_all(sums, "fde", 0, 0, tiled=True)
-    mine = back[:, 32 : 32 + nq * count // 128]
+    blocks = nq * count // 128
+    copies = call(
+        spread_kernel, pltpu.VMEM((shards // 2, groups, blocks, 128), f32), (in_vmem(back),)
+    )
     fde_scores = call(fold_kernel, S((nq, passage_fde.shape[0]), f32), (in_vmem(back),))
     half = shards // 2
     near = lax.all_to_all(
-        jnp.broadcast_to(mine[None], (half,) + mine.shape),
+        copies,
         "pas",
         0,
         0,
@@ -298,9 +317,16 @@
     rerank = call(
         final_kernel,
         S(candidates.shape, f32),
-        (in_hbm(query_token_totals), pos, in_hbm(candidates), in_vmem(near), in_vmem(far)),
+        (
+            in_hbm(query_token_totals),
+            in_vmem(want),
+            in_vmem(hot_near),
+            in_vmem(hot_far),
+            in_vmem(near),
+            in_vmem(far),
+        ),
         VM,
-        [SM, SM, VM, VM, VM],
+        [SM, VM, VM, VM, VM, VM],
     )
     return fde_scores, rerank
 

time: 86 us -> 85.4 us (level)
    all_to_all x1, blocking collectives: 14.3 us -> 15.6 us  [body(): lax.all_to_all(copies, 'pas', 0, 0, axis_index_groups=[[2 * k + c for k i...]
    pallas_call x7 -> x9, Pallas kernels: 26.8 us -> 26.9 us  [call(): pl.pallas_call(kernel, out_shape=outs, in_specs=[VM] * len(ins) if in_spe...]
  transfers between devices with their start and end apart: 2 -> 2, of which waited for: 1 -> 1; matrix products, arithmetic and copies ran while one was open for 0% -> 0% of each run, Pallas kernels for 18% -> 19%
where the time goes in v5:
time: 85.4 us; the launch traced here: 85.1 us
  blocking collectives  52.1 us (61%)
  Pallas kernels  26.9 us (31%)
  starting transfers between devices  4.25 us (5%)
    pallas_call x9, Pallas kernels, call(): pl.pallas_call(kernel, out_shape=outs, in_specs=[VM] * len(ins) if in_spe...  26.9 us
    all_to_all x1, blocking collectives, body(): near = lax.all_to_all(tiles, 'fde', 0, 0, tiled=True)  24.9 us
    all_to_all x1, blocking collectives, body(): lax.all_to_all(copies, 'pas', 0, 0, axis_index_groups=[[2 * k + c for k i...  15.6 us
    all_to_all x1, blocking collectives, body(): back = lax.all_to_all(sums, 'fde', 0, 0, tiled=True)  11.6 us
    ppermute x2, starting transfers between devices, body(): far = lax.ppermute(near, 'pas', swap)  4.25 us
  transfers between devices with their start and end apart: 2, of which 1 were waited for; matrix products, arithmetic and copies ran while one was open for 0% of the time, Pallas kernels for 19%

profile of v5, /device:TPU:1, one launch (start us, length us, event | category | flops | bytes accessed | tf_op | source)
XLA Modules:
  0.0 85.1 jit_solution(16853646989238477583)
XLA Ops:
  0.6 0.0 copy-start
  0.6 1.1 %shard_map.87 = (bf16[512,128]{1,0:T(8,128)(2,1)S(1)}, bf16[8,256,128]{2,1,0:T(8,128)(2,1)S(1)}) custom-call(s32[16]{0:T(128)} %count_ref.3, bf16[16,32,128]{2,1,0:T(8,128)(2,1)} %q_ref.1), custom_call_target="tpu_custom_call" | custom-call | tf_op jit(solution)/shard_map/pallas_call | solution.py:219
  1.7 24.9 %all_to_all.15 = bf16[8,256,128]{2,1,0:T(8,128)(2,1)S(1)} all-to-all(bf16[8,256,128]{2,1,0:T(8,128)(2,1)S(1)} %get-tuple-element.11), channel_id=1, replica_groups=mesh['fde'=8,'pas'=32] {'fde'}, dimensions={0} | all-to-all | bytes 1048576 | tf_op jit(solution)/shard_map/all_to_all | solution.py:251
  26.7 0.0 copy-start.3
  26.7 2.3 %collective-permute-start = (bf16[2048,128]{1,0:T(8,128)(2,1)S(1)}, bf16[2048,128]{1,0:T(8,128)(2,1)S(1)}, u32[]{:S(2)}, u32[]{:S(2)}) collective-permute-start(bf16[2048,128]{1,0:T(8,128)(2,1)S(1)} %bitcast.8), channel_id=1, source_target_pairs={{0,1},{1,0},{2,3},{3,2},{4,5},{5,4},{6,7},{7,6},{8,9},{9,8},{10,11... | collective-permute-start | bytes 1572872 | tf_op jit(solution)/shard_map/ppermute | solution.py:253
  29.0 3.3 %shard_map.86 = (bf16[32,256,128]{2,1,0:T(8,128)(2,1)S(1)}, s32[512]{0:T(512)S(1)}) custom-call(s32[32]{0:T(128)} %len_ref.1, bf16[32,256,128]{2,1,0:T(8,128)(2,1)} %p_ref.1), custom_call_target="tpu_custom_call" | custom-call | tf_op jit(solution)/shard_map/pallas_call | solution.py:219
  32.3 0.0 copy-start.1
  32.3 0.6 copy-done.1
  32.9 3.9 %shard_map.88.own_ref = f32[8,512]{1,0:T(8,128)S(1)} custom-call(s32[512]{0:T(512)} %copy-done.1, bf16[8192,128]{1,0:T(8,128)(2,1)S(1)} %bitcast.5, bf16[512,128]{1,0:T(8,128)(2,1)S(1)} %get-tuple-element.12.q_ref), custom_call_target="tpu_custom_call" | custom-call | tf_op jit(solution)/shard_map/pallas_call | solution.py:219
  36.8 0.0 copy-done
  36.8 0.0 copy-done.3
  36.8 0.4 fusion.fde_ref
  37.1 7.8 %shard_map.89.near_ref = f32[8,256]{1,0:T(8,128)S(1)} custom-call(s32[512]{0:T(512)} %copy-done.1, bf16[8192,128]{1,0:T(8,128)(2,1)S(1)} %bitcast.6, bf16[2048,128]{1,0:T(8,128)(2,1)S(1)} %bitcast.9), custom_call_target="tpu_custom_call" | custom-call | tf_op jit(solution)/shard_map/pallas_call | solution.py:219
  45.0 0.0 copy-start.2
  45.0 0.0 collective-permute-done.q_ref
  45.0 8.0 %shard_map.90 = f32[8,40,128]{2,1,0:T(8,128)S(1)} custom-call(s32[512]{0:T(512)} %copy-done.1, bf16[8192,128]{1,0:T(8,128)(2,1)S(1)} %bitcast.7, bf16[2048,128]{1,0:T(8,128)(2,1)S(1)} %collective-permute-done.q_ref, f32[8,512]{1,0:T(8,128)S(1)} %shard_map.88.own_ref, f32[8,256]{1,0:T(8,128)S(1)} %shard_map.89.near_ref, f32[128,256]{1,0:T(8,128)S(1)} %fusion.fde_ref), custom_call_target="tpu_custom_call" | custom-call | tf_op jit(solution)/shard_map/pallas_call | solution.py:219
  53.0 11.6 %all_to_all.16.x_ref = f32[8,40,128]{2,1,0:T(8,128)S(1)} all-to-all(f32[8,40,128]{2,1,0:T(8,128)S(1)} %shard_map.90), channel_id=1, replica_groups=mesh['fde'=8,'pas'=32] {'fde'}, dimensions={0} | all-to-all | bytes 327680 | tf_op jit(solution)/shard_map/all_to_all | solution.py:301
  64.6 15.6 %all_to_all.17 = f32[16,8,4,128]{3,2,1,0:T(4,128)S(1)} all-to-all(f32[16,8,4,128]{3,2,1,0:T(4,128)S(1)} %shard_map.93), channel_id=1, replica_groups={{0,2,4,6,8,10,12,14,16,18,20,22,24,26,28,30},{1,3,5,7,9,11,13,15,17,19,..., dimensions={0} | all-to-all | bytes 524288 | tf_op jit(solution)/shard_map/all_to_all | solution.py:308
  80.2 1.9 %collective-permute-start.1 = (f32[512,128]{1,0:T(8,128)S(1)}, f32[512,128]{1,0:T(8,128)S(1)}, u32[]{:S(2)}, u32[]{:S(2)}) collective-permute-start(f32[512,128]{1,0:T(8,128)S(1)} %bitcast.10), channel_id=1, source_target_pairs={{0,1},{1,0},{2,3},{3,2},{4,5},{5,4},{6,7},{7,6},{8,9},{9,8},{10,11... | collective-permute-start | bytes 786440 | tf_op jit(solution)/shard_map/ppermute | solution.py:316
  82.1 0.0 copy-done.2
  82.1 0.4 shard_map.92
  82.5 0.6 shard_map.91
  83.1 0.1 collective-permute-done.1.far_ref
  83.2 1.8 %shard_map.94 = f32[16,32]{1,0:T(8,128)} custom-call(s32[16]{0:T(128)} %count_ref.3, s32[8,512]{1,0:T(8,128)S(1)} %get-tuple-element.13.want_ref, bf16[512,512]{1,0:T(8,128)(2,1)S(1)} %get-tuple-element.14.hot_near_ref, bf16[512,512]{1,0:T(8,128)(2,1)S(1)} %get-tuple-element.15.hot_far_ref, f32[512,128]{1,0:T(8,128)S(1)} %bitcast.11, ...), custom_call_target="tpu_custom_call" | custom-call | tf_op jit(solution)/shard_map/pallas_call | solution.py:219
  (1 shorter events, 0.0 us)
Async XLA Ops:
  0.6 36.1 %copy-start = (bf16[256,1280]{1,0:T(8,128)(2,1)S(1)}, bf16[256,1280]{1,0:T(8,128)(2,1)}, u32[]{:S(2)}) copy-start(bf16[256,1280]{1,0:T(8,128)(2,1)} %param.8) | copy-start | bytes 1966084
  26.7 10.1 %copy-start.3 = (bf16[128,1280]{1,0:T(8,128)(2,1)S(1)}, bf16[128,1280]{1,0:T(8,128)(2,1)}, u32[]{:S(2)}) copy-start(bf16[128,1280]{1,0:T(8,128)(2,1)} %param.7) | copy-start | bytes 983044
  26.7 18.3 %collective-permute-start = (bf16[2048,128]{1,0:T(8,128)(2,1)S(1)}, bf16[2048,128]{1,0:T(8,128)(2,1)S(1)}, u32[]{:S(2)}, u32[]{:S(2)}) collective-permute-start(bf16[2048,128]{1,0:T(8,128)(2,1)S(1)} %bitcast.8), channel_id=1, source_target_pairs={{0,1},{1,0},{2,3},{3,2},{4,5},{5,4},{6,7},{7,6},{8,9},{9,8},{10,11... | collective-permute-start | bytes 1572872 | tf_op jit(solution)/shard_map/ppermute | solution.py:253
  32.3 0.6 copy-start.1
  45.0 37.1 %copy-start.2 = (s32[16,32]{1,0:T(8,128)S(1)}, s32[16,32]{1,0:T(8,128)}, u32[]{:S(2)}) copy-start(s32[16,32]{1,0:T(8,128)} %cand_ref.1) | copy-start | bytes 6148
  80.2 3.1 %collective-permute-start.1 = (f32[512,128]{1,0:T(8,128)S(1)}, f32[512,128]{1,0:T(8,128)S(1)}, u32[]{:S(2)}, u32[]{:S(2)}) collective-permute-start(f32[512,128]{1,0:T(8,128)S(1)} %bitcast.10), channel_id=1, source_target_pairs={{0,1},{1,0},{2,3},{3,2},{4,5},{5,4},{6,7},{7,6},{8,9},{9,8},{10,11... | collective-permute-start | bytes 786440 | tf_op jit(solution)/shard_map/ppermute | solution.py:316

commit v6 on v5

--- a/solution.py
+++ b/solution.py
@@ -53,17 +53,15 @@
     sched_ref[385] = jnp.where((rest > 0) & (rest <= GRP // 2), 1, 0)
 
 
-def best_matches(sched_ref, p_ref, q_ref, starts, part_ref, best_ref):
+def best_matches(sched_ref, p_ref, blocks, part_ref, best_ref):
     count = best_ref.shape[0]
 
     def run(at, n):
         rows = jnp.concatenate(
             [p_ref[pl.ds(pl.multiple_of(sched_ref[at + k], CH), CH), :] for k in range(n)], axis=0
         )
-        for c, start in enumerate(starts):
-            sim = lax.dot_general(
-                rows, q_ref[pl.ds(start, COLS), :], NT, preferred_element_type=f32
-            )
+        for c, block in enumerate(blocks):
+            sim = lax.dot_general(rows, block(), NT, preferred_element_type=f32)
             m = jnp.max(sim.reshape(n, CH // 8, 8, COLS), axis=1)
             part_ref[pl.ds(pl.multiple_of(at * 8, 64), n * 8), c * COLS : (c + 1) * COLS] = m.reshape(
                 n * 8, COLS
@@ -105,8 +103,19 @@
     return s[:, :count] + s[:, count:]
 
 
-def other_starts():
-    return [pl.multiple_of(((lax.axis_index("fde") + 1 + d) & 7) * COLS, COLS) for d in range(7)]
+def other_groups(a_ref, b_ref):
+    half = COLS // 2
+
+    def block(d):
+        at = pl.multiple_of(((lax.axis_index("fde") + 1 + d) & 7) * half, half)
+        return lambda: jnp.concatenate([r[pl.ds(at, half), :] for r in (a_ref, b_ref)], axis=0)
+
+    return [block(d) for d in range(7)]
+
+
+def place():
+    p = lax.axis_index("pas")
+    return ((p >> 3) + (p >> 1)) & 1, p & 1
 
 
 def query_sums(best_ref):
@@ -126,28 +135,29 @@
 
     for q in range(nq):
         all_ref[q * qt : (q + 1) * qt, :] = masked(q)
-    for k in range(nq // 2):
-        v = all_ref[pl.ds(pl.multiple_of(((lax.axis_index("pas") & 1) * (nq // 2) + k) * qt, qt), qt), :]
+    parity, core = place()
+    for k in range(nq // 4):
+        v = all_ref[pl.ds(pl.multiple_of(((parity * 2 + core) * (nq // 4) + k) * qt, qt), qt), :]
         for g in range(tiles_ref.shape[0]):
             tiles_ref[g, k * qt : (k + 1) * qt, :] = v
 
 
 def own_kernel(sched_ref, p_ref, q_ref, t_ref, part_ref, best_ref):
-    starts = range(0, q_ref.shape[0], COLS)
-    best_matches(sched_ref, p_ref, q_ref, starts, part_ref, best_ref)
+    blocks = [lambda at=at: q_ref[at : at + COLS, :] for at in range(0, q_ref.shape[0], COLS)]
+    best_matches(sched_ref, p_ref, blocks, part_ref, best_ref)
     shape = (q_ref.shape[0] // 32, q_ref.shape[0])
     s = add_rows(iota(shape, 1) // 32 == iota(shape, 0), best_ref)
     row = jnp.concatenate([s[q : q + 1] for q in range(shape[0])], axis=1)
     t_ref[...] = jnp.where(iota(t_ref.shape, 0) == lax.axis_index("fde"), row, 0.0)
 
 
-def first_kernel(sched_ref, p_ref, q_ref, t_ref, part_ref, best_ref):
-    best_matches(sched_ref, p_ref, q_ref, other_starts(), part_ref, best_ref)
+def first_kernel(sched_ref, p_ref, a_ref, b_ref, t_ref, part_ref, best_ref):
+    best_matches(sched_ref, p_ref, other_groups(a_ref, b_ref), part_ref, best_ref)
     t_ref[...] = query_sums(best_ref)
 
 
 def second_kernel(
-    sched_ref, p_ref, q_ref, own_ref, near_ref, fde_ref, o_ref, part_ref, best_ref
+    sched_ref, p_ref, a_ref, b_ref, own_ref, near_ref, fde_ref, o_ref, part_ref, best_ref
 ):
     nq = fde_ref.shape[0] // o_ref.shape[0]
     for i in range(o_ref.shape[0]):
@@ -156,19 +166,26 @@
                 i * nq : (i + 1) * nq, h * 128 : (h + 1) * 128
             ]
         o_ref[i, 32:40, :] = jnp.zeros((8, 128), f32)
-    best_matches(sched_ref, p_ref, q_ref, other_starts(), part_ref, best_ref)
-    near, far = near_ref[...], query_sums(best_ref)
-    low = (lax.axis_index("pas") & 1) == 0
-    wide = jnp.concatenate([jnp.where(low, near, far), jnp.where(low, far, near)], axis=1)
+    best_matches(sched_ref, p_ref, other_groups(a_ref, b_ref), part_ref, best_ref)
+    parity, core = place()
+
+    def ordered(swap, a, b):
+        return jnp.concatenate([jnp.where(swap, b, a), jnp.where(swap, a, b)], axis=1)
+
+    near, far = (
+        ordered(core == 1, t[:, :128], t[:, 128:]) for t in (near_ref[...], query_sums(best_ref))
+    )
+    wide = ordered(parity == 1, near, far)
     wide = wide + own_ref[...]
     for g in range(wide.shape[1] // 128):
         o_ref[:, 32 + g, :] = wide[:, g * 128 : (g + 1) * 128]
 
 
 def spread_kernel(x_ref, o_ref):
-    mine = x_ref[:, 32 : 32 + o_ref.shape[2], :]
-    for k in range(o_ref.shape[0]):
-        o_ref[k] = mine
+    for g in range(o_ref.shape[1]):
+        mine = x_ref[:, 32 + g, :]
+        for k in range(o_ref.shape[0]):
+            o_ref[k, g] = mine
 
 
 def fold_kernel(x_ref, o_ref):
@@ -186,25 +203,34 @@
     ids = jnp.concatenate([cand_ref[q : q + 1, :] for q in range(nq)], axis=1)
     query = iota((1, n), 1) // nc
     want_ref[...] = jnp.broadcast_to((query & 3) * 32 + (ids & 31), want_ref.shape)
-    key = (ids >> 5) * 4 + (query >> 2)
+    owner = ids >> 5
     r = iota((rows, 1), 0)
-    at = ((r >> 2) & 7) * 128 + (r >> 5) * 8 + (r & 3)
+    at = (r & 7) * 32 + (r >> 3) * 2
     core = lax.axis_index("pas") & 1
     for ref, c in ((near_ref, core), (far_ref, 1 - core)):
-        ref[...] = jnp.where(at + c * 4 == key, 1.0, 0.0).astype(bf16)
+        ref[...] = jnp.where(at + c == owner, 1.0, 0.0).astype(bf16)
 
 
 def final_kernel(count_ref, want_ref, hot_near_ref, hot_far_ref, near_ref, far_ref, o_ref):
     nq, nc = o_ref.shape
-    x = None
-    for ref, hot in ((near_ref, hot_near_ref), (far_ref, hot_far_ref)):
-        for part in split2(ref[...]):
-            y = lax.dot_general(part, hot[...], TN, preferred_element_type=f32)
+    blocks = nq * nc // 128
+    copies = near_ref.shape[0] // (blocks * 8)
+    for g in range(blocks):
+        lanes = slice(g * 128, (g + 1) * 128)
+        x = None
+        for ref, hot in ((near_ref, hot_near_ref), (far_ref, hot_far_ref)):
+            table = jnp.concatenate(
+                [ref[(k * blocks + g) * 8 : (k * blocks + g) * 8 + 8, :] for k in range(copies)], axis=0
+            )
+            both = jnp.concatenate(split2(table), axis=1)
+            y = lax.dot_general(both, hot[:, lanes], TN, preferred_element_type=f32)
             x = y if x is None else x + y
-    want = want_ref[0:1, :]
-    row = jnp.sum(jnp.where(iota(x.shape, 0) == want, x, 0.0), axis=0, keepdims=True)
-    for q in range(nq):
-        o_ref[q : q + 1, :] = row[:, q * nc : (q + 1) * nc] / count_ref[q].astype(f32)
+        x = x[:128] + x[128:]
+        want = want_ref[0:1, lanes]
+        row = jnp.sum(jnp.where(iota(x.shape, 0) == want, x, 0.0), axis=0, keepdims=True)
+        for j in range(128 // nc):
+            q = g * (128 // nc) + j
+            o_ref[q : q + 1, :] = row[:, j * nc : (j + 1) * nc] / count_ref[q].astype(f32)
 
 
 def in_vmem(x):
@@ -238,20 +264,23 @@
     groups, shards = lax.axis_size("fde"), lax.axis_size("pas")
     nq, qt, dim = query_tokens.shape
     count, pt, _ = passage_tokens.shape
-    swap = [(k, k ^ 1) for k in range(shards)]
     S = jax.ShapeDtypeStruct
 
     rows, tiles = call(
         pack_kernel,
-        (pltpu.VMEM((nq * qt, dim), bf16), pltpu.VMEM((groups, nq * qt // 2, dim), bf16)),
+        (pltpu.VMEM((nq * qt, dim), bf16), pltpu.VMEM((groups, nq * qt // 4, dim), bf16)),
         (in_hbm(query_token_totals), in_hbm(query_tokens)),
         (VM, VM),
         [SM, VM],
     )
     near = lax.all_to_all(tiles, "fde", 0, 0, tiled=True)
-    near = near.reshape(-1, dim)
-    far = lax.ppermute(near, "pas", swap)
-
+    quarter = near.reshape(-1, dim)
+
+    def moved(x, flip):
+        return lax.ppermute(x, "pas", [(k, k ^ flip) for k in range(shards)])
+
+    core_q = moved(quarter, 1)
+    x_q, y_q = moved(quarter, 8), moved(quarter, 3)
     clean, sched = call(
         prep_kernel,
         (pltpu.VMEM(passage_tokens.shape, bf16), S((512,), i32)),
@@ -264,8 +293,8 @@
     partial = lax.dot_general(
         query_fixed_encoding, passage_fde, NT, preferred_element_type=f32
     )
-    pairs, flat = nq * candidates.shape[1], shards // 2 * groups * nq * count // 128
-    hot = pltpu.VMEM((flat, pairs), bf16)
+    pairs = nq * candidates.shape[1]
+    hot = pltpu.VMEM((shards // 2 * groups, pairs), bf16)
     hot_near, hot_far, want = call(
         plan_kernel, (hot, hot, pltpu.VMEM((8, pairs), i32)), (candidates,), (VM, VM, VM)
     )
@@ -281,27 +310,35 @@
         [SM, VM, VM],
         scratch(nq * qt),
     )
-    width = near.shape[0] - COLS
+    width = (groups - 1) * COLS
     near_sums = call(
         first_kernel,
         pltpu.VMEM((groups, nq // 2 * count), f32),
-        (sched, in_vmem(clean), in_vmem(near)),
+        (sched, in_vmem(clean), in_vmem(quarter), in_vmem(core_q)),
         VM,
-        [SM, VM, VM],
+        [SM, VM, VM, VM],
         scratch(width),
     )
     sums = call(
         second_kernel,
         pltpu.VMEM((groups, 40, 128), f32),
-        (sched, in_vmem(clean), in_vmem(far), in_vmem(own_sums), in_vmem(near_sums), in_vmem(partial)),
+        (
+            sched,
+            in_vmem(clean),
+            in_vmem(x_q),
+            in_vmem(y_q),
+            in_vmem(own_sums),
+            in_vmem(near_sums),
+            in_vmem(partial),
+        ),
         VM,
-        [SM, VM, VM, VM, VM, VM],
+        [SM, VM, VM, VM, VM, VM, VM],
         scratch(width),
     )
     back = lax.all_to_all(sums, "fde", 0, 0, tiled=True)
     blocks = nq * count // 128
     copies = call(
-        spread_kernel, pltpu.VMEM((shards // 2, groups, blocks, 128), f32), (in_vmem(back),)
+        spread_kernel, pltpu.VMEM((shards // 2, blocks, groups, 128), f32), (in_vmem(back),)
     )
     fde_scores = call(fold_kernel, S((nq, passage_fde.shape[0]), f32), (in_vmem(back),))
     half = shards // 2
@@ -313,7 +350,7 @@
         axis_index_groups=[[2 * k + c for k in range(half)] for c in range(2)],
         tiled=True,
     ).reshape(-1, 128)
-    far = lax.ppermute(near, "pas", swap)
+    far = moved(near, 1)
     rerank = call(
         final_kernel,
         S(candidates.shape, f32),

time: 85.4 us -> 81.1 us (0.950)
  blocking collectives: 52.1 us -> 45.4 us
  starting transfers between devices: 4.25 us -> 6.93 us
    all_to_all x1, blocking collectives: 24.9 us -> 19.3 us  [body(): near = lax.all_to_all(tiles, 'fde', 0, 0, tiled=True)]
    ppermute x2 -> x4, starting transfers between devices: 4.25 us -> 6.93 us  [moved(): return lax.ppermute(x, 'pas', [(k, k ^ flip) for k in range(shards)])]
  transfers between devices with their start and end apart: 2 -> 4, of which waited for: 1 -> 1; matrix products, arithmetic and copies ran while one was open for 0% -> 0% of each run, Pallas kernels for 19% -> 19%
where the time goes in v6:
time: 81.1 us; the launch traced here: 80.7 us
  blocking collectives  45.4 us (56%)
  Pallas kernels  26.3 us (32%)
  starting transfers between devices  6.93 us (9%)
    pallas_call x9, Pallas kernels, call(): pl.pallas_call(kernel, out_shape=outs, in_specs=[VM] * len(ins) if in_spe...  26.3 us
    all_to_all x1, blocking collectives, body(): near = lax.all_to_all(tiles, 'fde', 0, 0, tiled=True)  19.3 us
    all_to_all x1, blocking collectives, body(): lax.all_to_all(copies, 'pas', 0, 0, axis_index_groups=[[2 * k + c for k i...  14.8 us
    all_to_all x1, blocking collectives, body(): back = lax.all_to_all(sums, 'fde', 0, 0, tiled=True)  11.3 us
    ppermute x4, starting transfers between devices, moved(): return lax.ppermute(x, 'pas', [(k, k ^ flip) for k in range(shards)])  6.93 us
  transfers between devices with their start and end apart: 4, of which 1 were waited for; matrix products, arithmetic and copies ran while one was open for 0% of the time, Pallas kernels for 19%

profile of v6, /device:TPU:1, one launch (start us, length us, event | category | flops | bytes accessed | tf_op | source)
XLA Modules:
  0.0 80.7 jit_solution(4242508223169031813)
XLA Ops:
  0.6 0.0 copy-start
  0.6 1.1 %shard_map.87 = (bf16[512,128]{1,0:T(8,128)(2,1)S(1)}, bf16[8,128,128]{2,1,0:T(8,128)(2,1)S(1)}) custom-call(s32[16]{0:T(128)} %count_ref.3, bf16[16,32,128]{2,1,0:T(8,128)(2,1)} %q_ref.1), custom_call_target="tpu_custom_call" | custom-call | tf_op jit(solution)/shard_map/pallas_call | solution.py:245
  1.7 19.3 %all_to_all.15 = bf16[8,128,128]{2,1,0:T(8,128)(2,1)S(1)} all-to-all(bf16[8,128,128]{2,1,0:T(8,128)(2,1)S(1)} %get-tuple-element.11), channel_id=1, replica_groups=mesh['fde'=8,'pas'=32] {'fde'}, dimensions={0} | all-to-all | bytes 524288 | tf_op jit(solution)/shard_map/all_to_all | solution.py:276
  21.0 0.0 copy-start.3
  21.0 2.3 %collective-permute-start.2 = (bf16[1024,128]{1,0:T(8,128)(2,1)S(1)}, bf16[1024,128]{1,0:T(8,128)(2,1)S(1)}, u32[]{:S(2)}, u32[]{:S(2)}) collective-permute-start(bf16[1024,128]{1,0:T(8,128)(2,1)S(1)} %bitcast.8), channel_id=1, source_target_pairs={{0,1},{1,0},{2,3},{3,2},{4,5},{5,4},{6,7},{7,6},{8,9},{9,8},{10,11... | collective-permute-start | bytes 786440 | tf_op jit(solution)/shard_map/ppermute | solution.py:280
  23.3 1.2 %collective-permute-start = (bf16[1024,128]{1,0:T(8,128)(2,1)S(1)}, bf16[1024,128]{1,0:T(8,128)(2,1)S(1)}, u32[]{:S(2)}, u32[]{:S(2)}) collective-permute-start(bf16[1024,128]{1,0:T(8,128)(2,1)S(1)} %bitcast.9), channel_id=1, source_target_pairs={{0,8},{1,9},{2,10},{3,11},{4,12},{5,13},{6,14},{7,15},{8,0},{9,1},... | collective-permute-start | bytes 786440 | tf_op jit(solution)/shard_map/ppermute | solution.py:280
  24.6 1.5 %collective-permute-start.1 = (bf16[1024,128]{1,0:T(8,128)(2,1)S(1)}, bf16[1024,128]{1,0:T(8,128)(2,1)S(1)}, u32[]{:S(2)}, u32[]{:S(2)}) collective-permute-start(bf16[1024,128]{1,0:T(8,128)(2,1)S(1)} %bitcast.10), channel_id=1, source_target_pairs={{0,3},{1,2},{2,1},{3,0},{4,7},{5,6},{6,5},{7,4},{8,11},{9,10},{10,... | collective-permute-start | bytes 786440 | tf_op jit(solution)/shard_map/ppermute | solution.py:280
  26.0 3.3 %shard_map.86 = (bf16[32,256,128]{2,1,0:T(8,128)(2,1)S(1)}, s32[512]{0:T(512)S(1)}) custom-call(s32[32]{0:T(128)} %len_ref.1, bf16[32,256,128]{2,1,0:T(8,128)(2,1)} %p_ref.1), custom_call_target="tpu_custom_call" | custom-call | tf_op jit(solution)/shard_map/pallas_call | solution.py:245
  29.3 0.0 copy-start.1
  29.3 0.6 copy-done.1
  29.9 3.9 %shard_map.88.own_ref = f32[8,512]{1,0:T(8,128)S(1)} custom-call(s32[512]{0:T(512)} %copy-done.1, bf16[8192,128]{1,0:T(8,128)(2,1)S(1)} %bitcast.5, bf16[512,128]{1,0:T(8,128)(2,1)S(1)} %get-tuple-element.12.q_ref), custom_call_target="tpu_custom_call" | custom-call | tf_op jit(solution)/shard_map/pallas_call | solution.py:245
  33.8 0.0 copy-done
  33.8 0.0 copy-done.3
  33.8 0.4 fusion.fde_ref
  34.2 0.0 collective-permute-done.2.b_ref
  34.2 7.8 %shard_map.89.near_ref = f32[8,256]{1,0:T(8,128)S(1)} custom-call(s32[512]{0:T(512)} %copy-done.1, bf16[8192,128]{1,0:T(8,128)(2,1)S(1)} %bitcast.6, bf16[1024,128]{1,0:T(8,128)(2,1)S(1)} %bitcast.11, bf16[1024,128]{1,0:T(8,128)(2,1)S(1)} %collective-permute-done.2.b_ref), custom_call_target="tpu_custom_call" | custom-call | tf_op jit(solution)/shard_map/pallas_call | solution.py:245
  42.0 0.0 copy-start.2
  42.0 0.0 collective-permute-done.a_ref
  42.0 0.0 collective-permute-done.1.b_ref
  42.0 7.8 %shard_map.90 = f32[8,40,128]{2,1,0:T(8,128)S(1)} custom-call(s32[512]{0:T(512)} %copy-done.1, bf16[8192,128]{1,0:T(8,128)(2,1)S(1)} %bitcast.7, bf16[1024,128]{1,0:T(8,128)(2,1)S(1)} %collective-permute-done.a_ref, bf16[1024,128]{1,0:T(8,128)(2,1)S(1)} %collective-permute-done.1.b_ref, f32[8,512]{1,0:T(8,128)S(1)} %shard_map.88.own_ref, ...), custom_call_target="tpu_custom_call" | custom-call | tf_op jit(solution)/shard_map/pallas_call | solution.py:245
  49.9 11.3 %all_to_all.16.x_ref = f32[8,40,128]{2,1,0:T(8,128)S(1)} all-to-all(f32[8,40,128]{2,1,0:T(8,128)S(1)} %shard_map.90), channel_id=1, replica_groups=mesh['fde'=8,'pas'=32] {'fde'}, dimensions={0} | all-to-all | bytes 327680 | tf_op jit(solution)/shard_map/all_to_all | solution.py:338
  61.2 14.8 %all_to_all.17 = f32[16,4,8,128]{3,2,1,0:T(8,128)S(1)} all-to-all(f32[16,4,8,128]{3,2,1,0:T(8,128)S(1)} %shard_map.93), channel_id=1, replica_groups={{0,2,4,6,8,10,12,14,16,18,20,22,24,26,28,30},{1,3,5,7,9,11,13,15,17,19,..., dimensions={0} | all-to-all | bytes 524288 | tf_op jit(solution)/shard_map/all_to_all | solution.py:345
  76.0 1.9 %collective-permute-start.3 = (f32[512,128]{1,0:T(8,128)S(1)}, f32[512,128]{1,0:T(8,128)S(1)}, u32[]{:S(2)}, u32[]{:S(2)}) collective-permute-start(f32[512,128]{1,0:T(8,128)S(1)} %bitcast.12), channel_id=1, source_target_pairs={{0,1},{1,0},{2,3},{3,2},{4,5},{5,4},{6,7},{7,6},{8,9},{9,8},{10,11... | collective-permute-start | bytes 786440 | tf_op jit(solution)/shard_map/ppermute | solution.py:280
  77.9 0.0 copy-done.2
  77.9 0.1 shard_map.92
  78.0 0.6 shard_map.91
  78.6 0.4 collective-permute-done.3.far_ref
  79.1 1.7 %shard_map.94 = f32[16,32]{1,0:T(8,128)} custom-call(s32[16]{0:T(128)} %count_ref.3, s32[8,512]{1,0:T(8,128)S(1)} %get-tuple-element.13.want_ref, bf16[128,512]{1,0:T(8,128)(2,1)S(1)} %get-tuple-element.14.hot_near_ref, bf16[128,512]{1,0:T(8,128)(2,1)S(1)} %get-tuple-element.15.hot_far_ref, f32[512,128]{1,0:T(8,128)S(1)} %bitcast.13, ...), custom_call_target="tpu_custom_call" | custom-call | tf_op jit(solution)/shard_map/pallas_call | solution.py:245
  (1 shorter events, 0.0 us)
Async XLA Ops:
  0.6 33.2 %copy-start = (bf16[256,1280]{1,0:T(8,128)(2,1)S(1)}, bf16[256,1280]{1,0:T(8,128)(2,1)}, u32[]{:S(2)}) copy-start(bf16[256,1280]{1,0:T(8,128)(2,1)} %param.8) | copy-start | bytes 1966084
  21.0 12.8 %copy-start.3 = (bf16[128,1280]{1,0:T(8,128)(2,1)S(1)}, bf16[128,1280]{1,0:T(8,128)(2,1)}, u32[]{:S(2)}) copy-start(bf16[128,1280]{1,0:T(8,128)(2,1)} %param.7) | copy-start | bytes 983044
  21.0 13.2 %collective-permute-start.2 = (bf16[1024,128]{1,0:T(8,128)(2,1)S(1)}, bf16[1024,128]{1,0:T(8,128)(2,1)S(1)}, u32[]{:S(2)}, u32[]{:S(2)}) collective-permute-start(bf16[1024,128]{1,0:T(8,128)(2,1)S(1)} %bitcast.8), channel_id=1, source_target_pairs={{0,1},{1,0},{2,3},{3,2},{4,5},{5,4},{6,7},{7,6},{8,9},{9,8},{10,11... | collective-permute-start | bytes 786440 | tf_op jit(solution)/shard_map/ppermute | solution.py:280
  23.3 18.7 %collective-permute-start = (bf16[1024,128]{1,0:T(8,128)(2,1)S(1)}, bf16[1024,128]{1,0:T(8,128)(2,1)S(1)}, u32[]{:S(2)}, u32[]{:S(2)}) collective-permute-start(bf16[1024,128]{1,0:T(8,128)(2,1)S(1)} %bitcast.9), channel_id=1, source_target_pairs={{0,8},{1,9},{2,10},{3,11},{4,12},{5,13},{6,14},{7,15},{8,0},{9,1},... | collective-permute-start | bytes 786440 | tf_op jit(solution)/shard_map/ppermute | solution.py:280
  24.6 17.5 %collective-permute-start.1 = (bf16[1024,128]{1,0:T(8,128)(2,1)S(1)}, bf16[1024,128]{1,0:T(8,128)(2,1)S(1)}, u32[]{:S(2)}, u32[]{:S(2)}) collective-permute-start(bf16[1024,128]{1,0:T(8,128)(2,1)S(1)} %bitcast.10), channel_id=1, source_target_pairs={{0,3},{1,2},{2,1},{3,0},{4,7},{5,6},{6,5},{7,4},{8,11},{9,10},{10,... | collective-permute-start | bytes 786440 | tf_op jit(solution)/shard_map/ppermute | solution.py:280
  29.3 0.6 copy-start.1
  42.0 35.9 %copy-start.2 = (s32[16,32]{1,0:T(8,128)S(1)}, s32[16,32]{1,0:T(8,128)}, u32[]{:S(2)}) copy-start(s32[16,32]{1,0:T(8,128)} %cand_ref.1) | copy-start | bytes 6148
  76.0 3.1 %collective-permute-start.3 = (f32[512,128]{1,0:T(8,128)S(1)}, f32[512,128]{1,0:T(8,128)S(1)}, u32[]{:S(2)}, u32[]{:S(2)}) collective-permute-start(f32[512,128]{1,0:T(8,128)S(1)} %bitcast.12), channel_id=1, source_target_pairs={{0,1},{1,0},{2,3},{3,2},{4,5},{5,4},{6,7},{7,6},{8,9},{9,8},{10,11... | collective-permute-start | bytes 786440 | tf_op jit(solution)/shard_map/ppermute | solution.py:280

commit v7 on v6

--- a/solution.py
+++ b/solution.py
@@ -25,17 +25,11 @@
     return hi, (x - hi.astype(f32)).astype(bf16)
 
 
-def prep_kernel(len_ref, p_ref, o_ref, sched_ref):
-    count, pt, dim = p_ref.shape
+def prep_kernel(len_ref, p_ref, o_ref, sched_ref, sem):
+    count, pt, dim = o_ref.shape
     per = pt // CH
-
-    def clean(p, _):
-        rows = p_ref[p].astype(f32)
-        keep = iota((pt, dim), 0) < len_ref[p]
-        o_ref[p] = jnp.where(keep, rows, rows[0:1, :]).astype(bf16)
-        return 0
-
-    lax.fori_loop(0, count, clean, 0, unroll=4)
+    copy = pltpu.make_async_copy(p_ref, o_ref, sem)
+    copy.start()
 
     def listed(p, at):
         live = (len_ref[p] + (CH - 1)) // CH
@@ -51,6 +45,17 @@
     rest = total % GRP
     sched_ref[384] = total // GRP + jnp.where(rest > GRP // 2, 1, 0)
     sched_ref[385] = jnp.where((rest > 0) & (rest <= GRP // 2), 1, 0)
+    copy.wait()
+
+    def clean(p, _):
+        at = pl.multiple_of((len_ref[p] - 1) // CH * CH, CH)
+        rows = o_ref[p, pl.ds(at, CH), :].astype(f32)
+        first = o_ref[p, 0:CH, :].astype(f32)[0:1, :]
+        keep = iota((CH, dim), 0) + at < len_ref[p]
+        o_ref[p, pl.ds(at, CH), :] = jnp.where(keep, rows, first).astype(bf16)
+        return 0
+
+    lax.fori_loop(0, count, clean, 0, unroll=4)
 
 
 def best_matches(sched_ref, p_ref, blocks, part_ref, best_ref):
@@ -197,12 +202,16 @@
         o_ref[:, h * 128 : (h + 1) * 128] = x
 
 
-def plan_kernel(cand_ref, near_ref, far_ref, want_ref):
+def plan_kernel(count_ref, cand_ref, near_ref, far_ref, want_ref, div_ref):
     nq, nc = cand_ref.shape
     rows, n = near_ref.shape
     ids = jnp.concatenate([cand_ref[q : q + 1, :] for q in range(nq)], axis=1)
     query = iota((1, n), 1) // nc
     want_ref[...] = jnp.broadcast_to((query & 3) * 32 + (ids & 31), want_ref.shape)
+    div = jnp.zeros((1, n), f32)
+    for q in range(nq):
+        div = jnp.where(query == q, count_ref[q].astype(f32), div)
+    div_ref[...] = jnp.broadcast_to(div, div_ref.shape)
     owner = ids >> 5
     r = iota((rows, 1), 0)
     at = (r & 7) * 32 + (r >> 3) * 2
@@ -211,7 +220,7 @@
         ref[...] = jnp.where(at + c == owner, 1.0, 0.0).astype(bf16)
 
 
-def final_kernel(count_ref, want_ref, hot_near_ref, hot_far_ref, near_ref, far_ref, o_ref):
+def final_kernel(want_ref, div_ref, hot_near_ref, hot_far_ref, near_ref, far_ref, o_ref):
     nq, nc = o_ref.shape
     blocks = nq * nc // 128
     copies = near_ref.shape[0] // (blocks * 8)
@@ -228,9 +237,10 @@
         x = x[:128] + x[128:]
         want = want_ref[0:1, lanes]
         row = jnp.sum(jnp.where(iota(x.shape, 0) == want, x, 0.0), axis=0, keepdims=True)
+        row = row / div_ref[0:1, lanes]
         for j in range(128 // nc):
             q = g * (128 // nc) + j
-            o_ref[q : q + 1, :] = row[:, j * nc : (j + 1) * nc] / count_ref[q].astype(f32)
+            o_ref[q : q + 1, :] = row[:, j * nc : (j + 1) * nc]
 
 
 def in_vmem(x):
@@ -283,10 +293,11 @@
     x_q, y_q = moved(quarter, 8), moved(quarter, 3)
     clean, sched = call(
         prep_kernel,
-        (pltpu.VMEM(passage_tokens.shape, bf16), S((512,), i32)),
+        (pltpu.VMEM(passage_tokens.shape, bf16), pltpu.HBM((512,), i32)),
         (in_hbm(passage_lengths), in_hbm(passage_tokens)),
         (VM, SM),
-        [SM, VM],
+        [SM, pl.BlockSpec(memory_space=pl.ANY)],
+        [pltpu.SemaphoreType.DMA],
     )
     clean, sched = clean.reshape(count * pt, dim), in_hbm(sched)
 
@@ -295,8 +306,12 @@
     )
     pairs = nq * candidates.shape[1]
     hot = pltpu.VMEM((shards // 2 * groups, pairs), bf16)
-    hot_near, hot_far, want = call(
-        plan_kernel, (hot, hot, pltpu.VMEM((8, pairs), i32)), (candidates,), (VM, VM, VM)
+    hot_near, hot_far, want, div = call(
+        plan_kernel,
+        (hot, hot, pltpu.VMEM((8, pairs), i32), pltpu.VMEM((8, pairs), f32)),
+        (in_hbm(query_token_totals), candidates),
+        (VM, VM, VM, VM),
+        [SM, VM],
     )
 
     def scratch(width):
@@ -355,15 +370,13 @@
         final_kernel,
         S(candidates.shape, f32),
         (
-            in_hbm(query_token_totals),
             in_vmem(want),
+            in_vmem(div),
             in_vmem(hot_near),
             in_vmem(hot_far),
             in_vmem(near),
             in_vmem(far),
         ),
-        VM,
-        [SM, VM, VM, VM, VM, VM],
     )
     return fde_scores, rerank
 

time: 81.1 us -> 79.9 us (0.985)
  transfers between devices with their start and end apart: 4 -> 4, of which waited for: 1 -> 0; matrix products, arithmetic and copies ran while one was open for 0% -> 0% of each run, Pallas kernels for 19% -> 20%
where the time goes in v7:
time: 79.9 us; the launch traced here: 79.6 us
  blocking collectives  45.4 us (57%)
  Pallas kernels  26.2 us (33%)
  starting transfers between devices  6.93 us (9%)
    pallas_call x9, Pallas kernels, call(): pl.pallas_call(kernel, out_shape=outs, in_specs=[VM] * len(ins) if in_spe...  26.2 us
    all_to_all x1, blocking collectives, body(): near = lax.all_to_all(tiles, 'fde', 0, 0, tiled=True)  19.3 us
    all_to_all x1, blocking collectives, body(): lax.all_to_all(copies, 'pas', 0, 0, axis_index_groups=[[2 * k + c for k i...  14.8 us
    all_to_all x1, blocking collectives, body(): back = lax.all_to_all(sums, 'fde', 0, 0, tiled=True)  11.3 us
    ppermute x4, starting transfers between devices, moved(): return lax.ppermute(x, 'pas', [(k, k ^ flip) for k in range(shards)])  6.93 us
  transfers between devices with their start and end apart: 4, of which 0 were waited for; matrix products, arithmetic and copies ran while one was open for 0% of the time, Pallas kernels for 20%

profile of v7, /device:TPU:1, one launch (start us, length us, event | category | flops | bytes accessed | tf_op | source)
XLA Modules:
  0.0 79.6 jit_solution(3076520944197330485)
XLA Ops:
  0.6 0.0 copy-start
  0.6 1.1 %shard_map.87 = (bf16[512,128]{1,0:T(8,128)(2,1)S(1)}, bf16[8,128,128]{2,1,0:T(8,128)(2,1)S(1)}) custom-call(s32[16]{0:T(128)} %count_ref.3, bf16[16,32,128]{2,1,0:T(8,128)(2,1)} %q_ref.1), custom_call_target="tpu_custom_call" | custom-call | tf_op jit(solution)/shard_map/pallas_call | solution.py:255
  1.7 19.3 %all_to_all.15 = bf16[8,128,128]{2,1,0:T(8,128)(2,1)S(1)} all-to-all(bf16[8,128,128]{2,1,0:T(8,128)(2,1)S(1)} %get-tuple-element.12), channel_id=1, replica_groups=mesh['fde'=8,'pas'=32] {'fde'}, dimensions={0} | all-to-all | bytes 524288 | tf_op jit(solution)/shard_map/all_to_all | solution.py:286
  21.0 0.0 copy-start.2
  21.0 2.3 %collective-permute-start.2 = (bf16[1024,128]{1,0:T(8,128)(2,1)S(1)}, bf16[1024,128]{1,0:T(8,128)(2,1)S(1)}, u32[]{:S(2)}, u32[]{:S(2)}) collective-permute-start(bf16[1024,128]{1,0:T(8,128)(2,1)S(1)} %bitcast.8), channel_id=1, source_target_pairs={{0,1},{1,0},{2,3},{3,2},{4,5},{5,4},{6,7},{7,6},{8,9},{9,8},{10,11... | collective-permute-start | bytes 786440 | tf_op jit(solution)/shard_map/ppermute | solution.py:290
  23.3 1.2 %collective-permute-start = (bf16[1024,128]{1,0:T(8,128)(2,1)S(1)}, bf16[1024,128]{1,0:T(8,128)(2,1)S(1)}, u32[]{:S(2)}, u32[]{:S(2)}) collective-permute-start(bf16[1024,128]{1,0:T(8,128)(2,1)S(1)} %bitcast.9), channel_id=1, source_target_pairs={{0,8},{1,9},{2,10},{3,11},{4,12},{5,13},{6,14},{7,15},{8,0},{9,1},... | collective-permute-start | bytes 786440 | tf_op jit(solution)/shard_map/ppermute | solution.py:290
  24.6 1.5 %collective-permute-start.1 = (bf16[1024,128]{1,0:T(8,128)(2,1)S(1)}, bf16[1024,128]{1,0:T(8,128)(2,1)S(1)}, u32[]{:S(2)}, u32[]{:S(2)}) collective-permute-start(bf16[1024,128]{1,0:T(8,128)(2,1)S(1)} %bitcast.10), channel_id=1, source_target_pairs={{0,3},{1,2},{2,1},{3,0},{4,7},{5,6},{6,5},{7,4},{8,11},{9,10},{10,... | collective-permute-start | bytes 786440 | tf_op jit(solution)/shard_map/ppermute | solution.py:290
  26.0 3.1 %shard_map.86 = (bf16[32,256,128]{2,1,0:T(8,128)(2,1)S(1)}, s32[512]{0:T(512)}) custom-call(s32[32]{0:T(128)} %len_ref.1, bf16[32,256,128]{2,1,0:T(8,128)(2,1)} %p_ref.1), custom_call_target="tpu_custom_call" | custom-call | tf_op jit(solution)/shard_map/pallas_call | solution.py:255
  29.1 3.9 %shard_map.88.own_ref = f32[8,512]{1,0:T(8,128)S(1)} custom-call(s32[512]{0:T(512)} %get-tuple-element.10.sched_ref, bf16[8192,128]{1,0:T(8,128)(2,1)S(1)} %bitcast.5, bf16[512,128]{1,0:T(8,128)(2,1)S(1)} %get-tuple-element.13.q_ref), custom_call_target="tpu_custom_call" | custom-call | tf_op jit(solution)/shard_map/pallas_call | solution.py:255
  33.0 0.0 copy-done
  33.0 0.0 copy-done.2
  33.0 0.4 fusion.fde_ref
  33.4 0.0 collective-permute-done.2.b_ref
  33.4 7.8 %shard_map.89.near_ref = f32[8,256]{1,0:T(8,128)S(1)} custom-call(s32[512]{0:T(512)} %get-tuple-element.10.sched_ref, bf16[8192,128]{1,0:T(8,128)(2,1)S(1)} %bitcast.6, bf16[1024,128]{1,0:T(8,128)(2,1)S(1)} %bitcast.11, bf16[1024,128]{1,0:T(8,128)(2,1)S(1)} %collective-permute-done.2.b_ref), custom_call_target="tpu_custom_call" | custom-call | tf_op jit(solution)/shard_map/pallas_call | solution.py:255
  41.2 0.0 copy-start.1
  41.2 0.0 collective-permute-done.a_ref
  41.2 0.0 collective-permute-done.1.b_ref
  41.3 7.8 %shard_map.90 = f32[8,40,128]{2,1,0:T(8,128)S(1)} custom-call(s32[512]{0:T(512)} %get-tuple-element.10.sched_ref, bf16[8192,128]{1,0:T(8,128)(2,1)S(1)} %bitcast.7, bf16[1024,128]{1,0:T(8,128)(2,1)S(1)} %collective-permute-done.a_ref, bf16[1024,128]{1,0:T(8,128)(2,1)S(1)} %collective-permute-done.1.b_ref, f32[8,512]{1,0:T(8,128)S(1)} %shard_map.88.own_ref, ...), custom_call_target="tpu_custom_call" | custom-call | tf_op jit(solution)/shard_map/pallas_call | solution.py:255
  49.1 11.3 %all_to_all.16.x_ref = f32[8,40,128]{2,1,0:T(8,128)S(1)} all-to-all(f32[8,40,128]{2,1,0:T(8,128)S(1)} %shard_map.90), channel_id=1, replica_groups=mesh['fde'=8,'pas'=32] {'fde'}, dimensions={0} | all-to-all | bytes 327680 | tf_op jit(solution)/shard_map/all_to_all | solution.py:353
  60.4 14.8 %all_to_all.17 = f32[16,4,8,128]{3,2,1,0:T(8,128)S(1)} all-to-all(f32[16,4,8,128]{3,2,1,0:T(8,128)S(1)} %shard_map.93), channel_id=1, replica_groups={{0,2,4,6,8,10,12,14,16,18,20,22,24,26,28,30},{1,3,5,7,9,11,13,15,17,19,..., dimensions={0} | all-to-all | bytes 524288 | tf_op jit(solution)/shard_map/all_to_all | solution.py:360
  75.2 1.9 %collective-permute-start.3 = (f32[512,128]{1,0:T(8,128)S(1)}, f32[512,128]{1,0:T(8,128)S(1)}, u32[]{:S(2)}, u32[]{:S(2)}) collective-permute-start(f32[512,128]{1,0:T(8,128)S(1)} %bitcast.12), channel_id=1, source_target_pairs={{0,1},{1,0},{2,3},{3,2},{4,5},{5,4},{6,7},{7,6},{8,9},{9,8},{10,11... | collective-permute-start | bytes 786440 | tf_op jit(solution)/shard_map/ppermute | solution.py:290
  77.1 0.0 copy-done.1
  77.1 0.8 shard_map.92
  77.9 0.6 shard_map.91
  78.5 0.0 collective-permute-done.3.far_ref
  78.5 1.0 %shard_map.94 = f32[16,32]{1,0:T(8,128)} custom-call(s32[8,512]{1,0:T(8,128)S(1)} %get-tuple-element.14.want_ref, f32[8,512]{1,0:T(8,128)S(1)} %get-tuple-element.15.div_ref, bf16[128,512]{1,0:T(8,128)(2,1)S(1)} %get-tuple-element.16.hot_near_ref, bf16[128,512]{1,0:T(8,128)(2,1)S(1)} %get-tuple-element.17.hot_far_ref, f32[512,128]{1,0:T(8,128)S(1)} %bitcast.13, ...), custom_call_target="tpu_custom_call" | custom-call | tf_op jit(solution)/shard_map/pallas_call | solution.py:255
  (1 shorter events, 0.0 us)
Async XLA Ops:
  0.6 32.4 %copy-start = (bf16[256,1280]{1,0:T(8,128)(2,1)S(1)}, bf16[256,1280]{1,0:T(8,128)(2,1)}, u32[]{:S(2)}) copy-start(bf16[256,1280]{1,0:T(8,128)(2,1)} %param.8) | copy-start | bytes 1966084
  21.0 12.0 %copy-start.2 = (bf16[128,1280]{1,0:T(8,128)(2,1)S(1)}, bf16[128,1280]{1,0:T(8,128)(2,1)}, u32[]{:S(2)}) copy-start(bf16[128,1280]{1,0:T(8,128)(2,1)} %param.7) | copy-start | bytes 983044
  21.0 12.4 %collective-permute-start.2 = (bf16[1024,128]{1,0:T(8,128)(2,1)S(1)}, bf16[1024,128]{1,0:T(8,128)(2,1)S(1)}, u32[]{:S(2)}, u32[]{:S(2)}) collective-permute-start(bf16[1024,128]{1,0:T(8,128)(2,1)S(1)} %bitcast.8), channel_id=1, source_target_pairs={{0,1},{1,0},{2,3},{3,2},{4,5},{5,4},{6,7},{7,6},{8,9},{9,8},{10,11... | collective-permute-start | bytes 786440 | tf_op jit(solution)/shard_map/ppermute | solution.py:290
  23.3 17.9 %collective-permute-start = (bf16[1024,128]{1,0:T(8,128)(2,1)S(1)}, bf16[1024,128]{1,0:T(8,128)(2,1)S(1)}, u32[]{:S(2)}, u32[]{:S(2)}) collective-permute-start(bf16[1024,128]{1,0:T(8,128)(2,1)S(1)} %bitcast.9), channel_id=1, source_target_pairs={{0,8},{1,9},{2,10},{3,11},{4,12},{5,13},{6,14},{7,15},{8,0},{9,1},... | collective-permute-start | bytes 786440 | tf_op jit(solution)/shard_map/ppermute | solution.py:290
  24.6 16.7 %collective-permute-start.1 = (bf16[1024,128]{1,0:T(8,128)(2,1)S(1)}, bf16[1024,128]{1,0:T(8,128)(2,1)S(1)}, u32[]{:S(2)}, u32[]{:S(2)}) collective-permute-start(bf16[1024,128]{1,0:T(8,128)(2,1)S(1)} %bitcast.10), channel_id=1, source_target_pairs={{0,3},{1,2},{2,1},{3,0},{4,7},{5,6},{6,5},{7,4},{8,11},{9,10},{10,... | collective-permute-start | bytes 786440 | tf_op jit(solution)/shard_map/ppermute | solution.py:290
  41.2 35.9 %copy-start.1 = (s32[16,32]{1,0:T(8,128)S(1)}, s32[16,32]{1,0:T(8,128)}, u32[]{:S(2)}) copy-start(s32[16,32]{1,0:T(8,128)} %cand_ref.1) | copy-start | bytes 6148
  75.2 3.3 %collective-permute-start.3 = (f32[512,128]{1,0:T(8,128)S(1)}, f32[512,128]{1,0:T(8,128)S(1)}, u32[]{:S(2)}, u32[]{:S(2)}) collective-permute-start(f32[512,128]{1,0:T(8,128)S(1)} %bitcast.12), channel_id=1, source_target_pairs={{0,1},{1,0},{2,3},{3,2},{4,5},{5,4},{6,7},{7,6},{8,9},{9,8},{10,11... | collective-permute-start | bytes 786440 | tf_op jit(solution)/shard_map/ppermute | solution.py:290

commit v8 on v7

--- a/solution.py
+++ b/solution.py
@@ -12,7 +12,7 @@
 VM = pl.BlockSpec(memory_space=pltpu.VMEM)
 SM = pl.BlockSpec(memory_space=pltpu.SMEM)
 CH = 32
-GRP = 32
+GRP = 64
 COLS = 256
 
 
@@ -193,16 +193,13 @@
             o_ref[k, g] = mine
 
 
-def fold_kernel(x_ref, o_ref):
-    nq, width = o_ref.shape
-    for h in range(width // 128):
-        x = x_ref[0, h * nq : (h + 1) * nq, :]
+def plan_kernel(count_ref, cand_ref, x_ref, fde_ref, near_ref, far_ref, want_ref, div_ref):
+    for h in range(fde_ref.shape[1] // 128):
+        rows = slice(h * fde_ref.shape[0], (h + 1) * fde_ref.shape[0])
+        total = x_ref[0, rows, :]
         for i in range(1, x_ref.shape[0]):
-            x = x + x_ref[i, h * nq : (h + 1) * nq, :]
-        o_ref[:, h * 128 : (h + 1) * 128] = x
-
-
-def plan_kernel(count_ref, cand_ref, near_ref, far_ref, want_ref, div_ref):
+            total = total + x_ref[i, rows, :]
+        fde_ref[:, h * 128 : (h + 1) * 128] = total
     nq, nc = cand_ref.shape
     rows, n = near_ref.shape
     ids = jnp.concatenate([cand_ref[q : q + 1, :] for q in range(nq)], axis=1)
@@ -306,13 +303,6 @@
     )
     pairs = nq * candidates.shape[1]
     hot = pltpu.VMEM((shards // 2 * groups, pairs), bf16)
-    hot_near, hot_far, want, div = call(
-        plan_kernel,
-        (hot, hot, pltpu.VMEM((8, pairs), i32), pltpu.VMEM((8, pairs), f32)),
-        (in_hbm(query_token_totals), candidates),
-        (VM, VM, VM, VM),
-        [SM, VM],
-    )
 
     def scratch(width):
         return [pltpu.VMEM((count * pt // CH * 8, width), f32), pltpu.VMEM((count, width), f32)]
@@ -355,7 +345,19 @@
     copies = call(
         spread_kernel, pltpu.VMEM((shards // 2, blocks, groups, 128), f32), (in_vmem(back),)
     )
-    fde_scores = call(fold_kernel, S((nq, passage_fde.shape[0]), f32), (in_vmem(back),))
+    fde_scores, hot_near, hot_far, want, div = call(
+        plan_kernel,
+        (
+            S((nq, passage_fde.shape[0]), f32),
+            hot,
+            hot,
+            pltpu.VMEM((8, pairs), i32),
+            pltpu.VMEM((8, pairs), f32),
+        ),
+        (in_hbm(query_token_totals), candidates, in_vmem(back)),
+        (VM, VM, VM, VM, VM),
+        [SM, VM, VM],
+    )
     half = shards // 2
     near = lax.all_to_all(
         copies,

time: 79.9 us -> 78.7 us (0.985)
  Pallas kernels: 26.2 us -> 25 us
    pallas_call x9 -> x8, Pallas kernels: 26.2 us -> 25 us  [call(): pl.pallas_call(kernel, out_shape=outs, in_specs=[VM] * len(ins) if in_spe...]
    all_to_all x1, blocking collectives: 11.3 us -> 10.4 us  [body(): back = lax.all_to_all(sums, 'fde', 0, 0, tiled=True)]
where the time goes in v8:
time: 78.7 us; the launch traced here: 78.3 us
  blocking collectives  45.1 us (57%)
  Pallas kernels  25 us (32%)
  starting transfers between devices  7.04 us (9%)
    pallas_call x8, Pallas kernels, call(): pl.pallas_call(kernel, out_shape=outs, in_specs=[VM] * len(ins) if in_spe...  25 us
    all_to_all x1, blocking collectives, body(): near = lax.all_to_all(tiles, 'fde', 0, 0, tiled=True)  19.3 us
    all_to_all x1, blocking collectives, body(): lax.all_to_all(copies, 'pas', 0, 0, axis_index_groups=[[2 * k + c for k i...  15.4 us
    all_to_all x1, blocking collectives, body(): back = lax.all_to_all(sums, 'fde', 0, 0, tiled=True)  10.4 us
    ppermute x4, starting transfers between devices, moved(): return lax.ppermute(x, 'pas', [(k, k ^ flip) for k in range(shards)])  7.04 us
  transfers between devices with their start and end apart: 4, of which 0 were waited for; matrix products, arithmetic and copies ran while one was open for 0% of the time, Pallas kernels for 20%

profile of v8, /device:TPU:1, one launch (start us, length us, event | category | flops | bytes accessed | tf_op | source)
XLA Modules:
  0.0 78.3 jit_solution(7704616370013005580)
XLA Ops:
  0.6 0.0 copy-start
  0.6 1.1 %shard_map.87 = (bf16[512,128]{1,0:T(8,128)(2,1)S(1)}, bf16[8,128,128]{2,1,0:T(8,128)(2,1)S(1)}) custom-call(s32[16]{0:T(128)} %count_ref.3, bf16[16,32,128]{2,1,0:T(8,128)(2,1)} %q_ref.1), custom_call_target="tpu_custom_call" | custom-call | tf_op jit(solution)/shard_map/pallas_call | solution.py:252
  1.7 19.3 %all_to_all.15 = bf16[8,128,128]{2,1,0:T(8,128)(2,1)S(1)} all-to-all(bf16[8,128,128]{2,1,0:T(8,128)(2,1)S(1)} %get-tuple-element.13), channel_id=1, replica_groups=mesh['fde'=8,'pas'=32] {'fde'}, dimensions={0} | all-to-all | bytes 524288 | tf_op jit(solution)/shard_map/all_to_all | solution.py:283
  21.0 0.0 copy-start.2
  21.0 2.3 %collective-permute-start.2 = (bf16[1024,128]{1,0:T(8,128)(2,1)S(1)}, bf16[1024,128]{1,0:T(8,128)(2,1)S(1)}, u32[]{:S(2)}, u32[]{:S(2)}) collective-permute-start(bf16[1024,128]{1,0:T(8,128)(2,1)S(1)} %bitcast.8), channel_id=1, source_target_pairs={{0,1},{1,0},{2,3},{3,2},{4,5},{5,4},{6,7},{7,6},{8,9},{9,8},{10,11... | collective-permute-start | bytes 786440 | tf_op jit(solution)/shard_map/ppermute | solution.py:287
  23.3 1.2 %collective-permute-start = (bf16[1024,128]{1,0:T(8,128)(2,1)S(1)}, bf16[1024,128]{1,0:T(8,128)(2,1)S(1)}, u32[]{:S(2)}, u32[]{:S(2)}) collective-permute-start(bf16[1024,128]{1,0:T(8,128)(2,1)S(1)} %bitcast.9), channel_id=1, source_target_pairs={{0,8},{1,9},{2,10},{3,11},{4,12},{5,13},{6,14},{7,15},{8,0},{9,1},... | collective-permute-start | bytes 786440 | tf_op jit(solution)/shard_map/ppermute | solution.py:287
  24.6 1.5 %collective-permute-start.1 = (bf16[1024,128]{1,0:T(8,128)(2,1)S(1)}, bf16[1024,128]{1,0:T(8,128)(2,1)S(1)}, u32[]{:S(2)}, u32[]{:S(2)}) collective-permute-start(bf16[1024,128]{1,0:T(8,128)(2,1)S(1)} %bitcast.10), channel_id=1, source_target_pairs={{0,3},{1,2},{2,1},{3,0},{4,7},{5,6},{6,5},{7,4},{8,11},{9,10},{10,... | collective-permute-start | bytes 786440 | tf_op jit(solution)/shard_map/ppermute | solution.py:287
  26.0 3.1 %shard_map.86 = (bf16[32,256,128]{2,1,0:T(8,128)(2,1)S(1)}, s32[512]{0:T(512)}) custom-call(s32[32]{0:T(128)} %len_ref.1, bf16[32,256,128]{2,1,0:T(8,128)(2,1)} %p_ref.1), custom_call_target="tpu_custom_call" | custom-call | tf_op jit(solution)/shard_map/pallas_call | solution.py:252
  29.1 3.5 %shard_map.88.own_ref = f32[8,512]{1,0:T(8,128)S(1)} custom-call(s32[512]{0:T(512)} %get-tuple-element.11.sched_ref, bf16[8192,128]{1,0:T(8,128)(2,1)S(1)} %bitcast.5, bf16[512,128]{1,0:T(8,128)(2,1)S(1)} %get-tuple-element.14.q_ref), custom_call_target="tpu_custom_call" | custom-call | tf_op jit(solution)/shard_map/pallas_call | solution.py:252
  32.7 0.0 copy-done
  32.7 0.0 copy-done.2
  32.7 0.4 fusion.fde_ref
  33.1 0.0 collective-permute-done.2.b_ref
  33.1 7.5 %shard_map.89.near_ref = f32[8,256]{1,0:T(8,128)S(1)} custom-call(s32[512]{0:T(512)} %get-tuple-element.11.sched_ref, bf16[8192,128]{1,0:T(8,128)(2,1)S(1)} %bitcast.6, bf16[1024,128]{1,0:T(8,128)(2,1)S(1)} %bitcast.11, bf16[1024,128]{1,0:T(8,128)(2,1)S(1)} %collective-permute-done.2.b_ref), custom_call_target="tpu_custom_call" | custom-call | tf_op jit(solution)/shard_map/pallas_call | solution.py:252
  40.5 0.0 copy-start.1
  40.5 0.0 collective-permute-done.a_ref
  40.6 0.0 collective-permute-done.1.b_ref
  40.6 7.5 %shard_map.90 = f32[8,40,128]{2,1,0:T(8,128)S(1)} custom-call(s32[512]{0:T(512)} %get-tuple-element.11.sched_ref, bf16[8192,128]{1,0:T(8,128)(2,1)S(1)} %bitcast.7, bf16[1024,128]{1,0:T(8,128)(2,1)S(1)} %collective-permute-done.a_ref, bf16[1024,128]{1,0:T(8,128)(2,1)S(1)} %collective-permute-done.1.b_ref, f32[8,512]{1,0:T(8,128)S(1)} %shard_map.88.own_ref, ...), custom_call_target="tpu_custom_call" | custom-call | tf_op jit(solution)/shard_map/pallas_call | solution.py:252
  48.1 10.4 %all_to_all.16.x_ref = f32[8,40,128]{2,1,0:T(8,128)S(1)} all-to-all(f32[8,40,128]{2,1,0:T(8,128)S(1)} %shard_map.90), channel_id=1, replica_groups=mesh['fde'=8,'pas'=32] {'fde'}, dimensions={0} | all-to-all | bytes 327680 | tf_op jit(solution)/shard_map/all_to_all | solution.py:343
  58.6 15.4 %all_to_all.17 = f32[16,4,8,128]{3,2,1,0:T(8,128)S(1)} all-to-all(f32[16,4,8,128]{3,2,1,0:T(8,128)S(1)} %shard_map.92), channel_id=1, replica_groups={{0,2,4,6,8,10,12,14,16,18,20,22,24,26,28,30},{1,3,5,7,9,11,13,15,17,19,..., dimensions={0} | all-to-all | bytes 524288 | tf_op jit(solution)/shard_map/all_to_all | solution.py:362
  74.0 2.0 %collective-permute-start.3 = (f32[512,128]{1,0:T(8,128)S(1)}, f32[512,128]{1,0:T(8,128)S(1)}, u32[]{:S(2)}, u32[]{:S(2)}) collective-permute-start(f32[512,128]{1,0:T(8,128)S(1)} %bitcast.12), channel_id=1, source_target_pairs={{0,1},{1,0},{2,3},{3,2},{4,5},{5,4},{6,7},{7,6},{8,9},{9,8},{10,11... | collective-permute-start | bytes 786440 | tf_op jit(solution)/shard_map/ppermute | solution.py:287
  76.0 0.0 copy-done.1
  76.0 1.3 %shard_map.91 = (f32[16,256]{1,0:T(8,128)}, bf16[128,512]{1,0:T(8,128)(2,1)S(1)}, bf16[128,512]{1,0:T(8,128)(2,1)S(1)}, s32[8,512]{1,0:T(8,128)S(1)}, f32[8,512]{1,0:T(8,128)S(1)}) custom-call(s32[16]{0:T(128)} %count_ref.3, s32[16,32]{1,0:T(8,128)S(1)} %copy-done.1, f32[8,40,128]{2,1,0:T(8,128)S(1)} %all_to_all.16.x_ref), custom_call_target="tpu_custom_call" | custom-call | tf_op jit(solution)/shard_map/pallas_call | solution.py:252
  77.3 0.0 collective-permute-done.3.far_ref
  77.3 1.0 %shard_map.93 = f32[16,32]{1,0:T(8,128)} custom-call(s32[8,512]{1,0:T(8,128)S(1)} %get-tuple-element.16.want_ref, f32[8,512]{1,0:T(8,128)S(1)} %get-tuple-element.17.div_ref, bf16[128,512]{1,0:T(8,128)(2,1)S(1)} %get-tuple-element.18.hot_near_ref, bf16[128,512]{1,0:T(8,128)(2,1)S(1)} %get-tuple-element.19.hot_far_ref, f32[512,128]{1,0:T(8,128)S(1)} %bitcast.13, ...), custom_call_target="tpu_custom_call" | custom-call | tf_op jit(solution)/shard_map/pallas_call | solution.py:252
  (1 shorter events, 0.0 us)
Async XLA Ops:
  0.6 32.0 %copy-start = (bf16[256,1280]{1,0:T(8,128)(2,1)S(1)}, bf16[256,1280]{1,0:T(8,128)(2,1)}, u32[]{:S(2)}) copy-start(bf16[256,1280]{1,0:T(8,128)(2,1)} %param.8) | copy-start | bytes 1966084
  21.0 11.7 %copy-start.2 = (bf16[128,1280]{1,0:T(8,128)(2,1)S(1)}, bf16[128,1280]{1,0:T(8,128)(2,1)}, u32[]{:S(2)}) copy-start(bf16[128,1280]{1,0:T(8,128)(2,1)} %param.7) | copy-start | bytes 983044
  21.0 12.1 %collective-permute-start.2 = (bf16[1024,128]{1,0:T(8,128)(2,1)S(1)}, bf16[1024,128]{1,0:T(8,128)(2,1)S(1)}, u32[]{:S(2)}, u32[]{:S(2)}) collective-permute-start(bf16[1024,128]{1,0:T(8,128)(2,1)S(1)} %bitcast.8), channel_id=1, source_target_pairs={{0,1},{1,0},{2,3},{3,2},{4,5},{5,4},{6,7},{7,6},{8,9},{9,8},{10,11... | collective-permute-start | bytes 786440 | tf_op jit(solution)/shard_map/ppermute | solution.py:287
  23.3 17.2 %collective-permute-start = (bf16[1024,128]{1,0:T(8,128)(2,1)S(1)}, bf16[1024,128]{1,0:T(8,128)(2,1)S(1)}, u32[]{:S(2)}, u32[]{:S(2)}) collective-permute-start(bf16[1024,128]{1,0:T(8,128)(2,1)S(1)} %bitcast.9), channel_id=1, source_target_pairs={{0,8},{1,9},{2,10},{3,11},{4,12},{5,13},{6,14},{7,15},{8,0},{9,1},... | collective-permute-start | bytes 786440 | tf_op jit(solution)/shard_map/ppermute | solution.py:287
  24.6 16.0 %collective-permute-start.1 = (bf16[1024,128]{1,0:T(8,128)(2,1)S(1)}, bf16[1024,128]{1,0:T(8,128)(2,1)S(1)}, u32[]{:S(2)}, u32[]{:S(2)}) collective-permute-start(bf16[1024,128]{1,0:T(8,128)(2,1)S(1)} %bitcast.10), channel_id=1, source_target_pairs={{0,3},{1,2},{2,1},{3,0},{4,7},{5,6},{6,5},{7,4},{8,11},{9,10},{10,... | collective-permute-start | bytes 786440 | tf_op jit(solution)/shard_map/ppermute | solution.py:287
  40.5 35.5 %copy-start.1 = (s32[16,32]{1,0:T(8,128)S(1)}, s32[16,32]{1,0:T(8,128)}, u32[]{:S(2)}) copy-start(s32[16,32]{1,0:T(8,128)} %cand_ref.1) | copy-start | bytes 6148
  74.0 3.3 %collective-permute-start.3 = (f32[512,128]{1,0:T(8,128)S(1)}, f32[512,128]{1,0:T(8,128)S(1)}, u32[]{:S(2)}, u32[]{:S(2)}) collective-permute-start(f32[512,128]{1,0:T(8,128)S(1)} %bitcast.12), channel_id=1, source_target_pairs={{0,1},{1,0},{2,3},{3,2},{4,5},{5,4},{6,7},{7,6},{8,9},{9,8},{10,11... | collective-permute-start | bytes 786440 | tf_op jit(solution)/shard_map/ppermute | solution.py:287

commit v9 on v8

--- a/solution.py
+++ b/solution.py
@@ -43,8 +43,9 @@
     for k in range(GRP):
         sched_ref[total + k] = 0
     rest = total % GRP
-    sched_ref[384] = total // GRP + jnp.where(rest > GRP // 2, 1, 0)
-    sched_ref[385] = jnp.where((rest > 0) & (rest <= GRP // 2), 1, 0)
+    quarters = (rest + (GRP // 4 - 1)) // (GRP // 4)
+    sched_ref[384] = total // GRP + quarters // 4
+    sched_ref[385] = quarters % 4
     copy.wait()
 
     def clean(p, _):
@@ -79,9 +80,15 @@
     full = sched_ref[384]
     lax.fori_loop(0, full, step, 0)
 
-    @pl.when(sched_ref[385] == 1)
+    tail = sched_ref[385]
+
+    @pl.when(tail >= 2)
     def _():
         run(full * GRP, GRP // 2)
+
+    @pl.when(tail % 2 == 1)
+    def _():
+        run(full * GRP + (tail // 2) * (GRP // 2), GRP // 4)
 
     def gather(p, _):
         at, live = sched_ref[320 + p], sched_ref[352 + p]
@@ -93,7 +100,7 @@
         best_ref[pl.ds(p, 1), :] = jnp.max(m, axis=0, keepdims=True)
         return 0
 
-    lax.fori_loop(0, count, gather, 0, unroll=8)
+    lax.fori_loop(0, count, gather, 0, unroll=32)
 
 
 def add_rows(member, best_ref):

time: 78.7 us -> 78.5 us (level)
    all_to_all x1, blocking collectives: 10.4 us -> 11.3 us  [body(): back = lax.all_to_all(sums, 'fde', 0, 0, tiled=True)]
  transfers between devices with their start and end apart: 4 -> 4, of which waited for: 0 -> 0; matrix products, arithmetic and copies ran while one was open for 0% -> 0% of each run, Pallas kernels for 20% -> 19%
where the time goes in v9:
time: 78.5 us; the launch traced here: 78.1 us
  blocking collectives  45.4 us (58%)
  Pallas kernels  24.7 us (31%)
  starting transfers between devices  6.93 us (9%)
    pallas_call x8, Pallas kernels, call(): pl.pallas_call(kernel, out_shape=outs, in_specs=[VM] * len(ins) if in_spe...  24.7 us
    all_to_all x1, blocking collectives, body(): near = lax.all_to_all(tiles, 'fde', 0, 0, tiled=True)  19.3 us
    all_to_all x1, blocking collectives, body(): lax.all_to_all(copies, 'pas', 0, 0, axis_index_groups=[[2 * k + c for k i...  14.7 us
    all_to_all x1, blocking collectives, body(): back = lax.all_to_all(sums, 'fde', 0, 0, tiled=True)  11.3 us
    ppermute x4, starting transfers between devices, moved(): return lax.ppermute(x, 'pas', [(k, k ^ flip) for k in range(shards)])  6.93 us
  transfers between devices with their start and end apart: 4, of which 0 were waited for; matrix products, arithmetic and copies ran while one was open for 0% of the time, Pallas kernels for 19%

profile of v9, /device:TPU:1, one launch (start us, length us, event | category | flops | bytes accessed | tf_op | source)
XLA Modules:
  0.0 78.1 jit_solution(4805956034289191639)
XLA Ops:
  0.6 0.0 copy-start
  0.6 1.1 %shard_map.87 = (bf16[512,128]{1,0:T(8,128)(2,1)S(1)}, bf16[8,128,128]{2,1,0:T(8,128)(2,1)S(1)}) custom-call(s32[16]{0:T(128)} %count_ref.3, bf16[16,32,128]{2,1,0:T(8,128)(2,1)} %q_ref.1), custom_call_target="tpu_custom_call" | custom-call | tf_op jit(solution)/shard_map/pallas_call | solution.py:259
  1.7 19.3 %all_to_all.15 = bf16[8,128,128]{2,1,0:T(8,128)(2,1)S(1)} all-to-all(bf16[8,128,128]{2,1,0:T(8,128)(2,1)S(1)} %get-tuple-element.13), channel_id=1, replica_groups=mesh['fde'=8,'pas'=32] {'fde'}, dimensions={0} | all-to-all | bytes 524288 | tf_op jit(solution)/shard_map/all_to_all | solution.py:290
  21.0 0.0 copy-start.2
  21.0 2.3 %collective-permute-start.2 = (bf16[1024,128]{1,0:T(8,128)(2,1)S(1)}, bf16[1024,128]{1,0:T(8,128)(2,1)S(1)}, u32[]{:S(2)}, u32[]{:S(2)}) collective-permute-start(bf16[1024,128]{1,0:T(8,128)(2,1)S(1)} %bitcast.8), channel_id=1, source_target_pairs={{0,1},{1,0},{2,3},{3,2},{4,5},{5,4},{6,7},{7,6},{8,9},{9,8},{10,11... | collective-permute-start | bytes 786440 | tf_op jit(solution)/shard_map/ppermute | solution.py:294
  23.3 1.2 %collective-permute-start = (bf16[1024,128]{1,0:T(8,128)(2,1)S(1)}, bf16[1024,128]{1,0:T(8,128)(2,1)S(1)}, u32[]{:S(2)}, u32[]{:S(2)}) collective-permute-start(bf16[1024,128]{1,0:T(8,128)(2,1)S(1)} %bitcast.9), channel_id=1, source_target_pairs={{0,8},{1,9},{2,10},{3,11},{4,12},{5,13},{6,14},{7,15},{8,0},{9,1},... | collective-permute-start | bytes 786440 | tf_op jit(solution)/shard_map/ppermute | solution.py:294
  24.6 1.5 %collective-permute-start.1 = (bf16[1024,128]{1,0:T(8,128)(2,1)S(1)}, bf16[1024,128]{1,0:T(8,128)(2,1)S(1)}, u32[]{:S(2)}, u32[]{:S(2)}) collective-permute-start(bf16[1024,128]{1,0:T(8,128)(2,1)S(1)} %bitcast.10), channel_id=1, source_target_pairs={{0,3},{1,2},{2,1},{3,0},{4,7},{5,6},{6,5},{7,4},{8,11},{9,10},{10,... | collective-permute-start | bytes 786440 | tf_op jit(solution)/shard_map/ppermute | solution.py:294
  26.0 3.1 %shard_map.86 = (bf16[32,256,128]{2,1,0:T(8,128)(2,1)S(1)}, s32[512]{0:T(512)}) custom-call(s32[32]{0:T(128)} %len_ref.1, bf16[32,256,128]{2,1,0:T(8,128)(2,1)} %p_ref.1), custom_call_target="tpu_custom_call" | custom-call | tf_op jit(solution)/shard_map/pallas_call | solution.py:259
  29.1 3.4 %shard_map.88.own_ref = f32[8,512]{1,0:T(8,128)S(1)} custom-call(s32[512]{0:T(512)} %get-tuple-element.11.sched_ref, bf16[8192,128]{1,0:T(8,128)(2,1)S(1)} %bitcast.5, bf16[512,128]{1,0:T(8,128)(2,1)S(1)} %get-tuple-element.14.q_ref), custom_call_target="tpu_custom_call" | custom-call | tf_op jit(solution)/shard_map/pallas_call | solution.py:259
  32.6 0.0 copy-done
  32.6 0.0 copy-done.2
  32.6 0.4 fusion.fde_ref
  33.0 0.0 collective-permute-done.2.b_ref
  33.0 7.3 %shard_map.89.near_ref = f32[8,256]{1,0:T(8,128)S(1)} custom-call(s32[512]{0:T(512)} %get-tuple-element.11.sched_ref, bf16[8192,128]{1,0:T(8,128)(2,1)S(1)} %bitcast.6, bf16[1024,128]{1,0:T(8,128)(2,1)S(1)} %bitcast.11, bf16[1024,128]{1,0:T(8,128)(2,1)S(1)} %collective-permute-done.2.b_ref), custom_call_target="tpu_custom_call" | custom-call | tf_op jit(solution)/shard_map/pallas_call | solution.py:259
  40.3 0.0 copy-start.1
  40.3 0.0 collective-permute-done.a_ref
  40.3 0.0 collective-permute-done.1.b_ref
  40.3 7.5 %shard_map.90 = f32[8,40,128]{2,1,0:T(8,128)S(1)} custom-call(s32[512]{0:T(512)} %get-tuple-element.11.sched_ref, bf16[8192,128]{1,0:T(8,128)(2,1)S(1)} %bitcast.7, bf16[1024,128]{1,0:T(8,128)(2,1)S(1)} %collective-permute-done.a_ref, bf16[1024,128]{1,0:T(8,128)(2,1)S(1)} %collective-permute-done.1.b_ref, f32[8,512]{1,0:T(8,128)S(1)} %shard_map.88.own_ref, ...), custom_call_target="tpu_custom_call" | custom-call | tf_op jit(solution)/shard_map/pallas_call | solution.py:259
  47.8 11.3 %all_to_all.16.x_ref = f32[8,40,128]{2,1,0:T(8,128)S(1)} all-to-all(f32[8,40,128]{2,1,0:T(8,128)S(1)} %shard_map.90), channel_id=1, replica_groups=mesh['fde'=8,'pas'=32] {'fde'}, dimensions={0} | all-to-all | bytes 327680 | tf_op jit(solution)/shard_map/all_to_all | solution.py:350
  59.2 14.7 %all_to_all.17 = f32[16,4,8,128]{3,2,1,0:T(8,128)S(1)} all-to-all(f32[16,4,8,128]{3,2,1,0:T(8,128)S(1)} %shard_map.92), channel_id=1, replica_groups={{0,2,4,6,8,10,12,14,16,18,20,22,24,26,28,30},{1,3,5,7,9,11,13,15,17,19,..., dimensions={0} | all-to-all | bytes 524288 | tf_op jit(solution)/shard_map/all_to_all | solution.py:369
  73.9 1.9 %collective-permute-start.3 = (f32[512,128]{1,0:T(8,128)S(1)}, f32[512,128]{1,0:T(8,128)S(1)}, u32[]{:S(2)}, u32[]{:S(2)}) collective-permute-start(f32[512,128]{1,0:T(8,128)S(1)} %bitcast.12), channel_id=1, source_target_pairs={{0,1},{1,0},{2,3},{3,2},{4,5},{5,4},{6,7},{7,6},{8,9},{9,8},{10,11... | collective-permute-start | bytes 786440 | tf_op jit(solution)/shard_map/ppermute | solution.py:294
  75.8 0.0 copy-done.1
  75.8 1.3 %shard_map.91 = (f32[16,256]{1,0:T(8,128)}, bf16[128,512]{1,0:T(8,128)(2,1)S(1)}, bf16[128,512]{1,0:T(8,128)(2,1)S(1)}, s32[8,512]{1,0:T(8,128)S(1)}, f32[8,512]{1,0:T(8,128)S(1)}) custom-call(s32[16]{0:T(128)} %count_ref.3, s32[16,32]{1,0:T(8,128)S(1)} %copy-done.1, f32[8,40,128]{2,1,0:T(8,128)S(1)} %all_to_all.16.x_ref), custom_call_target="tpu_custom_call" | custom-call | tf_op jit(solution)/shard_map/pallas_call | solution.py:259
  77.1 0.0 collective-permute-done.3.far_ref
  77.1 1.0 %shard_map.93 = f32[16,32]{1,0:T(8,128)} custom-call(s32[8,512]{1,0:T(8,128)S(1)} %get-tuple-element.16.want_ref, f32[8,512]{1,0:T(8,128)S(1)} %get-tuple-element.17.div_ref, bf16[128,512]{1,0:T(8,128)(2,1)S(1)} %get-tuple-element.18.hot_near_ref, bf16[128,512]{1,0:T(8,128)(2,1)S(1)} %get-tuple-element.19.hot_far_ref, f32[512,128]{1,0:T(8,128)S(1)} %bitcast.13, ...), custom_call_target="tpu_custom_call" | custom-call | tf_op jit(solution)/shard_map/pallas_call | solution.py:259
  (1 shorter events, 0.0 us)
Async XLA Ops:
  0.6 32.0 %copy-start = (bf16[256,1280]{1,0:T(8,128)(2,1)S(1)}, bf16[256,1280]{1,0:T(8,128)(2,1)}, u32[]{:S(2)}) copy-start(bf16[256,1280]{1,0:T(8,128)(2,1)} %param.8) | copy-start | bytes 1966084
  21.0 11.6 %copy-start.2 = (bf16[128,1280]{1,0:T(8,128)(2,1)S(1)}, bf16[128,1280]{1,0:T(8,128)(2,1)}, u32[]{:S(2)}) copy-start(bf16[128,1280]{1,0:T(8,128)(2,1)} %param.7) | copy-start | bytes 983044
  21.0 12.0 %collective-permute-start.2 = (bf16[1024,128]{1,0:T(8,128)(2,1)S(1)}, bf16[1024,128]{1,0:T(8,128)(2,1)S(1)}, u32[]{:S(2)}, u32[]{:S(2)}) collective-permute-start(bf16[1024,128]{1,0:T(8,128)(2,1)S(1)} %bitcast.8), channel_id=1, source_target_pairs={{0,1},{1,0},{2,3},{3,2},{4,5},{5,4},{6,7},{7,6},{8,9},{9,8},{10,11... | collective-permute-start | bytes 786440 | tf_op jit(solution)/shard_map/ppermute | solution.py:294
  23.3 17.0 %collective-permute-start = (bf16[1024,128]{1,0:T(8,128)(2,1)S(1)}, bf16[1024,128]{1,0:T(8,128)(2,1)S(1)}, u32[]{:S(2)}, u32[]{:S(2)}) collective-permute-start(bf16[1024,128]{1,0:T(8,128)(2,1)S(1)} %bitcast.9), channel_id=1, source_target_pairs={{0,8},{1,9},{2,10},{3,11},{4,12},{5,13},{6,14},{7,15},{8,0},{9,1},... | collective-permute-start | bytes 786440 | tf_op jit(solution)/shard_map/ppermute | solution.py:294
  24.6 15.8 %collective-permute-start.1 = (bf16[1024,128]{1,0:T(8,128)(2,1)S(1)}, bf16[1024,128]{1,0:T(8,128)(2,1)S(1)}, u32[]{:S(2)}, u32[]{:S(2)}) collective-permute-start(bf16[1024,128]{1,0:T(8,128)(2,1)S(1)} %bitcast.10), channel_id=1, source_target_pairs={{0,3},{1,2},{2,1},{3,0},{4,7},{5,6},{6,5},{7,4},{8,11},{9,10},{10,... | collective-permute-start | bytes 786440 | tf_op jit(solution)/shard_map/ppermute | solution.py:294
  40.3 35.5 %copy-start.1 = (s32[16,32]{1,0:T(8,128)S(1)}, s32[16,32]{1,0:T(8,128)}, u32[]{:S(2)}) copy-start(s32[16,32]{1,0:T(8,128)} %cand_ref.1) | copy-start | bytes 6148
  73.9 3.2 %collective-permute-start.3 = (f32[512,128]{1,0:T(8,128)S(1)}, f32[512,128]{1,0:T(8,128)S(1)}, u32[]{:S(2)}, u32[]{:S(2)}) collective-permute-start(f32[512,128]{1,0:T(8,128)S(1)} %bitcast.12), channel_id=1, source_target_pairs={{0,1},{1,0},{2,3},{3,2},{4,5},{5,4},{6,7},{7,6},{8,9},{9,8},{10,11... | collective-permute-start | bytes 786440 | tf_op jit(solution)/shard_map/ppermute | solution.py:294
